TPU v7x, 256 devices: a whole 4x4x8 slice. The times are simulated.
256 devices in a mesh: gx: 16 (over y_lo, x, core), gy: 16 (over y_hi, z).
Axes of the slice: x: 4, y: 4 (y_hi: 2, y_lo: 2; y = y_hi * 2 + y_lo), z: 8, core: 2. Of those that a mesh axis runs over, the one named last changes fastest.
Arguments:
- tensor: bfloat16 [8, 8192, 8192], P(None, 'gx', 'gy'), may hold values from -6 to 6
- y_factor: bfloat16 [8192, 64], P('gy'), may hold values from -0.0625 to 0.0625
- x_factor: bfloat16 [64, 8192], P(None, 'gx'), may hold values from -0.0625 to 0.0625
Outputs:
- new_basis: float32 [64, 8192], P(None, ('gx', 'gy'))
All inputs are finite; a program needn't handle non-finite values.
Results may differ from a plain program's by a relative error of at most 0.0003.
Values sent between devices are 32-bit elements; how exact they have to be, the bound alone decides.
No kernel may reach another device: no remote copies, remote signals or barrier semaphores. Data moves between devices by JAX's collectives and lax.ppermute only.
A program may use at most 64 MiB of HBM per device.

v0:
```python
import functools

import jax
import jax.numpy as jnp
from jax import lax
from jax.sharding import Mesh
from jax.sharding import PartitionSpec as P

GY = ("gy_0", "gy_1")
GX = ("gx_0", "gx_1", "gx_2")
GX_GY = ("gx_0", "gx_1", "gx_2", "gy_0", "gy_1")


def cut_along(array, dim, devices):
    before, after = (array.shape[:dim], array.shape[dim + 1 :])
    return jnp.moveaxis(array.reshape(*before, devices, -1, *after), dim, 0)


def sent_and_summed(array, axis, dim):
    devices = lax.axis_size(axis)
    tiles = lax.all_to_all(cut_along(array, dim, devices), axis, 0, 0, tiled=True)
    return jnp.sum(tiles, axis=0)


def from_everyone(array, axis):
    devices = lax.axis_size(axis)
    return lax.all_to_all(
        jnp.broadcast_to(array[None], (devices, *array.shape)), axis, 0, 0, tiled=True
    )


def of_everyone(array, axis):
    everything = from_everyone(array, axis)
    return jnp.sum(everything, axis=0)


def by_axis(array, axes):
    return functools.reduce(lax.psum, axes, array)


def per_device(tensor, y_factor, x_factor):
    width_x = tensor.shape[1]
    factor_wide = x_factor.astype(jnp.float32)
    proj_part = jnp.einsum("zxy,yr->zrx", tensor, y_factor, preferred_element_type=jnp.float32)
    proj_part = proj_part.reshape(-1, width_x)
    own_rows = sent_and_summed(proj_part, GY, 0)
    local_cols = lax.dot_general(
        factor_wide, own_rows, (((1,), (1,)), ((), ())), precision=lax.Precision.HIGHEST
    )
    folded = of_everyone(local_cols, GX)
    partial_value = jnp.dot(folded, own_rows, precision=lax.Precision.HIGHEST)
    update = sent_and_summed(partial_value, GY, 1)
    local_cross = jnp.dot(update, update.T, precision=lax.Precision.HIGHEST)
    cross_gram = by_axis(local_cross, GX_GY)
    cholesky_factor = jnp.linalg.cholesky(cross_gram)
    solved = jax.scipy.linalg.solve_triangular(cholesky_factor, update, lower=True)
    total_x = width_x * lax.axis_size(GX)
    return solved * jnp.sqrt(jnp.float32(total_x))


def solution(mesh):
    finer = Mesh(mesh.devices.reshape(2, 4, 2, 2, 8), ("gx_0", "gx_1", "gx_2", "gy_0", "gy_1"))
    in_specs = (P(None, GX, GY), P(GY, None), P(None, GX))
    out_specs = P(None, GX_GY)
    return jax.shard_map(
        per_device, mesh=finer, in_specs=in_specs, out_specs=out_specs, check_vma=False
    )
```

profile of v0, /device:TPU:2, one launch (start us, length us, event | category | flops | bytes accessed | tf_op | source)
XLA Modules:
  0.0 149.9 jit_solution(6204777461004257187)
XLA Ops:
  0.0 0.0 copy-start
  0.0 0.8 copy-done
  0.8 0.0 copy-start.1
  0.8 3.6 %fusion = f32[64,8,512]{2,0,1:T(8,128)S(1)} fusion(bf16[8,512,512]{2,1,0:T(8,128)(2,1)} %param.3, bf16[512,64]{0,1:T(8,128)(2,1)S(1)} %copy-done), kind=kOutput, calls=%fused_computation.3 | convolution fusion | flops 268435456 | bytes 5308416 | tf_op jit(solution)/shard_map/zxy,yr->zrx/dot_general | solution.py:44
  4.4 39.4 %all_to_all.15 = f32[16,32,512]{2,1,0:T(8,128)S(1)} all-to-all(f32[16,32,512]{2,1,0:T(8,128)S(1)} %bitcast.43), channel_id=1, replica_groups=mesh['gx_0'=2,'gx_1'=4,'gx_2'=2,'gy_0'=2,'gy_1'=8] {'gy_0','gy_1'}, dimensions={0} | all-to-all | bytes 2097152 | tf_op jit(solution)/shard_map/all_to_all | solution.py:21
  43.8 0.1 reduce_sum.27
  43.9 0.0 copy-done.1
  43.9 0.1 convolution_bitcast_fusion.1
  44.1 0.1 broadcast_bitcast_fusion
  44.1 0.8 reshape.15
  44.9 5.0 %all-to-all-start.1 = ((f32[16,1,2048]{2,1,0:T(1,128)}), f32[16,1,2048]{2,1,0:T(1,128)S(1)}, u32[]{:S(2)}, u32[]{:S(2)}) async-start(f32[16,1,2048]{2,1,0:T(1,128)} %reshape.15), calls=%async_computation.1 | async-start | bytes 262144 | tf_op jit(solution)/shard_map/all_to_all | solution.py:27
  49.9 0.1 copy.11
  50.0 4.8 %all-to-all-done.1 = f32[16,1,2048]{2,1,0:T(1,128)S(1)} async-done(((f32[16,1,2048]{2,1,0:T(1,128)}), f32[16,1,2048]{2,1,0:T(1,128)S(1)}, u32[]{:S(2)}, u32[]{:S(2)}) %all-to-all-start.1) | async-done | bytes 131104 | tf_op jit(solution)/shard_map/all_to_all | solution.py:27
  54.8 0.5 broadcast.54
  55.3 0.9 reduce.6
  56.3 0.1 reshape.16
  56.4 0.3 fusion.6
  56.8 0.2 reshape.17
  56.9 15.2 %all_to_all.16 = f32[16,1,2048]{2,1,0:T(1,128)S(1)} all-to-all(f32[16,1,2048]{2,1,0:T(1,128)S(1)} %reshape.17), channel_id=1, replica_groups=mesh['gx_0'=2,'gx_1'=4,'gx_2'=2,'gy_0'=2,'gy_1'=8] {'gy_0','gy_1'}, dimensions={0} | all-to-all | bytes 262144 | tf_op jit(solution)/shard_map/all_to_all | solution.py:21
  72.2 0.9 reduce.7
  73.1 0.1 reshape.18
  73.3 0.2 fusion.9
  73.5 7.0 %psum.35 = f32[64,64]{0,1:T(8,128)S(1)} all-reduce(f32[64,64]{0,1:T(8,128)S(1)} %fusion.9), channel_id=1, replica_groups=mesh['gx_0'=2,'gx_1'=4,'gx_2'=2,'gy_0'=2,'gy_1'=8] {'gx_0'}, use_global_device_ids=true, to_apply=%region_3.0 | all-reduce | flops 4096 | bytes 32768 | tf_op jit(solution)/shard_map/psum | solution.py:38
  80.6 14.7 %psum.36 = f32[64,64]{0,1:T(8,128)S(1)} all-reduce(f32[64,64]{0,1:T(8,128)S(1)} %psum.35), channel_id=1, replica_groups=mesh['gx_0'=2,'gx_1'=4,'gx_2'=2,'gy_0'=2,'gy_1'=8] {'gx_1'}, use_global_device_ids=true, to_apply=%region_4.0 | all-reduce | flops 4096 | bytes 32768 | tf_op jit(solution)/shard_map/psum | solution.py:38
  95.3 3.4 %psum.37 = f32[64,64]{0,1:T(8,128)S(1)} all-reduce(f32[64,64]{0,1:T(8,128)S(1)} %psum.36), channel_id=1, replica_groups=mesh['gx_0'=2,'gx_1'=4,'gx_2'=2,'gy_0'=2,'gy_1'=8] {'gx_2'}, use_global_device_ids=true, to_apply=%region_5.0 | all-reduce | flops 4096 | bytes 32768 | tf_op jit(solution)/shard_map/psum | solution.py:38
  98.7 9.9 %psum.38 = f32[64,64]{0,1:T(8,128)S(1)} all-reduce(f32[64,64]{0,1:T(8,128)S(1)} %psum.37), channel_id=1, replica_groups=mesh['gx_0'=2,'gx_1'=4,'gx_2'=2,'gy_0'=2,'gy_1'=8] {'gy_0'}, use_global_device_ids=true, to_apply=%region_6.0 | all-reduce | flops 4096 | bytes 32768 | tf_op jit(solution)/shard_map/psum | solution.py:38
  108.6 28.3 %psum.39 = f32[64,64]{0,1:T(8,128)S(1)} all-reduce(f32[64,64]{0,1:T(8,128)S(1)} %psum.38), channel_id=1, replica_groups=mesh['gx_0'=2,'gx_1'=4,'gx_2'=2,'gy_0'=2,'gy_1'=8] {'gy_1'}, use_global_device_ids=true, to_apply=%region_7.0 | all-reduce | flops 4096 | bytes 32768 | tf_op jit(solution)/shard_map/psum | solution.py:38
  136.9 0.1 copy.9
  137.0 5.8 %cholesky.16 = f32[64,64]{1,0:T(8,128)S(1)} custom-call(f32[64,64]{1,0:T(8,128)S(1)} %fusion.4), custom_call_target="Cholesky" | custom-call | tf_op jit(solution)/shard_map/jit(cholesky)/cholesky | solution.py:55
  142.9 0.6 compare_reduce_fusion
  143.5 0.7 fusion.2
  144.2 4.9 %custom-call.7 = f32[1,64,64]{1,2,0:T(8,128)S(1)} custom-call(f32[1,64,64]{2,1,0:T(8,128)S(1)} %fusion.2), custom_call_target="InvertDiagBlocksLowerTriangular" | custom-call | tf_op jit(solution)/shard_map/jit(_solve_triangular)/triangular_solve | solution.py:56
  149.1 0.8 convolution_multiply_fusion
  (4 shorter events, 0.1 us)
Async XLA Ops:
  0.0 0.8 copy-start
  0.8 43.1 %copy-start.1 = (bf16[64,512]{1,0:T(8,128)(2,1)S(1)}, bf16[64,512]{1,0:T(8,128)(2,1)}, u32[]{:S(2)}) copy-start(bf16[64,512]{1,0:T(8,128)(2,1)} %param.5) | copy-start | bytes 196612
  44.9 9.8 %all-to-all-start.1 = ((f32[16,1,2048]{2,1,0:T(1,128)}), f32[16,1,2048]{2,1,0:T(1,128)S(1)}, u32[]{:S(2)}, u32[]{:S(2)}) async-start(f32[16,1,2048]{2,1,0:T(1,128)} %reshape.15), calls=%async_computation.1 | async-start | bytes 262144 | tf_op jit(solution)/shard_map/all_to_all | solution.py:27
where the time goes:
time: 152 us; the launch traced here: 150 us
  blocking collectives  118 us (78%)
  other arithmetic  14.1 us (9%)
  matrix products  5.08 us (3%)
  starting transfers between devices  4.96 us (3%)
  waiting for transfers between devices  4.76 us (3%)
  local copies, waits for them, and re-layouts  2.81 us (2%)
    psum x5, blocking collectives, by_axis(): return functools.reduce(lax.psum, axes, array)  63.4 us
    all_to_all x2, blocking collectives, sent_and_summed(): lax.all_to_all(cut_along(array, dim, devices), axis, 0, 0, tiled=True)  54.6 us
    another operation x3, other arithmetic, per_device(): cholesky_factor = jnp.linalg.cholesky(cross_gram)  6.52 us
    another operation x2, other arithmetic, per_device(): jax.scipy.linalg.solve_triangular(cholesky_factor, update, lower=True)  5.55 us
    all_to_all x1, starting transfers between devices, from_everyone(): lax.all_to_all(jnp.broadcast_to(array[None], (devices, *array.shape)), ax...  4.96 us
    all_to_all x1, waiting for transfers between devices, from_everyone(): lax.all_to_all(jnp.broadcast_to(array[None], (devices, *array.shape)), ax...  4.76 us
    dot_general x1, matrix products, per_device(): jnp.einsum('zxy,yr->zrx', tensor, y_factor, preferred_element_type=jnp.fl...  3.58 us
  transfers between devices with their start and end apart: 1, of which 1 were waited for; matrix products, arithmetic and copies ran while one was open for 0% of the time, Pallas kernels for 0%

commit v1 on v0

v1 whole, which is shorter than its diff:
```python
import jax
import jax.numpy as jnp
from jax import lax
from jax.sharding import Mesh
from jax.sharding import PartitionSpec as P

AXES = ("y_lo", "x", "core", "y_hi", "z")
GX = ("y_lo", "x", "core")
GY = ("y_hi", "z")
PLANE = ("y_hi", "y_lo", "x", "core")
CHIPS = ("y_hi", "y_lo", "x")
HIGHEST = lax.Precision.HIGHEST


def exchanged(tiles, axis):
    return lax.all_to_all(tiles, axis, 0, 0, tiled=True)


def of_everyone(tile, axis):
    return exchanged(jnp.broadcast_to(tile[None], (lax.axis_size(axis), *tile.shape)), axis)


def tiles_of(matrix):
    rows, cols = matrix.shape
    return matrix.reshape(rows // 8, 8, cols // 128, 128).swapaxes(1, 2).reshape(-1, 8, 128)


def from_tiles(tiles, rows, cols):
    return tiles.reshape(rows // 8, cols // 128, 8, 128).swapaxes(1, 2).reshape(rows, cols)


def summed_everywhere(matrix):
    rows, cols = matrix.shape
    n = lax.axis_size(PLANE)
    tiles = tiles_of(matrix).reshape(n, -1, 128)
    own = jnp.sum(exchanged(tiles, PLANE), axis=0)
    own = jnp.sum(of_everyone(own, "z"), axis=0)
    return from_tiles(of_everyone(own, PLANE).reshape(-1, 8, 128), rows, cols)


def small_sum(square):
    half = square.shape[0] // 2
    wide = jnp.concatenate([square[:half], square[half:]], axis=1)
    wide = wide + lax.ppermute(wide, "core", [(0, 1), (1, 0)])
    wide = jnp.sum(of_everyone(wide, CHIPS), axis=0)
    wide = jnp.sum(of_everyone(wide, "z"), axis=0)
    return jnp.concatenate([wide[:, : 2 * half], wide[:, 2 * half :]], axis=0)


def per_device(tensor, y_factor, x_factor):
    width_x = tensor.shape[1]
    rank = x_factor.shape[0]
    factor_wide = x_factor.astype(jnp.float32)
    proj_t = jnp.einsum("zxy,yr->xzr", tensor, y_factor, preferred_element_type=jnp.float32)
    proj_t = proj_t.reshape(width_x, -1)
    folded = summed_everywhere(jnp.dot(factor_wide, proj_t, precision=HIGHEST))
    part = lax.dot_general(proj_t, folded, (((1,), (1,)), ((), ())), precision=HIGHEST)
    n = lax.axis_size(GY)
    own_x = width_x // n
    part = part.reshape(n, 2, own_x // 2, rank)
    part = jnp.concatenate([part[:, 0], part[:, 1]], axis=2)
    packed = jnp.sum(exchanged(part, GY), axis=0)
    update_t = jnp.concatenate([packed[:, :rank], packed[:, rank:]], axis=0)
    local_cross = lax.dot_general(update_t, update_t, (((0,), (0,)), ((), ())), precision=HIGHEST)
    cross_gram = small_sum(local_cross)
    cholesky_factor = jnp.linalg.cholesky(cross_gram)
    solved = jax.scipy.linalg.solve_triangular(cholesky_factor, update_t.T, lower=True)
    total_x = width_x * lax.axis_size(GX)
    return solved * jnp.sqrt(jnp.float32(total_x))


def solution(mesh):
    finer = Mesh(mesh.devices.reshape(2, 4, 2, 2, 8), AXES)
    in_specs = (P(None, GX, GY), P(GY, None), P(None, GX))
    out_specs = P(None, AXES)
    return jax.shard_map(
        per_device, mesh=finer, in_specs=in_specs, out_specs=out_specs, check_vma=False
    )
```

time: 152 us -> 101 us (0.66); the launches traced: 150 us -> 101 us
  blocking collectives: 118 us -> 67.3 us
  waiting for transfers between devices: 4.76 us -> 6.6 us
    psum x5 -> x0, blocking collectives: 63.4 us -> none  [by_axis(): return functools.reduce(lax.psum, axes, array)]
    all_to_all x2 -> x5, blocking collectives: 54.6 us -> 67.3 us  [exchanged(): return lax.all_to_all(tiles, axis, 0, 0, tiled=True)]
    all_to_all x2 -> x0, other arithmetic: 1.9 us -> none  [the longest x1 0.95 us: sent_and_summed(): lax.all_to_all(cut_along(array, dim, devices), axis, 0, 0, tiled=True)]
  transfers between devices with their start and end apart: 1 -> 2, of which waited for: 1 -> 2; matrix products, arithmetic and copies ran while one was open for 0% -> 1% of each run, Pallas kernels for 0% -> 0%
where the time goes in v1:
time: 101 us
  blocking collectives  67.3 us (67%)
  other arithmetic  12.6 us (12%)
  waiting for transfers between devices  6.6 us (7%)
  matrix products  6.22 us (6%)
  starting transfers between devices  4.96 us (5%)
  local copies, waits for them, and re-layouts  3.19 us (3%)
    all_to_all x5, blocking collectives, exchanged(): return lax.all_to_all(tiles, axis, 0, 0, tiled=True)  67.3 us
    another operation x3, other arithmetic, per_device(): cholesky_factor = jnp.linalg.cholesky(cross_gram)  6.53 us
    another operation x2, other arithmetic, per_device(): jax.scipy.linalg.solve_triangular(cholesky_factor, update_t.T, lower=True)  5.55 us
    all_to_all x1, waiting for transfers between devices, exchanged(): return lax.all_to_all(tiles, axis, 0, 0, tiled=True)  5.43 us
    all_to_all x1, starting transfers between devices, exchanged(): return lax.all_to_all(tiles, axis, 0, 0, tiled=True)  4.92 us
    dot_general x1, matrix products, per_device(): jnp.einsum('zxy,yr->xzr', tensor, y_factor, preferred_element_type=jnp.fl...  3.58 us
  transfers between devices with their start and end apart: 2, of which 2 were waited for; matrix products, arithmetic and copies ran while one was open for 1% of the time, Pallas kernels for 0%

profile of v1, /device:TPU:2, one launch (start us, length us, event | category | flops | bytes accessed | tf_op | source)
XLA Modules:
  0.0 101.0 jit_solution(17639364867679118064)
XLA Ops:
  0.0 0.0 copy-start
  0.0 0.8 copy-done
  0.8 0.0 copy-start.1
  0.8 3.6 %fusion = f32[64,8,512]{2,0,1:T(8,128)S(1)} fusion(bf16[8,512,512]{2,1,0:T(8,128)(2,1)} %param.3, bf16[512,64]{0,1:T(8,128)(2,1)S(1)} %copy-done), kind=kOutput, calls=%fused_computation.4 | convolution fusion | flops 268435456 | bytes 5308416 | tf_op jit(solution)/shard_map/zxy,yr->xzr/dot_general | solution.py:54
  4.4 0.0 copy-done.1
  4.4 0.7 fusion.11
  5.1 14.0 %all_to_all.30 = f32[32,8,128]{2,1,0:T(8,128)S(1)} all-to-all(f32[32,8,128]{2,1,0:T(8,128)S(1)} %bitcast.44), channel_id=1, replica_groups=mesh['y_lo'=2,'x'=4,'core'=2,'y_hi'=2,'z'=8] {'y_hi','y_lo','x','core'}, dimensions={0} | all-to-all | bytes 262144 | tf_op jit(solution)/shard_map/all_to_all | solution.py:16
  19.2 16.3 %all_to_all.31 = f32[8,8,128]{2,1,0:T(8,128)S(1)} all-to-all(f32[8,8,128]{2,1,0:T(8,128)S(1)} %broadcast_in_dim.9), channel_id=1, replica_groups=mesh['y_lo'=2,'x'=4,'core'=2,'y_hi'=2,'z'=8] {'z'}, dimensions={0} | all-to-all | bytes 65536 | tf_op jit(solution)/shard_map/all_to_all | solution.py:16
  35.5 0.6 broadcast_in_dim.10
  36.1 4.9 %all-to-all-start.2 = ((f32[32,8,128]{2,1,0:T(8,128)}), f32[32,8,128]{2,1,0:T(8,128)S(1)}, u32[]{:S(2)}, u32[]{:S(2)}) async-start(f32[32,8,128]{2,1,0:T(8,128)} %broadcast_in_dim.10), calls=%async_computation.2 | async-start | bytes 262144 | tf_op jit(solution)/shard_map/all_to_all | solution.py:16
  41.0 0.8 copy.10
  41.8 0.5 dot_general.17
  42.3 5.4 %all-to-all-done.2 = f32[32,8,128]{2,1,0:T(8,128)S(1)} async-done(((f32[32,8,128]{2,1,0:T(8,128)}), f32[32,8,128]{2,1,0:T(8,128)S(1)}, u32[]{:S(2)}, u32[]{:S(2)}) %all-to-all-start.2) | async-done | bytes 131104 | tf_op jit(solution)/shard_map/all_to_all | solution.py:16
  47.7 1.0 fusion.12
  48.7 0.1 pad_maximum_fusion
  48.9 12.8 %all_to_all.32 = f32[16,16,128]{2,1,0:T(8,128)S(1)} all-to-all(f32[16,16,128]{2,1,0:T(8,128)S(1)} %pad_maximum_fusion), channel_id=1, replica_groups=mesh['y_lo'=2,'x'=4,'core'=2,'y_hi'=2,'z'=8] {'y_hi','z'}, dimensions={0} | all-to-all | bytes 262144 | tf_op jit(solution)/shard_map/all_to_all | solution.py:16
  61.7 0.1 fusion.10
  61.7 0.2 fusion.5
  62.0 0.1 pad_maximum_fusion.3
  62.1 0.0 collective-permute-start
  62.1 1.2 %collective-permute-done = f32[32,128]{1,0:T(8,128)S(1)} collective-permute-done((f32[32,128]{1,0:T(8,128)S(1)}, f32[32,128]{1,0:T(8,128)S(1)}, u32[]{:S(2)}, u32[]{:S(2)}) %collective-permute-start) | collective-permute-done | bytes 16416 | tf_op jit(solution)/shard_map/ppermute | solution.py:44
  63.3 0.1 fusion.18
  63.4 12.1 %all_to_all.33 = f32[16,32,128]{2,1,0:T(8,128)S(1)} all-to-all(f32[16,32,128]{2,1,0:T(8,128)S(1)} %broadcast_in_dim.11), channel_id=1, replica_groups=mesh['y_lo'=2,'x'=4,'core'=2,'y_hi'=2,'z'=8] {'y_hi','y_lo','x'}, dimensions={0} | all-to-all | bytes 524288 | tf_op jit(solution)/shard_map/all_to_all | solution.py:16
  75.6 12.1 %all_to_all.34 = f32[8,32,128]{2,1,0:T(8,128)S(1)} all-to-all(f32[8,32,128]{2,1,0:T(8,128)S(1)} %broadcast_in_dim.12), channel_id=1, replica_groups=mesh['y_lo'=2,'x'=4,'core'=2,'y_hi'=2,'z'=8] {'z'}, dimensions={0} | all-to-all | bytes 262144 | tf_op jit(solution)/shard_map/all_to_all | solution.py:16
  87.6 0.1 fusion.9
  87.7 0.1 copy.17
  87.8 0.1 copy.18
  87.9 0.1 pad_maximum_fusion.1
  88.0 0.1 copy.14
  88.0 0.1 fusion.4
  88.1 5.9 %cholesky.16 = f32[64,64]{1,0:T(8,128)S(1)} custom-call(f32[64,64]{1,0:T(8,128)S(1)} %fusion.4), custom_call_target="Cholesky" | custom-call | tf_op jit(solution)/shard_map/jit(cholesky)/cholesky | solution.py:66
  94.0 0.6 compare_reduce_fusion
  94.7 0.7 fusion.2
  95.3 4.9 %custom-call.7 = f32[1,64,64]{1,2,0:T(8,128)S(1)} custom-call(f32[1,64,64]{2,1,0:T(8,128)S(1)} %fusion.2), custom_call_target="InvertDiagBlocksLowerTriangular" | custom-call | tf_op jit(solution)/shard_map/jit(_solve_triangular)/triangular_solve | solution.py:67
  100.2 0.8 convolution_multiply_fusion
  (11 shorter events, 0.2 us)
Async XLA Ops:
  0.0 0.8 copy-start
  0.8 3.6 %copy-start.1 = (bf16[64,512]{1,0:T(8,128)(2,1)S(1)}, bf16[64,512]{1,0:T(8,128)(2,1)}, u32[]{:S(2)}) copy-start(bf16[64,512]{1,0:T(8,128)(2,1)} %param.5) | copy-start | bytes 196612
  36.1 11.6 %all-to-all-start.2 = ((f32[32,8,128]{2,1,0:T(8,128)}), f32[32,8,128]{2,1,0:T(8,128)S(1)}, u32[]{:S(2)}, u32[]{:S(2)}) async-start(f32[32,8,128]{2,1,0:T(8,128)} %broadcast_in_dim.10), calls=%async_computation.2 | async-start | bytes 262144 | tf_op jit(solution)/shard_map/all_to_all | solution.py:16
  62.1 1.2 %collective-permute-start = (f32[32,128]{1,0:T(8,128)S(1)}, f32[32,128]{1,0:T(8,128)S(1)}, u32[]{:S(2)}, u32[]{:S(2)}) collective-permute-start(f32[32,128]{1,0:T(8,128)S(1)} %pad_maximum_fusion.3), channel_id=1, source_target_pairs={{0,16},{16,0},{1,17},{17,1},{2,18},{18,2},{3,19},{19,3},{4,20},{20... | collective-permute-start | bytes 49160 | tf_op jit(solution)/shard_map/ppermute | solution.py:44

commit v2 on v1

v2 whole, which is shorter than its diff:
```python
import functools

import jax
import jax.numpy as jnp
from jax import lax
from jax.experimental import pallas as pl
from jax.experimental.pallas import tpu as pltpu
from jax.sharding import Mesh
from jax.sharding import PartitionSpec as P

AXES = ("y_lo", "x", "core", "y_hi", "z")
GX = ("y_lo", "x", "core")
GY = ("y_hi", "z")
PLANE = ("y_hi", "y_lo", "x", "core")
CHIPS = ("y_hi", "y_lo", "x")
HIGHEST = lax.Precision.HIGHEST
ON_CHIP = pl.BlockSpec(memory_space=pltpu.VMEM)


def exchanged(tiles, axis):
    return lax.all_to_all(tiles, axis, 0, 0, tiled=True)


def of_everyone(tile, axis):
    return exchanged(jnp.broadcast_to(tile[None], (lax.axis_size(axis), *tile.shape)), axis)


def tiles_of(matrix):
    rows, cols = matrix.shape
    return matrix.reshape(rows // 8, 8, cols // 128, 128).swapaxes(1, 2).reshape(-1, 8, 128)


def from_tiles(tiles, rows, cols):
    return tiles.reshape(rows // 8, cols // 128, 8, 128).swapaxes(1, 2).reshape(rows, cols)


def summed_everywhere(matrix):
    rows, cols = matrix.shape
    n = lax.axis_size(PLANE)
    tiles = tiles_of(matrix).reshape(n, -1, 128)
    own = jnp.sum(exchanged(tiles, PLANE), axis=0)
    own = jnp.sum(of_everyone(own, "z"), axis=0)
    return from_tiles(of_everyone(own, PLANE).reshape(-1, 8, 128), rows, cols)


def cross_terms(wide):
    wide = wide + lax.ppermute(wide, "core", [(0, 1), (1, 0)])
    wide = jnp.sum(of_everyone(wide, CHIPS), axis=0)
    return of_everyone(wide, "z")


def rounded_parts(matrix):
    high = matrix.astype(jnp.bfloat16)
    rest = matrix - high.astype(jnp.float32)
    middle = rest.astype(jnp.bfloat16)
    low = (rest - middle.astype(jnp.float32)).astype(jnp.bfloat16)
    return high, middle, low


def project_kernel(
    tensor_ref,
    y_ref,
    x_ref,
    proj_ref,
    folded_ref,
    planes,
    y_here,
    x_here,
    proj_here,
    folded_here,
    arrived,
    left,
):
    depth = planes.shape[0]
    rank = y_ref.shape[0]
    y_copy = pltpu.make_async_copy(y_ref, y_here, arrived.at[depth])
    x_copy = pltpu.make_async_copy(x_ref, x_here, arrived.at[depth + 1])
    y_copy.start()

    def plane(z):
        return pltpu.make_async_copy(tensor_ref.at[z], planes.at[z], arrived.at[z])

    def results(pair):
        lanes = pl.ds(2 * rank * pair, 2 * rank)
        return [
            pltpu.make_async_copy(here.at[:, lanes], there.at[:, lanes], left.at[pair, i])
            for i, (here, there) in enumerate(
                ((proj_here, proj_ref), (folded_here, folded_ref))
            )
        ]

    for z in range(depth):
        plane(z).start()
    x_copy.start()
    y_copy.wait()
    y_t = y_here[...]
    none = jnp.zeros_like(y_t)
    sides = (jnp.concatenate([y_t, none], axis=0), jnp.concatenate([none, y_t], axis=0))
    contract = (((1,), (1,)), ((), ()))
    for pair in range(depth // 2):
        total = None
        for side in range(2):
            z = 2 * pair + side
            plane(z).wait()
            term = lax.dot_general(
                planes[z], sides[side], contract, preferred_element_type=jnp.float32
            )
            total = term if total is None else total + term
        lanes = pl.ds(2 * rank * pair, 2 * rank)
        proj_here[:, lanes] = total
        proj_copy, folded_copy = results(pair)
        proj_copy.start()
        if pair == 0:
            x_copy.wait()
        folded = None
        for part in rounded_parts(total):
            term = jnp.dot(x_here[...], part, preferred_element_type=jnp.float32)
            folded = term if folded is None else folded + term
        folded_here[:, lanes] = folded
        folded_copy.start()
    for pair in range(depth // 2):
        for copy in results(pair):
            copy.wait()


def projected(tensor, y_factor, x_factor):
    depth, width_x, width_y = tensor.shape
    rank = y_factor.shape[1]
    return pl.pallas_call(
        project_kernel,
        out_shape=[
            jax.ShapeDtypeStruct((width_x, depth * rank), jnp.float32),
            jax.ShapeDtypeStruct((rank, depth * rank), jnp.float32),
        ],
        in_specs=[pl.BlockSpec(memory_space=pltpu.HBM)] * 3,
        out_specs=[pl.BlockSpec(memory_space=pltpu.HBM)] * 2,
        scratch_shapes=[
            pltpu.VMEM(tensor.shape, tensor.dtype),
            pltpu.VMEM((rank, width_y), y_factor.dtype),
            pltpu.VMEM(x_factor.shape, x_factor.dtype),
            pltpu.VMEM((width_x, depth * rank), jnp.float32),
            pltpu.VMEM((rank, depth * rank), jnp.float32),
            pltpu.SemaphoreType.DMA((depth + 2,)),
            pltpu.SemaphoreType.DMA((depth // 2, 2)),
        ],
        compiler_params=pltpu.CompilerParams(vmem_limit_bytes=56 * 2**20),
        name="projected",
    )(tensor, y_factor.T, x_factor)


def update_kernel(proj_ref, folded_ref, out_ref):
    n, half, lanes = out_ref.shape
    rank = lanes // 2
    part = lax.dot_general(
        proj_ref[...],
        folded_ref[...],
        (((1,), (1,)), ((), ())),
        precision=HIGHEST,
        preferred_element_type=jnp.float32,
    )
    part = part.reshape(n, 2, half, rank)
    out_ref[...] = jnp.concatenate([part[:, 0], part[:, 1]], axis=2)


def update_parts(proj_t, folded, n):
    width_x = proj_t.shape[0]
    rank = folded.shape[0]
    return pl.pallas_call(
        update_kernel,
        out_shape=jax.ShapeDtypeStruct((n, width_x // n // 2, 2 * rank), jnp.float32),
        in_specs=[ON_CHIP, ON_CHIP],
        out_specs=ON_CHIP,
        compiler_params=pltpu.CompilerParams(vmem_limit_bytes=24 * 2**20),
        name="update_parts",
    )(proj_t, folded)


def cross_kernel(parts_ref, update_ref, cross_ref):
    rank = update_ref.shape[1]
    packed = jnp.sum(parts_ref[...], axis=0)
    update_t = jnp.concatenate([packed[:, :rank], packed[:, rank:]], axis=0)
    update_ref[...] = update_t
    square = lax.dot_general(
        update_t,
        update_t,
        (((0,), (0,)), ((), ())),
        precision=HIGHEST,
        preferred_element_type=jnp.float32,
    )
    cross_ref[...] = jnp.concatenate([square[: rank // 2], square[rank // 2 :]], axis=1)


def own_update(parts):
    _, half, lanes = parts.shape
    rank = lanes // 2
    return pl.pallas_call(
        cross_kernel,
        out_shape=(
            jax.ShapeDtypeStruct((2 * half, rank), jnp.float32),
            jax.ShapeDtypeStruct((rank // 2, 2 * rank), jnp.float32),
        ),
        in_specs=[ON_CHIP],
        out_specs=(ON_CHIP, ON_CHIP),
        compiler_params=pltpu.CompilerParams(vmem_limit_bytes=8 * 2**20),
        name="own_update",
    )(parts)


def inverse_root(pivot):
    guess = lax.rsqrt(pivot)
    return guess * (1.5 - 0.5 * pivot * guess * guess)


def whitened_kernel(scale, cross_ref, update_ref, out_ref, aug, lanes):
    rank = update_ref.shape[1]
    cols = update_ref.shape[0]
    blocks = rank // 8
    wide = cross_ref[0]
    for i in range(1, cross_ref.shape[0]):
        wide = wide + cross_ref[i]
    gram = jnp.concatenate([wide[:, :rank], wide[:, rank:]], axis=0)
    padded = jnp.concatenate(
        [update_ref[...], jnp.zeros((rank - cols, rank), jnp.float32)], axis=0
    )
    aug[...] = jnp.concatenate([gram, padded.T], axis=1)
    rows = [aug[8 * i : 8 * i + 8, :] for i in range(blocks)]
    for j in range(blocks):
        aug[8 * j : 8 * j + 8, :] = rows[j]
        columns = []
        for i in range(j, blocks):
            columns.append(
                [
                    jnp.broadcast_to(rows[i][:, 8 * j + k : 8 * j + k + 1], (8, 128))
                    for k in range(8)
                ]
            )
        for k in range(8):
            lanes[8 * k : 8 * k + 8, :] = columns[0][k]
        a = [
            [jnp.broadcast_to(lanes[8 * k + m : 8 * k + m + 1, :], (8, 128)) for k in range(m + 1)]
            for m in range(8)
        ]
        right = [
            jnp.broadcast_to(aug[8 * j + k : 8 * j + k + 1, :], (8, 128)) for k in range(8)
        ]
        for k in range(8):
            root = inverse_root(a[k][k])
            for m in range(k + 1, 8):
                a[m][k] = a[m][k] * root
            right[k] = right[k] * root
            for column in columns[1:]:
                column[k] = column[k] * root
            for m in range(k + 1, 8):
                for n in range(k + 1, m + 1):
                    a[m][n] = a[m][n] - a[m][k] * a[n][k]
                right[m] = right[m] - a[m][k] * right[k]
                for column in columns[1:]:
                    column[m] = column[m] - column[k] * a[m][k]
        for k in range(8):
            aug[8 * j + k : 8 * j + k + 1, :] = right[k][:1]
        for i in range(j + 1, blocks):
            column = columns[i - j]
            first = column[0] * right[0] + column[1] * right[1]
            second = column[2] * right[2] + column[3] * right[3]
            third = column[4] * right[4] + column[5] * right[5]
            fourth = column[6] * right[6] + column[7] * right[7]
            rows[i] = rows[i] - ((first + second) + (third + fourth))
    out_ref[...] = aug[...].T[rank : rank + cols, :] * scale


def whitened(terms, update_t, scale):
    cols, rank = update_t.shape
    return pl.pallas_call(
        functools.partial(whitened_kernel, scale),
        out_shape=jax.ShapeDtypeStruct((cols, rank), jnp.float32),
        in_specs=[ON_CHIP, ON_CHIP],
        out_specs=ON_CHIP,
        scratch_shapes=[pltpu.VMEM((rank, 2 * rank), jnp.float32)] * 2,
        compiler_params=pltpu.CompilerParams(vmem_limit_bytes=8 * 2**20),
        name="whitened",
    )(terms, update_t)


def per_device(tensor, y_factor, x_factor):
    width_x = x_factor.shape[1]
    proj_t, folded_part = projected(tensor, y_factor, x_factor)
    folded = summed_everywhere(folded_part)
    parts = update_parts(proj_t, folded, lax.axis_size(GY))
    update_t, wide = own_update(exchanged(parts, GY))
    total_x = width_x * lax.axis_size(GX)
    return whitened(cross_terms(wide), update_t, float(total_x) ** 0.5).T


def solution(mesh):
    finer = Mesh(mesh.devices.reshape(2, 4, 2, 2, 8), AXES)
    in_specs = (P(None, GX, GY), P(GY, None), P(None, GX))
    out_specs = P(None, AXES)
    return jax.shard_map(
        per_device, mesh=finer, in_specs=in_specs, out_specs=out_specs, check_vma=False
    )
```

time: 101 us -> 91.6 us (0.907)
  other arithmetic: 12.6 us -> 0.07 us
  blocking collectives: 67.3 us -> 78.7 us
  Pallas kernels: 0 us -> 9.92 us
  matrix products: 6.22 us -> 0 us
  waiting for transfers between devices: 6.6 us -> 1.17 us
  starting transfers between devices: 4.96 us -> 0.05 us
  local copies, waits for them, and re-layouts: 3.19 us -> 1.28 us
    another operation x5 -> x0, other arithmetic: 12.1 us -> none  [the longest x3 6.53 us: per_device(): cholesky_factor = jnp.linalg.cholesky(cross_gram)]
    all_to_all x5 -> x6, blocking collectives: 67.3 us -> 78.7 us  [exchanged(): return lax.all_to_all(tiles, axis, 0, 0, tiled=True)]
    pallas_call x0 -> x4, Pallas kernels: none -> 9.92 us  [the longest x1 5.92 us: projected(): pl.pallas_call(project_kernel, out_shape=[jax.ShapeDtypeStruct((width_x,...]
    dot_general x4 -> x0, matrix products: 5.45 us -> none  [the longest x1 3.58 us: per_device(): jnp.einsum('zxy,yr->xzr', tensor, y_factor, preferred_element_type=jnp.fl...]
    all_to_all x1 -> x0, waiting for transfers between devices: 5.43 us -> none  [exchanged(): return lax.all_to_all(tiles, axis, 0, 0, tiled=True)]
    all_to_all x1 -> x0, starting transfers between devices: 4.92 us -> none  [exchanged(): return lax.all_to_all(tiles, axis, 0, 0, tiled=True)]
  transfers between devices with their start and end apart: 2 -> 1, of which waited for: 2 -> 1; matrix products, arithmetic and copies ran while one was open for 1% -> 0% of each run, Pallas kernels for 0% -> 0%
where the time goes in v2:
time: 91.6 us; the launch traced here: 91.2 us
  blocking collectives  78.7 us (86%)
  Pallas kernels  9.92 us (11%)
  local copies, waits for them, and re-layouts  1.28 us (1%)
  waiting for transfers between devices  1.17 us (1%)
    all_to_all x6, blocking collectives, exchanged(): return lax.all_to_all(tiles, axis, 0, 0, tiled=True)  78.7 us
    pallas_call x1, Pallas kernels, projected(): pl.pallas_call(project_kernel, out_shape=[jax.ShapeDtypeStruct((width_x,...  5.92 us
    pallas_call x1, Pallas kernels, whitened(): pl.pallas_call(functools.partial(whitened_kernel, scale), out_shape=jax.S...  2.56 us
  transfers between devices with their start and end apart: 1, of which 1 were waited for; matrix products, arithmetic and copies ran while one was open for 0% of the time, Pallas kernels for 0%

profile of v2, /device:TPU:2, one launch (start us, length us, event | category | flops | bytes accessed | tf_op | source)
XLA Modules:
  0.0 91.2 jit_solution(2527089742475569658)
XLA Ops:
  0.0 5.9 %projected.1 = (f32[512,512]{1,0:T(8,128)}, f32[64,512]{1,0:T(8,128)}) custom-call(bf16[8,512,512]{2,1,0:T(8,128)(2,1)} %tensor_ref.1, bf16[64,512]{1,0:T(8,128)(2,1)} %bitcast.14, bf16[64,512]{1,0:T(8,128)(2,1)} %x_ref.1), custom_call_target="tpu_custom_call" | custom-call | tf_op jit(solution)/shard_map/projected/pallas_call | solution.py:129
  5.9 14.2 %all_to_all.30 = f32[32,8,128]{2,1,0:T(8,128)S(1)} all-to-all(f32[32,8,128]{2,1,0:T(8,128)} %bitcast.13), channel_id=1, replica_groups=mesh['y_lo'=2,'x'=4,'core'=2,'y_hi'=2,'z'=8] {'y_hi','y_lo','x','core'}, dimensions={0} | all-to-all | bytes 262144 | tf_op jit(solution)/shard_map/all_to_all | solution.py:21
  20.2 16.3 %all_to_all.31 = f32[8,8,128]{2,1,0:T(8,128)S(1)} all-to-all(f32[8,8,128]{2,1,0:T(8,128)S(1)} %broadcast_in_dim.8), channel_id=1, replica_groups=mesh['y_lo'=2,'x'=4,'core'=2,'y_hi'=2,'z'=8] {'z'}, dimensions={0} | all-to-all | bytes 65536 | tf_op jit(solution)/shard_map/all_to_all | solution.py:21
  36.5 11.2 %all_to_all.32 = f32[32,8,128]{2,1,0:T(8,128)S(1)} all-to-all(f32[32,8,128]{2,1,0:T(8,128)S(1)} %broadcast_in_dim.9), channel_id=1, replica_groups=mesh['y_lo'=2,'x'=4,'core'=2,'y_hi'=2,'z'=8] {'y_hi','y_lo','x','core'}, dimensions={0} | all-to-all | bytes 262144 | tf_op jit(solution)/shard_map/all_to_all | solution.py:21
  47.8 0.0 copy-start
  47.8 1.2 %copy-done = f32[512,512]{1,0:T(8,128)S(1)} copy-done((f32[512,512]{1,0:T(8,128)S(1)}, f32[512,512]{1,0:T(8,128)}, u32[]{:S(2)}) %copy-start) | copy-done | bytes 1048600
  49.0 1.1 %update_parts.1 = f32[16,16,128]{2,1,0:T(8,128)S(1)} custom-call(f32[512,512]{1,0:T(8,128)S(1)} %copy-done, f32[64,512]{1,0:T(8,128)S(1)} %bitcast.12), custom_call_target="tpu_custom_call" | custom-call | tf_op jit(solution)/shard_map/update_parts/pallas_call | solution.py:168
  50.1 12.8 %all_to_all.33.parts_ref = f32[16,16,128]{2,1,0:T(8,128)S(1)} all-to-all(f32[16,16,128]{2,1,0:T(8,128)S(1)} %update_parts.1), channel_id=1, replica_groups=mesh['y_lo'=2,'x'=4,'core'=2,'y_hi'=2,'z'=8] {'y_hi','z'}, dimensions={0} | all-to-all | bytes 262144 | tf_op jit(solution)/shard_map/all_to_all | solution.py:21
  62.8 0.4 own_update.1
  63.2 0.0 collective-permute-start
  63.3 1.2 %collective-permute-done = f32[32,128]{1,0:T(8,128)S(1)} collective-permute-done((f32[32,128]{1,0:T(8,128)S(1)}, f32[32,128]{1,0:T(8,128)S(1)}, u32[]{:S(2)}, u32[]{:S(2)}) %collective-permute-start) | collective-permute-done | bytes 16416 | tf_op jit(solution)/shard_map/ppermute | solution.py:47
  64.5 12.1 %all_to_all.34 = f32[16,32,128]{2,1,0:T(8,128)S(1)} all-to-all(f32[16,32,128]{2,1,0:T(8,128)S(1)} %broadcast_in_dim.10), channel_id=1, replica_groups=mesh['y_lo'=2,'x'=4,'core'=2,'y_hi'=2,'z'=8] {'y_hi','y_lo','x'}, dimensions={0} | all-to-all | bytes 524288 | tf_op jit(solution)/shard_map/all_to_all | solution.py:21
  76.6 12.1 %all_to_all.35.cross_ref = f32[8,32,128]{2,1,0:T(8,128)S(1)} all-to-all(f32[8,32,128]{2,1,0:T(8,128)S(1)} %broadcast_in_dim.11), channel_id=1, replica_groups=mesh['y_lo'=2,'x'=4,'core'=2,'y_hi'=2,'z'=8] {'z'}, dimensions={0} | all-to-all | bytes 262144 | tf_op jit(solution)/shard_map/all_to_all | solution.py:21
  88.7 2.6 %whitened.1 = f32[32,64]{1,0:T(8,128)} custom-call(f32[8,32,128]{2,1,0:T(8,128)S(1)} %all_to_all.35.cross_ref, f32[32,64]{1,0:T(8,128)S(1)} %get-tuple-element.12.update_ref), custom_call_target="tpu_custom_call" | custom-call | tf_op jit(solution)/shard_map/whitened/pallas_call | solution.py:273
  (8 shorter events, 0.1 us)
Async XLA Ops:
  47.8 1.2 %copy-start = (f32[512,512]{1,0:T(8,128)S(1)}, f32[512,512]{1,0:T(8,128)}, u32[]{:S(2)}) copy-start(f32[512,512]{1,0:T(8,128)} %get-tuple-element.9.proj_ref) | copy-start | bytes 3145732
  63.2 1.2 %collective-permute-start = (f32[32,128]{1,0:T(8,128)S(1)}, f32[32,128]{1,0:T(8,128)S(1)}, u32[]{:S(2)}, u32[]{:S(2)}) collective-permute-start(f32[32,128]{1,0:T(8,128)S(1)} %get-tuple-element.11), channel_id=1, source_target_pairs={{0,16},{16,0},{1,17},{17,1},{2,18},{18,2},{3,19},{19,3},{4,20},{20... | collective-permute-start | bytes 49160 | tf_op jit(solution)/shard_map/ppermute | solution.py:47

commit v3 on v2

--- a/solution.py
+++ b/solution.py
@@ -11,7 +11,6 @@
 AXES = ("y_lo", "x", "core", "y_hi", "z")
 GX = ("y_lo", "x", "core")
 GY = ("y_hi", "z")
-PLANE = ("y_hi", "y_lo", "x", "core")
 CHIPS = ("y_hi", "y_lo", "x")
 HIGHEST = lax.Precision.HIGHEST
 ON_CHIP = pl.BlockSpec(memory_space=pltpu.VMEM)
@@ -36,11 +35,10 @@
 
 def summed_everywhere(matrix):
     rows, cols = matrix.shape
-    n = lax.axis_size(PLANE)
-    tiles = tiles_of(matrix).reshape(n, -1, 128)
-    own = jnp.sum(exchanged(tiles, PLANE), axis=0)
-    own = jnp.sum(of_everyone(own, "z"), axis=0)
-    return from_tiles(of_everyone(own, PLANE).reshape(-1, 8, 128), rows, cols)
+    tiles = tiles_of(matrix).reshape(lax.axis_size(GX), -1, 128)
+    own = jnp.sum(exchanged(tiles, GX), axis=0)
+    own = jnp.sum(of_everyone(own, GY), axis=0)
+    return from_tiles(of_everyone(own, GX).reshape(-1, 8, 128), rows, cols)
 
 
 def cross_terms(wide):
@@ -58,18 +56,7 @@
 
 
 def project_kernel(
-    tensor_ref,
-    y_ref,
-    x_ref,
-    proj_ref,
-    folded_ref,
-    planes,
-    y_here,
-    x_here,
-    proj_here,
-    folded_here,
-    arrived,
-    left,
+    tensor_ref, y_ref, x_ref, kept_ref, sent_ref, folded_ref, planes, y_here, x_here, arrived
 ):
     depth = planes.shape[0]
     rank = y_ref.shape[0]
@@ -80,18 +67,10 @@
     def plane(z):
         return pltpu.make_async_copy(tensor_ref.at[z], planes.at[z], arrived.at[z])
 
-    def results(pair):
-        lanes = pl.ds(2 * rank * pair, 2 * rank)
-        return [
-            pltpu.make_async_copy(here.at[:, lanes], there.at[:, lanes], left.at[pair, i])
-            for i, (here, there) in enumerate(
-                ((proj_here, proj_ref), (folded_here, folded_ref))
-            )
-        ]
-
     for z in range(depth):
         plane(z).start()
     x_copy.start()
+    first = lax.axis_index("y_hi") == 0
     y_copy.wait()
     y_t = y_here[...]
     none = jnp.zeros_like(y_t)
@@ -107,20 +86,16 @@
             )
             total = term if total is None else total + term
         lanes = pl.ds(2 * rank * pair, 2 * rank)
-        proj_here[:, lanes] = total
-        proj_copy, folded_copy = results(pair)
-        proj_copy.start()
+        half = total.shape[0] // 2
+        kept_ref[:, lanes] = jnp.where(first, total[:half], total[half:])
+        sent_ref[:, lanes] = jnp.where(first, total[half:], total[:half])
         if pair == 0:
             x_copy.wait()
         folded = None
         for part in rounded_parts(total):
             term = jnp.dot(x_here[...], part, preferred_element_type=jnp.float32)
             folded = term if folded is None else folded + term
-        folded_here[:, lanes] = folded
-        folded_copy.start()
-    for pair in range(depth // 2):
-        for copy in results(pair):
-            copy.wait()
+        folded_ref[:, lanes] = folded
 
 
 def projected(tensor, y_factor, x_factor):
@@ -128,31 +103,29 @@
     rank = y_factor.shape[1]
     return pl.pallas_call(
         project_kernel,
-        out_shape=[
-            jax.ShapeDtypeStruct((width_x, depth * rank), jnp.float32),
+        out_shape=(
+            jax.ShapeDtypeStruct((width_x // 2, depth * rank), jnp.float32),
+            jax.ShapeDtypeStruct((width_x // 2, depth * rank), jnp.float32),
             jax.ShapeDtypeStruct((rank, depth * rank), jnp.float32),
-        ],
+        ),
         in_specs=[pl.BlockSpec(memory_space=pltpu.HBM)] * 3,
-        out_specs=[pl.BlockSpec(memory_space=pltpu.HBM)] * 2,
+        out_specs=(ON_CHIP, ON_CHIP, ON_CHIP),
         scratch_shapes=[
             pltpu.VMEM(tensor.shape, tensor.dtype),
             pltpu.VMEM((rank, width_y), y_factor.dtype),
             pltpu.VMEM(x_factor.shape, x_factor.dtype),
-            pltpu.VMEM((width_x, depth * rank), jnp.float32),
-            pltpu.VMEM((rank, depth * rank), jnp.float32),
             pltpu.SemaphoreType.DMA((depth + 2,)),
-            pltpu.SemaphoreType.DMA((depth // 2, 2)),
         ],
-        compiler_params=pltpu.CompilerParams(vmem_limit_bytes=56 * 2**20),
+        compiler_params=pltpu.CompilerParams(vmem_limit_bytes=24 * 2**20),
         name="projected",
-    )(tensor, y_factor.T, x_factor)
-
-
-def update_kernel(proj_ref, folded_ref, out_ref):
+    )(*(pltpu.with_memory_space_constraint(a, pltpu.HBM) for a in (tensor, y_factor.T, x_factor)))
+
+
+def update_kernel(kept_ref, come_ref, folded_ref, out_ref):
     n, half, lanes = out_ref.shape
     rank = lanes // 2
     part = lax.dot_general(
-        proj_ref[...],
+        kept_ref[...] + come_ref[...],
         folded_ref[...],
         (((1,), (1,)), ((), ())),
         precision=HIGHEST,
@@ -162,17 +135,17 @@
     out_ref[...] = jnp.concatenate([part[:, 0], part[:, 1]], axis=2)
 
 
-def update_parts(proj_t, folded, n):
-    width_x = proj_t.shape[0]
+def update_parts(kept, come, folded, n):
+    width_x = kept.shape[0]
     rank = folded.shape[0]
     return pl.pallas_call(
         update_kernel,
         out_shape=jax.ShapeDtypeStruct((n, width_x // n // 2, 2 * rank), jnp.float32),
-        in_specs=[ON_CHIP, ON_CHIP],
+        in_specs=[ON_CHIP] * 3,
         out_specs=ON_CHIP,
         compiler_params=pltpu.CompilerParams(vmem_limit_bytes=24 * 2**20),
         name="update_parts",
-    )(proj_t, folded)
+    )(kept, come, folded)
 
 
 def cross_kernel(parts_ref, update_ref, cross_ref):
@@ -283,10 +256,11 @@
 
 def per_device(tensor, y_factor, x_factor):
     width_x = x_factor.shape[1]
-    proj_t, folded_part = projected(tensor, y_factor, x_factor)
+    kept, sent, folded_part = projected(tensor, y_factor, x_factor)
+    come = lax.ppermute(sent, "y_hi", [(0, 1), (1, 0)])
     folded = summed_everywhere(folded_part)
-    parts = update_parts(proj_t, folded, lax.axis_size(GY))
-    update_t, wide = own_update(exchanged(parts, GY))
+    parts = update_parts(kept, come, folded, lax.axis_size("z"))
+    update_t, wide = own_update(exchanged(parts, "z"))
     total_x = width_x * lax.axis_size(GX)
     return whitened(cross_terms(wide), update_t, float(total_x) ** 0.5).T
 

time: 91.6 us -> 91.9 us (level)
  starting transfers between devices: 0.05 us -> 3.33 us
  local copies, waits for them, and re-layouts: 1.28 us -> 0.05 us
  Pallas kernels: 9.92 us -> 8.82 us
    ppermute x0 -> x1, starting transfers between devices: none -> 3.28 us  [per_device(): come = lax.ppermute(sent, 'y_hi', [(0, 1), (1, 0)])]
    unnamed x2 -> x0, local copies, waits for them, and re-layouts: 1.22 us -> none
  transfers between devices with their start and end apart: 1 -> 2, of which waited for: 1 -> 1; matrix products, arithmetic and copies ran while one was open for 0% -> 0% of each run, Pallas kernels for 0% -> 0%
where the time goes in v3:
time: 91.9 us; the launch traced here: 91.6 us
  blocking collectives  78.1 us (85%)
  Pallas kernels  8.82 us (10%)
  starting transfers between devices  3.33 us (4%)
  waiting for transfers between devices  1.17 us (1%)
    all_to_all x6, blocking collectives, exchanged(): return lax.all_to_all(tiles, axis, 0, 0, tiled=True)  78.1 us
    pallas_call x1, Pallas kernels, projected(): pl.pallas_call(project_kernel, out_shape=(jax.ShapeDtypeStruct((width_x /...  5.25 us
    ppermute x1, starting transfers between devices, per_device(): come = lax.ppermute(sent, 'y_hi', [(0, 1), (1, 0)])  3.28 us
    pallas_call x1, Pallas kernels, whitened(): pl.pallas_call(functools.partial(whitened_kernel, scale), out_shape=jax.S...  2.56 us
  transfers between devices with their start and end apart: 2, of which 1 were waited for; matrix products, arithmetic and copies ran while one was open for 0% of the time, Pallas kernels for 0%

profile of v3, /device:TPU:2, one launch (start us, length us, event | category | flops | bytes accessed | tf_op | source)
XLA Modules:
  0.0 91.6 jit_solution(8780941430742559431)
XLA Ops:
  0.0 5.2 %projected.1 = (f32[256,512]{1,0:T(8,128)S(1)}, f32[256,512]{1,0:T(8,128)S(1)}, f32[64,512]{1,0:T(8,128)S(1)}) custom-call(bf16[8,512,512]{2,1,0:T(8,128)(2,1)} %tensor_ref.1, bf16[64,512]{1,0:T(8,128)(2,1)} %bitcast.14, bf16[64,512]{1,0:T(8,128)(2,1)} %x_ref.1), custom_call_target="tpu_custom_call" | custom-call | tf_op jit(solution)/shard_map/projected/pallas_call | solution.py:104
  5.3 3.3 %collective-permute-start = (f32[256,512]{1,0:T(8,128)S(1)}, f32[256,512]{1,0:T(8,128)S(1)}, u32[]{:S(2)}, u32[]{:S(2)}) collective-permute-start(f32[256,512]{1,0:T(8,128)S(1)} %get-tuple-element.11), channel_id=1, source_target_pairs={{0,8},{8,0},{1,9},{9,1},{2,10},{10,2},{3,11},{11,3},{4,12},{12,4},... | collective-permute-start | bytes 1572872 | tf_op jit(solution)/shard_map/ppermute | solution.py:260
  8.5 13.6 %all_to_all.30 = f32[16,16,128]{2,1,0:T(8,128)S(1)} all-to-all(f32[16,16,128]{2,1,0:T(8,128)S(1)} %bitcast.13), channel_id=1, replica_groups=mesh['y_lo'=2,'x'=4,'core'=2,'y_hi'=2,'z'=8] {'y_lo','x','core'}, dimensions={0} | all-to-all | bytes 262144 | tf_op jit(solution)/shard_map/all_to_all | solution.py:20
  22.2 19.9 %all_to_all.31 = f32[16,16,128]{2,1,0:T(8,128)S(1)} all-to-all(f32[16,16,128]{2,1,0:T(8,128)S(1)} %broadcast_in_dim.8), channel_id=1, replica_groups=mesh['y_lo'=2,'x'=4,'core'=2,'y_hi'=2,'z'=8] {'y_hi','z'}, dimensions={0} | all-to-all | bytes 262144 | tf_op jit(solution)/shard_map/all_to_all | solution.py:20
  42.1 9.5 %all_to_all.32 = f32[16,16,128]{2,1,0:T(8,128)S(1)} all-to-all(f32[16,16,128]{2,1,0:T(8,128)S(1)} %broadcast_in_dim.9), channel_id=1, replica_groups=mesh['y_lo'=2,'x'=4,'core'=2,'y_hi'=2,'z'=8] {'y_lo','x','core'}, dimensions={0} | all-to-all | bytes 262144 | tf_op jit(solution)/shard_map/all_to_all | solution.py:20
  51.7 0.0 collective-permute-done.come_ref
  51.7 0.7 update_parts.1
  52.3 11.4 %all_to_all.33.parts_ref = f32[8,16,128]{2,1,0:T(8,128)S(1)} all-to-all(f32[8,16,128]{2,1,0:T(8,128)S(1)} %update_parts.1), channel_id=1, replica_groups=mesh['y_lo'=2,'x'=4,'core'=2,'y_hi'=2,'z'=8] {'z'}, dimensions={0} | all-to-all | bytes 131072 | tf_op jit(solution)/shard_map/all_to_all | solution.py:20
  63.8 0.4 own_update.1
  64.1 0.0 collective-permute-start.1
  64.2 1.2 %collective-permute-done.1 = f32[32,128]{1,0:T(8,128)S(1)} collective-permute-done((f32[32,128]{1,0:T(8,128)S(1)}, f32[32,128]{1,0:T(8,128)S(1)}, u32[]{:S(2)}, u32[]{:S(2)}) %collective-permute-start.1) | collective-permute-done | bytes 16416 | tf_op jit(solution)/shard_map/ppermute | solution.py:45
  65.4 12.1 %all_to_all.34 = f32[16,32,128]{2,1,0:T(8,128)S(1)} all-to-all(f32[16,32,128]{2,1,0:T(8,128)S(1)} %broadcast_in_dim.10), channel_id=1, replica_groups=mesh['y_lo'=2,'x'=4,'core'=2,'y_hi'=2,'z'=8] {'y_hi','y_lo','x'}, dimensions={0} | all-to-all | bytes 524288 | tf_op jit(solution)/shard_map/all_to_all | solution.py:20
  77.5 11.5 %all_to_all.35.cross_ref = f32[8,32,128]{2,1,0:T(8,128)S(1)} all-to-all(f32[8,32,128]{2,1,0:T(8,128)S(1)} %broadcast_in_dim.11), channel_id=1, replica_groups=mesh['y_lo'=2,'x'=4,'core'=2,'y_hi'=2,'z'=8] {'z'}, dimensions={0} | all-to-all | bytes 262144 | tf_op jit(solution)/shard_map/all_to_all | solution.py:20
  89.0 2.6 %whitened.1 = f32[32,64]{1,0:T(8,128)} custom-call(f32[8,32,128]{2,1,0:T(8,128)S(1)} %all_to_all.35.cross_ref, f32[32,64]{1,0:T(8,128)S(1)} %get-tuple-element.14.update_ref), custom_call_target="tpu_custom_call" | custom-call | tf_op jit(solution)/shard_map/whitened/pallas_call | solution.py:246
  (8 shorter events, 0.1 us)
Async XLA Ops:
  5.3 46.4 %collective-permute-start = (f32[256,512]{1,0:T(8,128)S(1)}, f32[256,512]{1,0:T(8,128)S(1)}, u32[]{:S(2)}, u32[]{:S(2)}) collective-permute-start(f32[256,512]{1,0:T(8,128)S(1)} %get-tuple-element.11), channel_id=1, source_target_pairs={{0,8},{8,0},{1,9},{9,1},{2,10},{10,2},{3,11},{11,3},{4,12},{12,4},... | collective-permute-start | bytes 1572872 | tf_op jit(solution)/shard_map/ppermute | solution.py:260
  64.1 1.2 %collective-permute-start.1 = (f32[32,128]{1,0:T(8,128)S(1)}, f32[32,128]{1,0:T(8,128)S(1)}, u32[]{:S(2)}, u32[]{:S(2)}) collective-permute-start(f32[32,128]{1,0:T(8,128)S(1)} %get-tuple-element.13), channel_id=1, source_target_pairs={{0,16},{16,0},{1,17},{17,1},{2,18},{18,2},{3,19},{19,3},{4,20},{20... | collective-permute-start | bytes 49160 | tf_op jit(solution)/shard_map/ppermute | solution.py:45

commit v4 on v3

--- a/solution.py
+++ b/solution.py
@@ -11,6 +11,7 @@
 AXES = ("y_lo", "x", "core", "y_hi", "z")
 GX = ("y_lo", "x", "core")
 GY = ("y_hi", "z")
+PLANE = ("y_hi", "y_lo", "x", "core")
 CHIPS = ("y_hi", "y_lo", "x")
 HIGHEST = lax.Precision.HIGHEST
 ON_CHIP = pl.BlockSpec(memory_space=pltpu.VMEM)
@@ -33,18 +34,20 @@
     return tiles.reshape(rows // 8, cols // 128, 8, 128).swapaxes(1, 2).reshape(rows, cols)
 
 
-def summed_everywhere(matrix):
+def summed_everywhere(matrix, sent):
     rows, cols = matrix.shape
-    tiles = tiles_of(matrix).reshape(lax.axis_size(GX), -1, 128)
-    own = jnp.sum(exchanged(tiles, GX), axis=0)
-    own = jnp.sum(of_everyone(own, GY), axis=0)
-    return from_tiles(of_everyone(own, GX).reshape(-1, 8, 128), rows, cols)
-
-
-def cross_terms(wide):
-    wide = wide + lax.ppermute(wide, "core", [(0, 1), (1, 0)])
-    wide = jnp.sum(of_everyone(wide, CHIPS), axis=0)
-    return of_everyone(wide, "z")
+    tiles = tiles_of(matrix).reshape(lax.axis_size(PLANE), -1, 128)
+    own = jnp.sum(exchanged(tiles, PLANE), axis=0)
+    own, sent = lax.optimization_barrier((own, sent))
+    come = lax.ppermute(sent, "y_hi", [(0, 1), (1, 0)])
+    own = jnp.sum(of_everyone(own, "z"), axis=0)
+    everything = of_everyone(own, PLANE).reshape(-1, 8, 128)
+    return from_tiles(everything, rows, cols), come
+
+
+def with_neighbour(value, axis):
+    pairs = [(i, i ^ 1) for i in range(lax.axis_size(axis))]
+    return value + lax.ppermute(value, axis, pairs)
 
 
 def rounded_parts(matrix):
@@ -122,8 +125,9 @@
 
 
 def update_kernel(kept_ref, come_ref, folded_ref, out_ref):
-    n, half, lanes = out_ref.shape
+    n, rows, lanes = out_ref.shape
     rank = lanes // 2
+    half = 2 * rows // n
     part = lax.dot_general(
         kept_ref[...] + come_ref[...],
         folded_ref[...],
@@ -132,7 +136,10 @@
         preferred_element_type=jnp.float32,
     )
     part = part.reshape(n, 2, half, rank)
-    out_ref[...] = jnp.concatenate([part[:, 0], part[:, 1]], axis=2)
+    packed = jnp.concatenate([part[:, 0], part[:, 1]], axis=2)
+    packed = packed.reshape(n // 2, 2, half, lanes)
+    for z in range(n):
+        out_ref[z] = packed[:, z % 2].reshape(rows, lanes)
 
 
 def update_parts(kept, come, folded, n):
@@ -140,7 +147,7 @@
     rank = folded.shape[0]
     return pl.pallas_call(
         update_kernel,
-        out_shape=jax.ShapeDtypeStruct((n, width_x // n // 2, 2 * rank), jnp.float32),
+        out_shape=jax.ShapeDtypeStruct((n, width_x // 4, 2 * rank), jnp.float32),
         in_specs=[ON_CHIP] * 3,
         out_specs=ON_CHIP,
         compiler_params=pltpu.CompilerParams(vmem_limit_bytes=24 * 2**20),
@@ -148,11 +155,12 @@
     )(kept, come, folded)
 
 
-def cross_kernel(parts_ref, update_ref, cross_ref):
+def cross_kernel(parts_ref, update_ref, cross_ref, packed_ref):
     rank = update_ref.shape[1]
+    half = update_ref.shape[0] // 2
     packed = jnp.sum(parts_ref[...], axis=0)
+    packed_ref[...] = packed
     update_t = jnp.concatenate([packed[:, :rank], packed[:, rank:]], axis=0)
-    update_ref[...] = update_t
     square = lax.dot_general(
         update_t,
         update_t,
@@ -161,19 +169,23 @@
         preferred_element_type=jnp.float32,
     )
     cross_ref[...] = jnp.concatenate([square[: rank // 2], square[rank // 2 :]], axis=1)
+    start = pl.multiple_of(lax.axis_index("z") // 2 * half, half)
+    own = packed_ref[pl.ds(start, half), :]
+    update_ref[...] = jnp.concatenate([own[:, :rank], own[:, rank:]], axis=0)
 
 
 def own_update(parts):
-    _, half, lanes = parts.shape
+    n, rows, lanes = parts.shape
     rank = lanes // 2
     return pl.pallas_call(
         cross_kernel,
         out_shape=(
-            jax.ShapeDtypeStruct((2 * half, rank), jnp.float32),
+            jax.ShapeDtypeStruct((4 * rows // n, rank), jnp.float32),
             jax.ShapeDtypeStruct((rank // 2, 2 * rank), jnp.float32),
         ),
         in_specs=[ON_CHIP],
         out_specs=(ON_CHIP, ON_CHIP),
+        scratch_shapes=[pltpu.VMEM((rows, lanes), jnp.float32)],
         compiler_params=pltpu.CompilerParams(vmem_limit_bytes=8 * 2**20),
         name="own_update",
     )(parts)
@@ -257,12 +269,12 @@
 def per_device(tensor, y_factor, x_factor):
     width_x = x_factor.shape[1]
     kept, sent, folded_part = projected(tensor, y_factor, x_factor)
-    come = lax.ppermute(sent, "y_hi", [(0, 1), (1, 0)])
-    folded = summed_everywhere(folded_part)
+    folded, come = summed_everywhere(folded_part, sent)
     parts = update_parts(kept, come, folded, lax.axis_size("z"))
     update_t, wide = own_update(exchanged(parts, "z"))
+    wide = with_neighbour(with_neighbour(wide, "core"), "z")
     total_x = width_x * lax.axis_size(GX)
-    return whitened(cross_terms(wide), update_t, float(total_x) ** 0.5).T
+    return whitened(of_everyone(wide, CHIPS), update_t, float(total_x) ** 0.5).T
 
 
 def solution(mesh):

time: 91.9 us -> 84.6 us (0.921)
  blocking collectives: 78.1 us -> 69 us
  waiting for transfers between devices: 1.17 us -> 4.33 us
  starting transfers between devices: 3.33 us -> 2 us
    all_to_all x6 -> x5, blocking collectives: 78.1 us -> 69 us  [exchanged(): return lax.all_to_all(tiles, axis, 0, 0, tiled=True)]
    ppermute x2 -> x3, waiting for transfers between devices: 1.17 us -> 4.33 us  [the longest x2 4.33 us: with_neighbour(): return value + lax.ppermute(value, axis, pairs)]
    ppermute x2 -> x3, starting transfers between devices: 3.33 us -> 2 us  [the longest x1 1.38 us: summed_everywhere(): come = lax.ppermute(sent, 'y_hi', [(0, 1), (1, 0)])]
  transfers between devices with their start and end apart: 2 -> 3, of which waited for: 1 -> 2; matrix products, arithmetic and copies ran while one was open for 0% -> 0% of each run, Pallas kernels for 0% -> 0%
where the time goes in v4:
time: 84.6 us; the launch traced here: 84.3 us
  blocking collectives  69 us (82%)
  Pallas kernels  8.82 us (10%)
  waiting for transfers between devices  4.33 us (5%)
  starting transfers between devices  2 us (2%)
    all_to_all x5, blocking collectives, exchanged(): return lax.all_to_all(tiles, axis, 0, 0, tiled=True)  69 us
    pallas_call x1, Pallas kernels, projected(): pl.pallas_call(project_kernel, out_shape=(jax.ShapeDtypeStruct((width_x /...  5.25 us
    ppermute x2, waiting for transfers between devices, with_neighbour(): return value + lax.ppermute(value, axis, pairs)  4.33 us
    pallas_call x1, Pallas kernels, whitened(): pl.pallas_call(functools.partial(whitened_kernel, scale), out_shape=jax.S...  2.56 us
  transfers between devices with their start and end apart: 3, of which 2 were waited for; matrix products, arithmetic and copies ran while one was open for 0% of the time, Pallas kernels for 0%

profile of v4, /device:TPU:2, one launch (start us, length us, event | category | flops | bytes accessed | tf_op | source)
XLA Modules:
  0.0 84.3 jit_solution(7152805566579302349)
XLA Ops:
  0.0 5.2 %projected.1 = (f32[256,512]{1,0:T(8,128)S(1)}, f32[256,512]{1,0:T(8,128)S(1)}, f32[64,512]{1,0:T(8,128)S(1)}) custom-call(bf16[8,512,512]{2,1,0:T(8,128)(2,1)} %tensor_ref.1, bf16[64,512]{1,0:T(8,128)(2,1)} %bitcast.14, bf16[64,512]{1,0:T(8,128)(2,1)} %x_ref.1), custom_call_target="tpu_custom_call" | custom-call | tf_op jit(solution)/shard_map/projected/pallas_call | solution.py:107
  5.3 14.0 %all_to_all.25 = f32[32,8,128]{2,1,0:T(8,128)S(1)} all-to-all(f32[32,8,128]{2,1,0:T(8,128)S(1)} %bitcast.13), channel_id=1, replica_groups=mesh['y_lo'=2,'x'=4,'core'=2,'y_hi'=2,'z'=8] {'y_hi','y_lo','x','core'}, dimensions={0} | all-to-all | bytes 262144 | tf_op jit(solution)/shard_map/all_to_all | solution.py:21
  19.3 1.4 %collective-permute-start = (f32[256,512]{1,0:T(8,128)S(1)}, f32[256,512]{1,0:T(8,128)S(1)}, u32[]{:S(2)}, u32[]{:S(2)}) collective-permute-start(f32[256,512]{1,0:T(8,128)S(1)} %get-tuple-element.15), channel_id=1, source_target_pairs={{0,8},{8,0},{1,9},{9,1},{2,10},{10,2},{3,11},{11,3},{4,12},{12,4},... | collective-permute-start | bytes 1572872 | tf_op jit(solution)/shard_map/ppermute | solution.py:42
  20.7 16.3 %all_to_all.26 = f32[8,8,128]{2,1,0:T(8,128)S(1)} all-to-all(f32[8,8,128]{2,1,0:T(8,128)S(1)} %broadcast_in_dim.6), channel_id=1, replica_groups=mesh['y_lo'=2,'x'=4,'core'=2,'y_hi'=2,'z'=8] {'z'}, dimensions={0} | all-to-all | bytes 65536 | tf_op jit(solution)/shard_map/all_to_all | solution.py:21
  37.0 12.2 %all_to_all.27 = f32[32,8,128]{2,1,0:T(8,128)S(1)} all-to-all(f32[32,8,128]{2,1,0:T(8,128)S(1)} %broadcast_in_dim.7), channel_id=1, replica_groups=mesh['y_lo'=2,'x'=4,'core'=2,'y_hi'=2,'z'=8] {'y_hi','y_lo','x','core'}, dimensions={0} | all-to-all | bytes 262144 | tf_op jit(solution)/shard_map/all_to_all | solution.py:21
  49.2 0.0 collective-permute-done.come_ref
  49.2 0.7 update_parts.1
  49.8 14.9 %all_to_all.28.parts_ref = f32[8,64,128]{2,1,0:T(8,128)S(1)} all-to-all(f32[8,64,128]{2,1,0:T(8,128)S(1)} %update_parts.1), channel_id=1, replica_groups=mesh['y_lo'=2,'x'=4,'core'=2,'y_hi'=2,'z'=8] {'z'}, dimensions={0} | all-to-all | bytes 524288 | tf_op jit(solution)/shard_map/all_to_all | solution.py:21
  64.7 0.4 own_update.1
  65.1 0.1 collective-permute-start.1
  65.1 1.2 %collective-permute-done.1 = f32[32,128]{1,0:T(8,128)S(1)} collective-permute-done((f32[32,128]{1,0:T(8,128)S(1)}, f32[32,128]{1,0:T(8,128)S(1)}, u32[]{:S(2)}, u32[]{:S(2)}) %collective-permute-start.1) | collective-permute-done | bytes 16416 | tf_op jit(solution)/shard_map/ppermute | solution.py:50
  66.3 0.6 collective-permute-start.2
  66.9 3.2 %collective-permute-done.2 = f32[32,128]{1,0:T(8,128)S(1)} collective-permute-done((f32[32,128]{1,0:T(8,128)S(1)}, f32[32,128]{1,0:T(8,128)S(1)}, u32[]{:S(2)}, u32[]{:S(2)}) %collective-permute-start.2) | collective-permute-done | bytes 16416 | tf_op jit(solution)/shard_map/ppermute | solution.py:50
  70.1 11.7 %all_to_all.29.cross_ref = f32[16,32,128]{2,1,0:T(8,128)S(1)} all-to-all(f32[16,32,128]{2,1,0:T(8,128)S(1)} %broadcast_in_dim.8), channel_id=1, replica_groups=mesh['y_lo'=2,'x'=4,'core'=2,'y_hi'=2,'z'=8] {'y_hi','y_lo','x'}, dimensions={0} | all-to-all | bytes 524288 | tf_op jit(solution)/shard_map/all_to_all | solution.py:21
  81.7 2.6 %whitened.1 = f32[32,64]{1,0:T(8,128)} custom-call(f32[16,32,128]{2,1,0:T(8,128)S(1)} %all_to_all.29.cross_ref, f32[32,64]{1,0:T(8,128)S(1)} %get-tuple-element.18.update_ref), custom_call_target="tpu_custom_call" | custom-call | tf_op jit(solution)/shard_map/whitened/pallas_call | solution.py:258
  (7 shorter events, 0.1 us)
Async XLA Ops:
  19.3 29.9 %collective-permute-start = (f32[256,512]{1,0:T(8,128)S(1)}, f32[256,512]{1,0:T(8,128)S(1)}, u32[]{:S(2)}, u32[]{:S(2)}) collective-permute-start(f32[256,512]{1,0:T(8,128)S(1)} %get-tuple-element.15), channel_id=1, source_target_pairs={{0,8},{8,0},{1,9},{9,1},{2,10},{10,2},{3,11},{11,3},{4,12},{12,4},... | collective-permute-start | bytes 1572872 | tf_op jit(solution)/shard_map/ppermute | solution.py:42
  65.1 1.2 %collective-permute-start.1 = (f32[32,128]{1,0:T(8,128)S(1)}, f32[32,128]{1,0:T(8,128)S(1)}, u32[]{:S(2)}, u32[]{:S(2)}) collective-permute-start(f32[32,128]{1,0:T(8,128)S(1)} %get-tuple-element.17), channel_id=1, source_target_pairs={{0,16},{16,0},{1,17},{17,1},{2,18},{18,2},{3,19},{19,3},{4,20},{20... | collective-permute-start | bytes 49160 | tf_op jit(solution)/shard_map/ppermute | solution.py:50
  66.3 3.7 %collective-permute-start.2 = (f32[32,128]{1,0:T(8,128)S(1)}, f32[32,128]{1,0:T(8,128)S(1)}, u32[]{:S(2)}, u32[]{:S(2)}) collective-permute-start(f32[32,128]{1,0:T(8,128)S(1)} %add.6), channel_id=1, source_target_pairs={{0,1},{1,0},{2,3},{3,2},{4,5},{5,4},{6,7},{7,6},{8,9},{9,8},{10,11... | collective-permute-start | bytes 49160 | tf_op jit(solution)/shard_map/ppermute | solution.py:50

commit v5 on v4

--- a/solution.py
+++ b/solution.py
@@ -11,9 +11,9 @@
 AXES = ("y_lo", "x", "core", "y_hi", "z")
 GX = ("y_lo", "x", "core")
 GY = ("y_hi", "z")
-PLANE = ("y_hi", "y_lo", "x", "core")
 CHIPS = ("y_hi", "y_lo", "x")
 HIGHEST = lax.Precision.HIGHEST
+EARLY = 6
 ON_CHIP = pl.BlockSpec(memory_space=pltpu.VMEM)
 
 
@@ -34,20 +34,24 @@
     return tiles.reshape(rows // 8, cols // 128, 8, 128).swapaxes(1, 2).reshape(rows, cols)
 
 
-def summed_everywhere(matrix, sent):
-    rows, cols = matrix.shape
-    tiles = tiles_of(matrix).reshape(lax.axis_size(PLANE), -1, 128)
-    own = jnp.sum(exchanged(tiles, PLANE), axis=0)
-    own, sent = lax.optimization_barrier((own, sent))
-    come = lax.ppermute(sent, "y_hi", [(0, 1), (1, 0)])
-    own = jnp.sum(of_everyone(own, "z"), axis=0)
-    everything = of_everyone(own, PLANE).reshape(-1, 8, 128)
-    return from_tiles(everything, rows, cols), come
+def from_partner(array, axis):
+    return lax.ppermute(array, axis, [(i, i ^ 1) for i in range(lax.axis_size(axis))])
+
+
+def summed_everywhere(own, other, sent):
+    rows, cols = own.shape
+    own = own + from_partner(other, "core")
+    tiles = tiles_of(own).reshape(lax.axis_size(CHIPS), -1, 128)
+    tile = jnp.sum(exchanged(tiles, CHIPS), axis=0)
+    tile, sent = lax.optimization_barrier((tile, sent))
+    come = from_partner(sent, "y_hi")
+    tile = jnp.sum(of_everyone(tile, "z"), axis=0)
+    own = from_tiles(of_everyone(tile, CHIPS).reshape(-1, 8, 128), rows, cols)
+    return own, from_partner(own, "core"), come
 
 
 def with_neighbour(value, axis):
-    pairs = [(i, i ^ 1) for i in range(lax.axis_size(axis))]
-    return value + lax.ppermute(value, axis, pairs)
+    return value + from_partner(value, axis)
 
 
 def rounded_parts(matrix):
@@ -59,10 +63,21 @@
 
 
 def project_kernel(
-    tensor_ref, y_ref, x_ref, kept_ref, sent_ref, folded_ref, planes, y_here, x_here, arrived
+    tensor_ref,
+    y_ref,
+    x_ref,
+    kept_ref,
+    sent_ref,
+    own_ref,
+    other_ref,
+    planes,
+    y_here,
+    x_here,
+    arrived,
 ):
-    depth = planes.shape[0]
+    depth, width_x, _ = planes.shape
     rank = y_ref.shape[0]
+    half = width_x // 2
     y_copy = pltpu.make_async_copy(y_ref, y_here, arrived.at[depth])
     x_copy = pltpu.make_async_copy(x_ref, x_here, arrived.at[depth + 1])
     y_copy.start()
@@ -70,49 +85,64 @@
     def plane(z):
         return pltpu.make_async_copy(tensor_ref.at[z], planes.at[z], arrived.at[z])
 
-    for z in range(depth):
+    for z in range(EARLY):
         plane(z).start()
     x_copy.start()
-    first = lax.axis_index("y_hi") == 0
+    kept_at = pl.multiple_of(lax.axis_index("y_hi") * half, half)
+    sides = ((kept_ref, kept_at), (sent_ref, pl.multiple_of(half - kept_at, half)))
+    first = lax.axis_index("core") == 0
     y_copy.wait()
     y_t = y_here[...]
     none = jnp.zeros_like(y_t)
-    sides = (jnp.concatenate([y_t, none], axis=0), jnp.concatenate([none, y_t], axis=0))
+    y_left, y_right = jnp.concatenate([y_t, none], axis=0), jnp.concatenate([none, y_t], axis=0)
     contract = (((1,), (1,)), ((), ()))
-    for pair in range(depth // 2):
-        total = None
-        for side in range(2):
-            z = 2 * pair + side
-            plane(z).wait()
-            term = lax.dot_general(
-                planes[z], sides[side], contract, preferred_element_type=jnp.float32
-            )
-            total = term if total is None else total + term
-        lanes = pl.ds(2 * rank * pair, 2 * rank)
-        half = total.shape[0] // 2
-        kept_ref[:, lanes] = jnp.where(first, total[:half], total[half:])
-        sent_ref[:, lanes] = jnp.where(first, total[half:], total[:half])
-        if pair == 0:
+    pairs = depth // 2
+    for step in range(pairs + 1):
+        if step < pairs:
+            plane(2 * step).wait()
+            plane(2 * step + 1).wait()
+            for z in range(2 * step + EARLY, min(2 * step + EARLY + 2, depth)):
+                plane(z).start()
+        if step == 1:
             x_copy.wait()
         folded = None
-        for part in rounded_parts(total):
-            term = jnp.dot(x_here[...], part, preferred_element_type=jnp.float32)
-            folded = term if folded is None else folded + term
-        folded_ref[:, lanes] = folded
+        for there, start in sides:
+            if step < pairs:
+                rows = pl.ds(start, half)
+                left = lax.dot_general(
+                    planes[2 * step, rows, :], y_left, contract, preferred_element_type=jnp.float32
+                )
+                right = lax.dot_general(
+                    planes[2 * step + 1, rows, :],
+                    y_right,
+                    contract,
+                    preferred_element_type=jnp.float32,
+                )
+                there[:, pl.ds(2 * rank * step, 2 * rank)] = left + right
+            if step > 0:
+                x_part = x_here[:, pl.ds(start, half)]
+                for part in rounded_parts(there[:, pl.ds(2 * rank * (step - 1), 2 * rank)]):
+                    term = jnp.dot(x_part, part, preferred_element_type=jnp.float32)
+                    folded = term if folded is None else folded + term
+        if step > 0:
+            lanes = pl.ds(2 * rank * (step - 1), 2 * rank)
+            upper, lower = folded[: rank // 2], folded[rank // 2 :]
+            own_ref[:, lanes] = jnp.where(first, upper, lower)
+            other_ref[:, lanes] = jnp.where(first, lower, upper)
 
 
 def projected(tensor, y_factor, x_factor):
     depth, width_x, width_y = tensor.shape
     rank = y_factor.shape[1]
+    rows = depth * rank
     return pl.pallas_call(
         project_kernel,
-        out_shape=(
-            jax.ShapeDtypeStruct((width_x // 2, depth * rank), jnp.float32),
-            jax.ShapeDtypeStruct((width_x // 2, depth * rank), jnp.float32),
-            jax.ShapeDtypeStruct((rank, depth * rank), jnp.float32),
-        ),
+        out_shape=[
+            jax.ShapeDtypeStruct((n, rows), jnp.float32)
+            for n in (width_x // 2, width_x // 2, rank // 2, rank // 2)
+        ],
         in_specs=[pl.BlockSpec(memory_space=pltpu.HBM)] * 3,
-        out_specs=(ON_CHIP, ON_CHIP, ON_CHIP),
+        out_specs=[ON_CHIP] * 4,
         scratch_shapes=[
             pltpu.VMEM(tensor.shape, tensor.dtype),
             pltpu.VMEM((rank, width_y), y_factor.dtype),
@@ -124,13 +154,16 @@
     )(*(pltpu.with_memory_space_constraint(a, pltpu.HBM) for a in (tensor, y_factor.T, x_factor)))
 
 
-def update_kernel(kept_ref, come_ref, folded_ref, out_ref):
+def update_kernel(kept_ref, come_ref, own_ref, other_ref, out_ref):
     n, rows, lanes = out_ref.shape
     rank = lanes // 2
     half = 2 * rows // n
+    first = lax.axis_index("core") == 0
+    own, other = own_ref[...], other_ref[...]
+    folded = jnp.concatenate([jnp.where(first, own, other), jnp.where(first, other, own)], axis=0)
     part = lax.dot_general(
         kept_ref[...] + come_ref[...],
-        folded_ref[...],
+        folded,
         (((1,), (1,)), ((), ())),
         precision=HIGHEST,
         preferred_element_type=jnp.float32,
@@ -142,17 +175,17 @@
         out_ref[z] = packed[:, z % 2].reshape(rows, lanes)
 
 
-def update_parts(kept, come, folded, n):
+def update_parts(kept, come, own, other, n):
     width_x = kept.shape[0]
-    rank = folded.shape[0]
+    rank = 2 * own.shape[0]
     return pl.pallas_call(
         update_kernel,
         out_shape=jax.ShapeDtypeStruct((n, width_x // 4, 2 * rank), jnp.float32),
-        in_specs=[ON_CHIP] * 3,
+        in_specs=[ON_CHIP] * 4,
         out_specs=ON_CHIP,
         compiler_params=pltpu.CompilerParams(vmem_limit_bytes=24 * 2**20),
         name="update_parts",
-    )(kept, come, folded)
+    )(kept, come, own, other)
 
 
 def cross_kernel(parts_ref, update_ref, cross_ref, packed_ref):
@@ -268,9 +301,9 @@
 
 def per_device(tensor, y_factor, x_factor):
     width_x = x_factor.shape[1]
-    kept, sent, folded_part = projected(tensor, y_factor, x_factor)
-    folded, come = summed_everywhere(folded_part, sent)
-    parts = update_parts(kept, come, folded, lax.axis_size("z"))
+    kept, sent, own, other = projected(tensor, y_factor, x_factor)
+    own, other, come = summed_everywhere(own, other, sent)
+    parts = update_parts(kept, come, own, other, lax.axis_size("z"))
     update_t, wide = own_update(exchanged(parts, "z"))
     wide = with_neighbour(with_neighbour(wide, "core"), "z")
     total_x = width_x * lax.axis_size(GX)

time: 84.6 us -> 84.8 us (level)
  waiting for transfers between devices: 4.33 us -> 6.83 us
  Pallas kernels: 8.82 us -> 7.15 us
    ppermute x3 -> x5, waiting for transfers between devices: 4.33 us -> 6.83 us  [from_partner(): lax.ppermute(array, axis, [(i, i ^ 1) for i in range(lax.axis_size(axis))])]
    pallas_call x1, Pallas kernels: 5.25 us -> 3.57 us  [projected(): pl.pallas_call(project_kernel, out_shape=[jax.ShapeDtypeStruct((n, rows),...]
    ppermute x3 -> x5, starting transfers between devices: 2 us -> 1.98 us  [from_partner(): lax.ppermute(array, axis, [(i, i ^ 1) for i in range(lax.axis_size(axis))])]
  transfers between devices with their start and end apart: 3 -> 5, of which waited for: 2 -> 4; matrix products, arithmetic and copies ran while one was open for 0% -> 0% of each run, Pallas kernels for 0% -> 0%
where the time goes in v5:
time: 84.8 us; the launch traced here: 84.6 us
  blocking collectives  68.5 us (81%)
  Pallas kernels  7.15 us (8%)
  waiting for transfers between devices  6.83 us (8%)
  starting transfers between devices  1.98 us (2%)
    all_to_all x5, blocking collectives, exchanged(): return lax.all_to_all(tiles, axis, 0, 0, tiled=True)  68.5 us
    ppermute x5, waiting for transfers between devices, from_partner(): lax.ppermute(array, axis, [(i, i ^ 1) for i in range(lax.axis_size(axis))])  6.83 us
    pallas_call x1, Pallas kernels, projected(): pl.pallas_call(project_kernel, out_shape=[jax.ShapeDtypeStruct((n, rows),...  3.57 us
    pallas_call x1, Pallas kernels, whitened(): pl.pallas_call(functools.partial(whitened_kernel, scale), out_shape=jax.S...  2.56 us
    ppermute x5, starting transfers between devices, from_partner(): lax.ppermute(array, axis, [(i, i ^ 1) for i in range(lax.axis_size(axis))])  1.98 us
  transfers between devices with their start and end apart: 5, of which 4 were waited for; matrix products, arithmetic and copies ran while one was open for 0% of the time, Pallas kernels for 0%

profile of v5, /device:TPU:2, one launch (start us, length us, event | category | flops | bytes accessed | tf_op | source)
XLA Modules:
  0.0 84.6 jit_solution(15541042867799852233)
XLA Ops:
  0.0 3.6 %projected.1 = (f32[256,512]{1,0:T(8,128)S(1)}, f32[256,512]{1,0:T(8,128)S(1)}, f32[32,512]{1,0:T(8,128)S(1)}, f32[32,512]{1,0:T(8,128)S(1)}) custom-call(bf16[8,512,512]{2,1,0:T(8,128)(2,1)} %tensor_ref.1, bf16[64,512]{1,0:T(8,128)(2,1)} %bitcast.15, bf16[64,512]{1,0:T(8,128)(2,1)} %x_ref.1), custom_call_target="tpu_custom_call" | custom-call | tf_op jit(solution)/shard_map/projected/pallas_call | solution.py:138
  3.6 0.1 collective-permute-start
  3.7 1.2 %collective-permute-done = f32[32,512]{1,0:T(8,128)S(1)} collective-permute-done((f32[32,512]{1,0:T(8,128)S(1)}, f32[32,512]{1,0:T(8,128)S(1)}, u32[]{:S(2)}, u32[]{:S(2)}) %collective-permute-start) | collective-permute-done | bytes 65568 | tf_op jit(solution)/shard_map/ppermute | solution.py:38
  4.9 13.6 %all_to_all.25 = f32[16,8,128]{2,1,0:T(8,128)S(1)} all-to-all(f32[16,8,128]{2,1,0:T(8,128)S(1)} %bitcast.14), channel_id=1, replica_groups=mesh['y_lo'=2,'x'=4,'core'=2,'y_hi'=2,'z'=8] {'y_hi','y_lo','x'}, dimensions={0} | all-to-all | bytes 131072 | tf_op jit(solution)/shard_map/all_to_all | solution.py:21
  18.5 1.3 %collective-permute-start.1 = (f32[256,512]{1,0:T(8,128)S(1)}, f32[256,512]{1,0:T(8,128)S(1)}, u32[]{:S(2)}, u32[]{:S(2)}) collective-permute-start(f32[256,512]{1,0:T(8,128)S(1)} %get-tuple-element.17), channel_id=1, source_target_pairs={{0,8},{8,0},{1,9},{9,1},{2,10},{10,2},{3,11},{11,3},{4,12},{12,4},... | collective-permute-start | bytes 1572872 | tf_op jit(solution)/shard_map/ppermute | solution.py:38
  19.8 16.3 %all_to_all.26 = f32[8,8,128]{2,1,0:T(8,128)S(1)} all-to-all(f32[8,8,128]{2,1,0:T(8,128)S(1)} %broadcast_in_dim.6), channel_id=1, replica_groups=mesh['y_lo'=2,'x'=4,'core'=2,'y_hi'=2,'z'=8] {'z'}, dimensions={0} | all-to-all | bytes 65536 | tf_op jit(solution)/shard_map/all_to_all | solution.py:21
  36.1 11.9 %all_to_all.27 = f32[16,8,128]{2,1,0:T(8,128)S(1)} all-to-all(f32[16,8,128]{2,1,0:T(8,128)S(1)} %broadcast_in_dim.7), channel_id=1, replica_groups=mesh['y_lo'=2,'x'=4,'core'=2,'y_hi'=2,'z'=8] {'y_hi','y_lo','x'}, dimensions={0} | all-to-all | bytes 131072 | tf_op jit(solution)/shard_map/all_to_all | solution.py:21
  48.0 0.0 collective-permute-start.2
  48.0 1.3 %collective-permute-done.2.other_ref = f32[32,512]{1,0:T(8,128)S(1)} collective-permute-done((f32[32,512]{1,0:T(8,128)S(1)}, f32[32,512]{1,0:T(8,128)S(1)}, u32[]{:S(2)}, u32[]{:S(2)}) %collective-permute-start.2) | collective-permute-done | bytes 65568 | tf_op jit(solution)/shard_map/ppermute | solution.py:38
  49.3 0.0 collective-permute-done.1.come_ref
  49.3 0.7 update_parts.1
  50.0 14.9 %all_to_all.28.parts_ref = f32[8,64,128]{2,1,0:T(8,128)S(1)} all-to-all(f32[8,64,128]{2,1,0:T(8,128)S(1)} %update_parts.1), channel_id=1, replica_groups=mesh['y_lo'=2,'x'=4,'core'=2,'y_hi'=2,'z'=8] {'z'}, dimensions={0} | all-to-all | bytes 524288 | tf_op jit(solution)/shard_map/all_to_all | solution.py:21
  64.8 0.4 own_update.1
  65.2 0.1 collective-permute-start.3
  65.3 1.2 %collective-permute-done.3 = f32[32,128]{1,0:T(8,128)S(1)} collective-permute-done((f32[32,128]{1,0:T(8,128)S(1)}, f32[32,128]{1,0:T(8,128)S(1)}, u32[]{:S(2)}, u32[]{:S(2)}) %collective-permute-start.3) | collective-permute-done | bytes 16416 | tf_op jit(solution)/shard_map/ppermute | solution.py:38
  66.4 0.6 collective-permute-start.4
  67.0 3.2 %collective-permute-done.4 = f32[32,128]{1,0:T(8,128)S(1)} collective-permute-done((f32[32,128]{1,0:T(8,128)S(1)}, f32[32,128]{1,0:T(8,128)S(1)}, u32[]{:S(2)}, u32[]{:S(2)}) %collective-permute-start.4) | collective-permute-done | bytes 16416 | tf_op jit(solution)/shard_map/ppermute | solution.py:38
  70.2 11.8 %all_to_all.29.cross_ref = f32[16,32,128]{2,1,0:T(8,128)S(1)} all-to-all(f32[16,32,128]{2,1,0:T(8,128)S(1)} %broadcast_in_dim.8), channel_id=1, replica_groups=mesh['y_lo'=2,'x'=4,'core'=2,'y_hi'=2,'z'=8] {'y_hi','y_lo','x'}, dimensions={0} | all-to-all | bytes 524288 | tf_op jit(solution)/shard_map/all_to_all | solution.py:21
  82.0 2.6 %whitened.1 = f32[32,64]{1,0:T(8,128)} custom-call(f32[16,32,128]{2,1,0:T(8,128)S(1)} %all_to_all.29.cross_ref, f32[32,64]{1,0:T(8,128)S(1)} %get-tuple-element.20.update_ref), custom_call_target="tpu_custom_call" | custom-call | tf_op jit(solution)/shard_map/whitened/pallas_call | solution.py:291
  (8 shorter events, 0.1 us)
Async XLA Ops:
  3.6 1.3 %collective-permute-start = (f32[32,512]{1,0:T(8,128)S(1)}, f32[32,512]{1,0:T(8,128)S(1)}, u32[]{:S(2)}, u32[]{:S(2)}) collective-permute-start(f32[32,512]{1,0:T(8,128)S(1)} %get-tuple-element.15), channel_id=1, source_target_pairs={{0,16},{16,0},{1,17},{17,1},{2,18},{18,2},{3,19},{19,3},{4,20},{20... | collective-permute-start | bytes 196616 | tf_op jit(solution)/shard_map/ppermute | solution.py:38
  18.5 30.8 %collective-permute-start.1 = (f32[256,512]{1,0:T(8,128)S(1)}, f32[256,512]{1,0:T(8,128)S(1)}, u32[]{:S(2)}, u32[]{:S(2)}) collective-permute-start(f32[256,512]{1,0:T(8,128)S(1)} %get-tuple-element.17), channel_id=1, source_target_pairs={{0,8},{8,0},{1,9},{9,1},{2,10},{10,2},{3,11},{11,3},{4,12},{12,4},... | collective-permute-start | bytes 1572872 | tf_op jit(solution)/shard_map/ppermute | solution.py:38
  48.0 1.3 %collective-permute-start.2 = (f32[32,512]{1,0:T(8,128)S(1)}, f32[32,512]{1,0:T(8,128)S(1)}, u32[]{:S(2)}, u32[]{:S(2)}) collective-permute-start(f32[32,512]{1,0:T(8,128)S(1)} %bitcast.12), channel_id=1, source_target_pairs={{0,16},{16,0},{1,17},{17,1},{2,18},{18,2},{3,19},{19,3},{4,20},{20... | collective-permute-start | bytes 196616 | tf_op jit(solution)/shard_map/ppermute | solution.py:38
  65.2 1.2 %collective-permute-start.3 = (f32[32,128]{1,0:T(8,128)S(1)}, f32[32,128]{1,0:T(8,128)S(1)}, u32[]{:S(2)}, u32[]{:S(2)}) collective-permute-start(f32[32,128]{1,0:T(8,128)S(1)} %get-tuple-element.19), channel_id=1, source_target_pairs={{0,16},{16,0},{1,17},{17,1},{2,18},{18,2},{3,19},{19,3},{4,20},{20... | collective-permute-start | bytes 49160 | tf_op jit(solution)/shard_map/ppermute | solution.py:38
  66.4 3.7 %collective-permute-start.4 = (f32[32,128]{1,0:T(8,128)S(1)}, f32[32,128]{1,0:T(8,128)S(1)}, u32[]{:S(2)}, u32[]{:S(2)}) collective-permute-start(f32[32,128]{1,0:T(8,128)S(1)} %add.10), channel_id=1, source_target_pairs={{0,1},{1,0},{2,3},{3,2},{4,5},{5,4},{6,7},{7,6},{8,9},{9,8},{10,11... | collective-permute-start | bytes 49160 | tf_op jit(solution)/shard_map/ppermute | solution.py:38

commit v6 on v5

--- a/solution.py
+++ b/solution.py
@@ -11,6 +11,7 @@
 AXES = ("y_lo", "x", "core", "y_hi", "z")
 GX = ("y_lo", "x", "core")
 GY = ("y_hi", "z")
+PLANE = ("y_hi", "y_lo", "x", "core")
 CHIPS = ("y_hi", "y_lo", "x")
 HIGHEST = lax.Precision.HIGHEST
 EARLY = 6
@@ -38,16 +39,16 @@
     return lax.ppermute(array, axis, [(i, i ^ 1) for i in range(lax.axis_size(axis))])
 
 
-def summed_everywhere(own, other, sent):
-    rows, cols = own.shape
-    own = own + from_partner(other, "core")
-    tiles = tiles_of(own).reshape(lax.axis_size(CHIPS), -1, 128)
-    tile = jnp.sum(exchanged(tiles, CHIPS), axis=0)
-    tile, sent = lax.optimization_barrier((tile, sent))
+def summed_everywhere(matrix, sent):
+    rows, cols = matrix.shape
+    chips, cores = lax.axis_size(CHIPS), lax.axis_size("core")
+    tiles = tiles_of(matrix).reshape(chips, 1, -1, 128)
+    tiles = jnp.broadcast_to(tiles, (chips, cores, *tiles.shape[2:]))
+    own = jnp.sum(exchanged(tiles.reshape(chips * cores, -1, 128), PLANE), axis=0)
+    own, sent = lax.optimization_barrier((own, sent))
     come = from_partner(sent, "y_hi")
-    tile = jnp.sum(of_everyone(tile, "z"), axis=0)
-    own = from_tiles(of_everyone(tile, CHIPS).reshape(-1, 8, 128), rows, cols)
-    return own, from_partner(own, "core"), come
+    own = jnp.sum(of_everyone(own, "z"), axis=0)
+    return from_tiles(of_everyone(own, CHIPS).reshape(-1, 8, 128), rows, cols), come
 
 
 def with_neighbour(value, axis):
@@ -68,8 +69,7 @@
     x_ref,
     kept_ref,
     sent_ref,
-    own_ref,
-    other_ref,
+    folded_ref,
     planes,
     y_here,
     x_here,
@@ -90,7 +90,6 @@
     x_copy.start()
     kept_at = pl.multiple_of(lax.axis_index("y_hi") * half, half)
     sides = ((kept_ref, kept_at), (sent_ref, pl.multiple_of(half - kept_at, half)))
-    first = lax.axis_index("core") == 0
     y_copy.wait()
     y_t = y_here[...]
     none = jnp.zeros_like(y_t)
@@ -125,10 +124,7 @@
                     term = jnp.dot(x_part, part, preferred_element_type=jnp.float32)
                     folded = term if folded is None else folded + term
         if step > 0:
-            lanes = pl.ds(2 * rank * (step - 1), 2 * rank)
-            upper, lower = folded[: rank // 2], folded[rank // 2 :]
-            own_ref[:, lanes] = jnp.where(first, upper, lower)
-            other_ref[:, lanes] = jnp.where(first, lower, upper)
+            folded_ref[:, pl.ds(2 * rank * (step - 1), 2 * rank)] = folded
 
 
 def projected(tensor, y_factor, x_factor):
@@ -139,10 +135,10 @@
         project_kernel,
         out_shape=[
             jax.ShapeDtypeStruct((n, rows), jnp.float32)
-            for n in (width_x // 2, width_x // 2, rank // 2, rank // 2)
+            for n in (width_x // 2, width_x // 2, rank)
         ],
         in_specs=[pl.BlockSpec(memory_space=pltpu.HBM)] * 3,
-        out_specs=[ON_CHIP] * 4,
+        out_specs=[ON_CHIP] * 3,
         scratch_shapes=[
             pltpu.VMEM(tensor.shape, tensor.dtype),
             pltpu.VMEM((rank, width_y), y_factor.dtype),
@@ -154,16 +150,13 @@
     )(*(pltpu.with_memory_space_constraint(a, pltpu.HBM) for a in (tensor, y_factor.T, x_factor)))
 
 
-def update_kernel(kept_ref, come_ref, own_ref, other_ref, out_ref):
+def update_kernel(kept_ref, come_ref, folded_ref, out_ref):
     n, rows, lanes = out_ref.shape
     rank = lanes // 2
     half = 2 * rows // n
-    first = lax.axis_index("core") == 0
-    own, other = own_ref[...], other_ref[...]
-    folded = jnp.concatenate([jnp.where(first, own, other), jnp.where(first, other, own)], axis=0)
     part = lax.dot_general(
         kept_ref[...] + come_ref[...],
-        folded,
+        folded_ref[...],
         (((1,), (1,)), ((), ())),
         precision=HIGHEST,
         preferred_element_type=jnp.float32,
@@ -175,17 +168,17 @@
         out_ref[z] = packed[:, z % 2].reshape(rows, lanes)
 
 
-def update_parts(kept, come, own, other, n):
+def update_parts(kept, come, folded, n):
     width_x = kept.shape[0]
-    rank = 2 * own.shape[0]
+    rank = folded.shape[0]
     return pl.pallas_call(
         update_kernel,
         out_shape=jax.ShapeDtypeStruct((n, width_x // 4, 2 * rank), jnp.float32),
-        in_specs=[ON_CHIP] * 4,
+        in_specs=[ON_CHIP] * 3,
         out_specs=ON_CHIP,
         compiler_params=pltpu.CompilerParams(vmem_limit_bytes=24 * 2**20),
         name="update_parts",
-    )(kept, come, own, other)
+    )(kept, come, folded)
 
 
 def cross_kernel(parts_ref, update_ref, cross_ref, packed_ref):
@@ -222,11 +215,6 @@
         compiler_params=pltpu.CompilerParams(vmem_limit_bytes=8 * 2**20),
         name="own_update",
     )(parts)
-
-
-def inverse_root(pivot):
-    guess = lax.rsqrt(pivot)
-    return guess * (1.5 - 0.5 * pivot * guess * guess)
 
 
 def whitened_kernel(scale, cross_ref, update_ref, out_ref, aug, lanes):
@@ -262,7 +250,7 @@
             jnp.broadcast_to(aug[8 * j + k : 8 * j + k + 1, :], (8, 128)) for k in range(8)
         ]
         for k in range(8):
-            root = inverse_root(a[k][k])
+            root = lax.rsqrt(a[k][k])
             for m in range(k + 1, 8):
                 a[m][k] = a[m][k] * root
             right[k] = right[k] * root
@@ -301,9 +289,9 @@
 
 def per_device(tensor, y_factor, x_factor):
     width_x = x_factor.shape[1]
-    kept, sent, own, other = projected(tensor, y_factor, x_factor)
-    own, other, come = summed_everywhere(own, other, sent)
-    parts = update_parts(kept, come, own, other, lax.axis_size("z"))
+    kept, sent, folded_part = projected(tensor, y_factor, x_factor)
+    folded, come = summed_everywhere(folded_part, sent)
+    parts = update_parts(kept, come, folded, lax.axis_size("z"))
     update_t, wide = own_update(exchanged(parts, "z"))
     wide = with_neighbour(with_neighbour(wide, "core"), "z")
     total_x = width_x * lax.axis_size(GX)

time: 84.8 us -> 82.1 us (0.968)
  waiting for transfers between devices: 6.83 us -> 4.34 us
    ppermute x5 -> x3, waiting for transfers between devices: 6.83 us -> 4.34 us  [from_partner(): lax.ppermute(array, axis, [(i, i ^ 1) for i in range(lax.axis_size(axis))])]
    ppermute x5 -> x3, starting transfers between devices: 1.98 us -> 2.07 us  [from_partner(): lax.ppermute(array, axis, [(i, i ^ 1) for i in range(lax.axis_size(axis))])]
  transfers between devices with their start and end apart: 5 -> 3, of which waited for: 4 -> 2; matrix products, arithmetic and copies ran while one was open for 0% -> 0% of each run, Pallas kernels for 0% -> 0%
where the time goes in v6:
time: 82.1 us; the launch traced here: 81.8 us
  blocking collectives  68.3 us (83%)
  Pallas kernels  6.88 us (8%)
  waiting for transfers between devices  4.34 us (5%)
  starting transfers between devices  2.07 us (3%)
    all_to_all x5, blocking collectives, exchanged(): return lax.all_to_all(tiles, axis, 0, 0, tiled=True)  68.3 us
    ppermute x3, waiting for transfers between devices, from_partner(): lax.ppermute(array, axis, [(i, i ^ 1) for i in range(lax.axis_size(axis))])  4.34 us
    pallas_call x1, Pallas kernels, projected(): pl.pallas_call(project_kernel, out_shape=[jax.ShapeDtypeStruct((n, rows),...  3.57 us
    pallas_call x1, Pallas kernels, whitened(): pl.pallas_call(functools.partial(whitened_kernel, scale), out_shape=jax.S...  2.3 us
    ppermute x3, starting transfers between devices, from_partner(): lax.ppermute(array, axis, [(i, i ^ 1) for i in range(lax.axis_size(axis))])  2.07 us
  transfers between devices with their start and end apart: 3, of which 2 were waited for; matrix products, arithmetic and copies ran while one was open for 0% of the time, Pallas kernels for 0%

profile of v6, /device:TPU:2, one launch (start us, length us, event | category | flops | bytes accessed | tf_op | source)
XLA Modules:
  0.0 81.8 jit_solution(12864626633477612134)
XLA Ops:
  0.0 3.6 %projected.1 = (f32[256,512]{1,0:T(8,128)S(1)}, f32[256,512]{1,0:T(8,128)S(1)}, f32[64,512]{1,0:T(8,128)S(1)}) custom-call(bf16[8,512,512]{2,1,0:T(8,128)(2,1)} %tensor_ref.1, bf16[64,512]{1,0:T(8,128)(2,1)} %bitcast.16, bf16[64,512]{1,0:T(8,128)(2,1)} %x_ref.1), custom_call_target="tpu_custom_call" | custom-call | tf_op jit(solution)/shard_map/projected/pallas_call | solution.py:134
  3.6 15.0 %all_to_all.25 = f32[32,16,128]{2,1,0:T(8,128)S(1)} all-to-all(f32[32,16,128]{2,1,0:T(8,128)S(1)} %bitcast.15), channel_id=1, replica_groups=mesh['y_lo'=2,'x'=4,'core'=2,'y_hi'=2,'z'=8] {'y_hi','y_lo','x','core'}, dimensions={0} | all-to-all | bytes 524288 | tf_op jit(solution)/shard_map/all_to_all | solution.py:22
  18.6 1.5 %collective-permute-start = (f32[256,512]{1,0:T(8,128)S(1)}, f32[256,512]{1,0:T(8,128)S(1)}, u32[]{:S(2)}, u32[]{:S(2)}) collective-permute-start(f32[256,512]{1,0:T(8,128)S(1)} %get-tuple-element.15), channel_id=1, source_target_pairs={{0,8},{8,0},{1,9},{9,1},{2,10},{10,2},{3,11},{11,3},{4,12},{12,4},... | collective-permute-start | bytes 1572872 | tf_op jit(solution)/shard_map/ppermute | solution.py:39
  20.1 16.6 %all_to_all.26 = f32[8,16,128]{2,1,0:T(8,128)S(1)} all-to-all(f32[8,16,128]{2,1,0:T(8,128)S(1)} %broadcast_in_dim.12), channel_id=1, replica_groups=mesh['y_lo'=2,'x'=4,'core'=2,'y_hi'=2,'z'=8] {'z'}, dimensions={0} | all-to-all | bytes 131072 | tf_op jit(solution)/shard_map/all_to_all | solution.py:22
  36.8 12.1 %all_to_all.27 = f32[16,16,128]{2,1,0:T(8,128)S(1)} all-to-all(f32[16,16,128]{2,1,0:T(8,128)S(1)} %broadcast_in_dim.13), channel_id=1, replica_groups=mesh['y_lo'=2,'x'=4,'core'=2,'y_hi'=2,'z'=8] {'y_hi','y_lo','x'}, dimensions={0} | all-to-all | bytes 262144 | tf_op jit(solution)/shard_map/all_to_all | solution.py:22
  48.8 0.0 collective-permute-done.come_ref
  48.8 0.7 update_parts.1
  49.5 12.9 %all_to_all.28.parts_ref = f32[8,64,128]{2,1,0:T(8,128)S(1)} all-to-all(f32[8,64,128]{2,1,0:T(8,128)S(1)} %update_parts.1), channel_id=1, replica_groups=mesh['y_lo'=2,'x'=4,'core'=2,'y_hi'=2,'z'=8] {'z'}, dimensions={0} | all-to-all | bytes 524288 | tf_op jit(solution)/shard_map/all_to_all | solution.py:22
  62.4 0.4 own_update.1
  62.7 0.0 collective-permute-start.1
  62.8 1.2 %collective-permute-done.1 = f32[32,128]{1,0:T(8,128)S(1)} collective-permute-done((f32[32,128]{1,0:T(8,128)S(1)}, f32[32,128]{1,0:T(8,128)S(1)}, u32[]{:S(2)}, u32[]{:S(2)}) %collective-permute-start.1) | collective-permute-done | bytes 16416 | tf_op jit(solution)/shard_map/ppermute | solution.py:39
  63.9 0.6 collective-permute-start.2
  64.5 3.2 %collective-permute-done.2 = f32[32,128]{1,0:T(8,128)S(1)} collective-permute-done((f32[32,128]{1,0:T(8,128)S(1)}, f32[32,128]{1,0:T(8,128)S(1)}, u32[]{:S(2)}, u32[]{:S(2)}) %collective-permute-start.2) | collective-permute-done | bytes 16416 | tf_op jit(solution)/shard_map/ppermute | solution.py:39
  67.7 11.8 %all_to_all.29.cross_ref = f32[16,32,128]{2,1,0:T(8,128)S(1)} all-to-all(f32[16,32,128]{2,1,0:T(8,128)S(1)} %broadcast_in_dim.14), channel_id=1, replica_groups=mesh['y_lo'=2,'x'=4,'core'=2,'y_hi'=2,'z'=8] {'y_hi','y_lo','x'}, dimensions={0} | all-to-all | bytes 524288 | tf_op jit(solution)/shard_map/all_to_all | solution.py:22
  79.5 2.3 %whitened.1 = f32[32,64]{1,0:T(8,128)} custom-call(f32[16,32,128]{2,1,0:T(8,128)S(1)} %all_to_all.29.cross_ref, f32[32,64]{1,0:T(8,128)S(1)} %get-tuple-element.18.update_ref), custom_call_target="tpu_custom_call" | custom-call | tf_op jit(solution)/shard_map/whitened/pallas_call | solution.py:279
  (8 shorter events, 0.1 us)
Async XLA Ops:
  18.6 30.2 %collective-permute-start = (f32[256,512]{1,0:T(8,128)S(1)}, f32[256,512]{1,0:T(8,128)S(1)}, u32[]{:S(2)}, u32[]{:S(2)}) collective-permute-start(f32[256,512]{1,0:T(8,128)S(1)} %get-tuple-element.15), channel_id=1, source_target_pairs={{0,8},{8,0},{1,9},{9,1},{2,10},{10,2},{3,11},{11,3},{4,12},{12,4},... | collective-permute-start | bytes 1572872 | tf_op jit(solution)/shard_map/ppermute | solution.py:39
  62.7 1.2 %collective-permute-start.1 = (f32[32,128]{1,0:T(8,128)S(1)}, f32[32,128]{1,0:T(8,128)S(1)}, u32[]{:S(2)}, u32[]{:S(2)}) collective-permute-start(f32[32,128]{1,0:T(8,128)S(1)} %get-tuple-element.17), channel_id=1, source_target_pairs={{0,16},{16,0},{1,17},{17,1},{2,18},{18,2},{3,19},{19,3},{4,20},{20... | collective-permute-start | bytes 49160 | tf_op jit(solution)/shard_map/ppermute | solution.py:39
  63.9 3.7 %collective-permute-start.2 = (f32[32,128]{1,0:T(8,128)S(1)}, f32[32,128]{1,0:T(8,128)S(1)}, u32[]{:S(2)}, u32[]{:S(2)}) collective-permute-start(f32[32,128]{1,0:T(8,128)S(1)} %add.6), channel_id=1, source_target_pairs={{0,1},{1,0},{2,3},{3,2},{4,5},{5,4},{6,7},{7,6},{8,9},{9,8},{10,11... | collective-permute-start | bytes 49160 | tf_op jit(solution)/shard_map/ppermute | solution.py:39

commit v7 on v6

--- a/solution.py
+++ b/solution.py
@@ -8,13 +8,15 @@
 from jax.sharding import Mesh
 from jax.sharding import PartitionSpec as P
 
+
 AXES = ("y_lo", "x", "core", "y_hi", "z")
 GX = ("y_lo", "x", "core")
 GY = ("y_hi", "z")
-PLANE = ("y_hi", "y_lo", "x", "core")
+Y = ("y_lo", "y_hi")
 CHIPS = ("y_hi", "y_lo", "x")
 HIGHEST = lax.Precision.HIGHEST
 EARLY = 6
+CLASSES = 4
 ON_CHIP = pl.BlockSpec(memory_space=pltpu.VMEM)
 
 
@@ -39,20 +41,33 @@
     return lax.ppermute(array, axis, [(i, i ^ 1) for i in range(lax.axis_size(axis))])
 
 
+def with_neighbour(value, axis):
+    return value + from_partner(value, axis)
+
+
+def ring_terms(value, axis):
+    n = lax.axis_size(axis)
+    at = [0, 2, 1, 3] if axis == Y else list(range(n))
+
+    def shifted(by):
+        return lax.ppermute(value, axis, [(at[i], at[(i + by) % n]) for i in range(n)])
+
+    right, left, far = shifted(n - 1), shifted(1), shifted(2)
+    return value, far, left, right
+
+
+def with_ring(value, axis):
+    own, far, left, right = ring_terms(value, axis)
+    return (own + far) + (left + right)
+
+
 def summed_everywhere(matrix, sent):
     rows, cols = matrix.shape
-    chips, cores = lax.axis_size(CHIPS), lax.axis_size("core")
-    tiles = tiles_of(matrix).reshape(chips, 1, -1, 128)
-    tiles = jnp.broadcast_to(tiles, (chips, cores, *tiles.shape[2:]))
-    own = jnp.sum(exchanged(tiles.reshape(chips * cores, -1, 128), PLANE), axis=0)
-    own, sent = lax.optimization_barrier((own, sent))
+    tiles = tiles_of(with_neighbour(matrix, "core")).reshape(lax.axis_size(CHIPS), -1, 128)
+    own = jnp.sum(exchanged(tiles, CHIPS), axis=0)
     come = from_partner(sent, "y_hi")
     own = jnp.sum(of_everyone(own, "z"), axis=0)
     return from_tiles(of_everyone(own, CHIPS).reshape(-1, 8, 128), rows, cols), come
-
-
-def with_neighbour(value, axis):
-    return value + from_partner(value, axis)
 
 
 def rounded_parts(matrix):
@@ -153,7 +168,7 @@
 def update_kernel(kept_ref, come_ref, folded_ref, out_ref):
     n, rows, lanes = out_ref.shape
     rank = lanes // 2
-    half = 2 * rows // n
+    half = kept_ref.shape[0] // n // 2
     part = lax.dot_general(
         kept_ref[...] + come_ref[...],
         folded_ref[...],
@@ -163,9 +178,10 @@
     )
     part = part.reshape(n, 2, half, rank)
     packed = jnp.concatenate([part[:, 0], part[:, 1]], axis=2)
-    packed = packed.reshape(n // 2, 2, half, lanes)
+    classes = n * half // rows
+    packed = packed.reshape(n // classes, classes, half, lanes)
     for z in range(n):
-        out_ref[z] = packed[:, z % 2].reshape(rows, lanes)
+        out_ref[z] = packed[:, z % classes].reshape(rows, lanes)
 
 
 def update_parts(kept, come, folded, n):
@@ -173,7 +189,7 @@
     rank = folded.shape[0]
     return pl.pallas_call(
         update_kernel,
-        out_shape=jax.ShapeDtypeStruct((n, width_x // 4, 2 * rank), jnp.float32),
+        out_shape=jax.ShapeDtypeStruct((n, width_x // CLASSES // 2, 2 * rank), jnp.float32),
         in_specs=[ON_CHIP] * 3,
         out_specs=ON_CHIP,
         compiler_params=pltpu.CompilerParams(vmem_limit_bytes=24 * 2**20),
@@ -195,7 +211,7 @@
         preferred_element_type=jnp.float32,
     )
     cross_ref[...] = jnp.concatenate([square[: rank // 2], square[rank // 2 :]], axis=1)
-    start = pl.multiple_of(lax.axis_index("z") // 2 * half, half)
+    start = pl.multiple_of(lax.axis_index("z") // CLASSES * half, half)
     own = packed_ref[pl.ds(start, half), :]
     update_ref[...] = jnp.concatenate([own[:, :rank], own[:, rank:]], axis=0)
 
@@ -206,7 +222,7 @@
     return pl.pallas_call(
         cross_kernel,
         out_shape=(
-            jax.ShapeDtypeStruct((4 * rows // n, rank), jnp.float32),
+            jax.ShapeDtypeStruct((2 * rows * CLASSES // n, rank), jnp.float32),
             jax.ShapeDtypeStruct((rank // 2, 2 * rank), jnp.float32),
         ),
         in_specs=[ON_CHIP],
@@ -217,13 +233,11 @@
     )(parts)
 
 
-def whitened_kernel(scale, cross_ref, update_ref, out_ref, aug, lanes):
+def whitened_kernel(scale, own_ref, far_ref, left_ref, right_ref, update_ref, out_ref, aug, lanes):
     rank = update_ref.shape[1]
     cols = update_ref.shape[0]
     blocks = rank // 8
-    wide = cross_ref[0]
-    for i in range(1, cross_ref.shape[0]):
-        wide = wide + cross_ref[i]
+    wide = (own_ref[...] + far_ref[...]) + (left_ref[...] + right_ref[...])
     gram = jnp.concatenate([wide[:, :rank], wide[:, rank:]], axis=0)
     padded = jnp.concatenate(
         [update_ref[...], jnp.zeros((rank - cols, rank), jnp.float32)], axis=0
@@ -279,23 +293,23 @@
     return pl.pallas_call(
         functools.partial(whitened_kernel, scale),
         out_shape=jax.ShapeDtypeStruct((cols, rank), jnp.float32),
-        in_specs=[ON_CHIP, ON_CHIP],
+        in_specs=[ON_CHIP] * 5,
         out_specs=ON_CHIP,
         scratch_shapes=[pltpu.VMEM((rank, 2 * rank), jnp.float32)] * 2,
         compiler_params=pltpu.CompilerParams(vmem_limit_bytes=8 * 2**20),
         name="whitened",
-    )(terms, update_t)
-
-
-def per_device(tensor, y_factor, x_factor):
+    )(*terms, update_t)
+
+
+def new_basis(tensor, y_factor, x_factor):
     width_x = x_factor.shape[1]
     kept, sent, folded_part = projected(tensor, y_factor, x_factor)
     folded, come = summed_everywhere(folded_part, sent)
     parts = update_parts(kept, come, folded, lax.axis_size("z"))
     update_t, wide = own_update(exchanged(parts, "z"))
-    wide = with_neighbour(with_neighbour(wide, "core"), "z")
+    wide = with_ring(with_ring(with_neighbour(wide, "core"), "z"), "x")
     total_x = width_x * lax.axis_size(GX)
-    return whitened(of_everyone(wide, CHIPS), update_t, float(total_x) ** 0.5).T
+    return whitened(ring_terms(wide, Y), update_t, float(total_x) ** 0.5).T
 
 
 def solution(mesh):
@@ -303,5 +317,5 @@
     in_specs = (P(None, GX, GY), P(GY, None), P(None, GX))
     out_specs = P(None, AXES)
     return jax.shard_map(
-        per_device, mesh=finer, in_specs=in_specs, out_specs=out_specs, check_vma=False
+        new_basis, mesh=finer, in_specs=in_specs, out_specs=out_specs, check_vma=False
     )

time: 82.1 us -> 90.1 us (1.097)
  blocking collectives: 68.3 us -> 54.1 us
  starting transfers between devices: 2.07 us -> 13.3 us
  waiting for transfers between devices: 4.34 us -> 15.1 us
    all_to_all x5 -> x4, blocking collectives: 68.3 us -> 54.1 us  [exchanged(): return lax.all_to_all(tiles, axis, 0, 0, tiled=True)]
    ppermute x0 -> x9, waiting for transfers between devices: none -> 12.6 us  [shifted(): lax.ppermute(value, axis, [(at[i], at[(i + by) % n]) for i in range(n)])]
    ppermute x0 -> x9, starting transfers between devices: none -> 9.98 us  [shifted(): lax.ppermute(value, axis, [(at[i], at[(i + by) % n]) for i in range(n)])]
    ppermute x3, waiting for transfers between devices: 4.34 us -> 2.52 us  [from_partner(): lax.ppermute(array, axis, [(i, i ^ 1) for i in range(lax.axis_size(axis))])]
    ppermute x3, starting transfers between devices: 2.07 us -> 3.33 us  [from_partner(): lax.ppermute(array, axis, [(i, i ^ 1) for i in range(lax.axis_size(axis))])]
  transfers between devices with their start and end apart: 3 -> 12, of which waited for: 2 -> 10; matrix products, arithmetic and copies ran while one was open for 0% -> 0% of each run, Pallas kernels for 0% -> 0%
where the time goes in v7:
time: 90.1 us; the launch traced here: 89.6 us
  blocking collectives  54.1 us (60%)
  waiting for transfers between devices  15.1 us (17%)
  starting transfers between devices  13.3 us (15%)
  Pallas kernels  6.88 us (8%)
    all_to_all x4, blocking collectives, exchanged(): return lax.all_to_all(tiles, axis, 0, 0, tiled=True)  54.1 us
    ppermute x9, waiting for transfers between devices, shifted(): lax.ppermute(value, axis, [(at[i], at[(i + by) % n]) for i in range(n)])  12.6 us
    ppermute x9, starting transfers between devices, shifted(): lax.ppermute(value, axis, [(at[i], at[(i + by) % n]) for i in range(n)])  9.98 us
    pallas_call x1, Pallas kernels, projected(): pl.pallas_call(project_kernel, out_shape=[jax.ShapeDtypeStruct((n, rows),...  3.57 us
    ppermute x3, starting transfers between devices, from_partner(): lax.ppermute(array, axis, [(i, i ^ 1) for i in range(lax.axis_size(axis))])  3.33 us
    ppermute x3, waiting for transfers between devices, from_partner(): lax.ppermute(array, axis, [(i, i ^ 1) for i in range(lax.axis_size(axis))])  2.52 us
    pallas_call x1, Pallas kernels, whitened(): pl.pallas_call(functools.partial(whitened_kernel, scale), out_shape=jax.S...  2.3 us
  transfers between devices with their start and end apart: 12, of which 10 were waited for; matrix products, arithmetic and copies ran while one was open for 0% of the time, Pallas kernels for 0%

profile of v7, /device:TPU:2, one launch (start us, length us, event | category | flops | bytes accessed | tf_op | source)
XLA Modules:
  0.0 89.6 jit_solution(886190304485524551)
XLA Ops:
  0.0 3.6 %projected.1 = (f32[256,512]{1,0:T(8,128)S(1)}, f32[256,512]{1,0:T(8,128)S(1)}, f32[64,512]{1,0:T(8,128)S(1)}) custom-call(bf16[8,512,512]{2,1,0:T(8,128)(2,1)} %tensor_ref.1, bf16[64,512]{1,0:T(8,128)(2,1)} %bitcast.14, bf16[64,512]{1,0:T(8,128)(2,1)} %x_ref.1), custom_call_target="tpu_custom_call" | custom-call | tf_op jit(solution)/shard_map/projected/pallas_call | solution.py:149
  3.6 3.3 %collective-permute-start = (f32[256,512]{1,0:T(8,128)S(1)}, f32[256,512]{1,0:T(8,128)S(1)}, u32[]{:S(2)}, u32[]{:S(2)}) collective-permute-start(f32[256,512]{1,0:T(8,128)S(1)} %get-tuple-element.11), channel_id=1, source_target_pairs={{0,8},{8,0},{1,9},{9,1},{2,10},{10,2},{3,11},{11,3},{4,12},{12,4},... | collective-permute-start | bytes 1572872 | tf_op jit(solution)/shard_map/ppermute | solution.py:41
  6.9 0.0 collective-permute-start.1
  6.9 1.3 %collective-permute-done.1 = f32[64,512]{1,0:T(8,128)S(1)} collective-permute-done((f32[64,512]{1,0:T(8,128)S(1)}, f32[64,512]{1,0:T(8,128)S(1)}, u32[]{:S(2)}, u32[]{:S(2)}) %collective-permute-start.1) | collective-permute-done | bytes 131104 | tf_op jit(solution)/shard_map/ppermute | solution.py:41
  8.2 12.5 %all_to_all.20 = f32[16,16,128]{2,1,0:T(8,128)S(1)} all-to-all(f32[16,16,128]{2,1,0:T(8,128)S(1)} %bitcast.13), channel_id=1, replica_groups=mesh['y_lo'=2,'x'=4,'core'=2,'y_hi'=2,'z'=8] {'y_hi','y_lo','x'}, dimensions={0} | all-to-all | bytes 262144 | tf_op jit(solution)/shard_map/all_to_all | solution.py:24
  20.7 16.6 %all_to_all.21 = f32[8,16,128]{2,1,0:T(8,128)S(1)} all-to-all(f32[8,16,128]{2,1,0:T(8,128)S(1)} %broadcast_in_dim.4), channel_id=1, replica_groups=mesh['y_lo'=2,'x'=4,'core'=2,'y_hi'=2,'z'=8] {'z'}, dimensions={0} | all-to-all | bytes 131072 | tf_op jit(solution)/shard_map/all_to_all | solution.py:24
  37.4 13.6 %all_to_all.22 = f32[16,16,128]{2,1,0:T(8,128)S(1)} all-to-all(f32[16,16,128]{2,1,0:T(8,128)S(1)} %broadcast_in_dim.5), channel_id=1, replica_groups=mesh['y_lo'=2,'x'=4,'core'=2,'y_hi'=2,'z'=8] {'y_hi','y_lo','x'}, dimensions={0} | all-to-all | bytes 262144 | tf_op jit(solution)/shard_map/all_to_all | solution.py:24
  51.0 0.0 collective-permute-done.come_ref
  51.0 0.7 update_parts.1
  51.6 11.5 %all_to_all.23.parts_ref = f32[8,32,128]{2,1,0:T(8,128)S(1)} all-to-all(f32[8,32,128]{2,1,0:T(8,128)S(1)} %update_parts.1), channel_id=1, replica_groups=mesh['y_lo'=2,'x'=4,'core'=2,'y_hi'=2,'z'=8] {'z'}, dimensions={0} | all-to-all | bytes 262144 | tf_op jit(solution)/shard_map/all_to_all | solution.py:24
  63.1 0.4 own_update.1
  63.5 0.0 collective-permute-start.2
  63.5 1.2 %collective-permute-done.2 = f32[32,128]{1,0:T(8,128)S(1)} collective-permute-done((f32[32,128]{1,0:T(8,128)S(1)}, f32[32,128]{1,0:T(8,128)S(1)}, u32[]{:S(2)}, u32[]{:S(2)}) %collective-permute-start.2) | collective-permute-done | bytes 16416 | tf_op jit(solution)/shard_map/ppermute | solution.py:41
  64.7 0.0 collective-permute-start.5
  64.7 2.0 %collective-permute-start.4 = (f32[32,128]{1,0:T(8,128)S(1)}, f32[32,128]{1,0:T(8,128)S(1)}, u32[]{:S(2)}, u32[]{:S(2)}) collective-permute-start(f32[32,128]{1,0:T(8,128)S(1)} %add.25), channel_id=1, source_target_pairs={{0,1},{1,2},{2,3},{3,4},{4,5},{5,6},{6,7},{7,0},{8,9},{9,10},{10,1... | collective-permute-start | bytes 49160 | tf_op jit(solution)/shard_map/ppermute | solution.py:53
  66.7 0.4 collective-permute-start.3
  67.1 1.3 %collective-permute-done.5 = f32[32,128]{1,0:T(8,128)S(1)} collective-permute-done((f32[32,128]{1,0:T(8,128)S(1)}, f32[32,128]{1,0:T(8,128)S(1)}, u32[]{:S(2)}, u32[]{:S(2)}) %collective-permute-start.5) | collective-permute-done | bytes 16416 | tf_op jit(solution)/shard_map/ppermute | solution.py:53
  68.4 1.3 %collective-permute-done.4 = f32[32,128]{1,0:T(8,128)S(1)} collective-permute-done((f32[32,128]{1,0:T(8,128)S(1)}, f32[32,128]{1,0:T(8,128)S(1)}, u32[]{:S(2)}, u32[]{:S(2)}) %collective-permute-start.4) | collective-permute-done | bytes 16416 | tf_op jit(solution)/shard_map/ppermute | solution.py:53
  69.7 2.8 %collective-permute-done.3 = f32[32,128]{1,0:T(8,128)S(1)} collective-permute-done((f32[32,128]{1,0:T(8,128)S(1)}, f32[32,128]{1,0:T(8,128)S(1)}, u32[]{:S(2)}, u32[]{:S(2)}) %collective-permute-start.3) | collective-permute-done | bytes 16416 | tf_op jit(solution)/shard_map/ppermute | solution.py:53
  72.6 1.5 %collective-permute-start.8 = (f32[32,128]{1,0:T(8,128)S(1)}, f32[32,128]{1,0:T(8,128)S(1)}, u32[]{:S(2)}, u32[]{:S(2)}) collective-permute-start(f32[32,128]{1,0:T(8,128)S(1)} %add_add_fusion.1), channel_id=1, source_target_pairs={{0,96},{32,0},{64,32},{96,64},{1,97},{33,1},{65,33},{97,65},{2,98}... | collective-permute-start | bytes 49160 | tf_op jit(solution)/shard_map/ppermute | solution.py:53
  74.1 0.6 collective-permute-start.7
  74.7 2.4 %collective-permute-start.6 = (f32[32,128]{1,0:T(8,128)S(1)}, f32[32,128]{1,0:T(8,128)S(1)}, u32[]{:S(2)}, u32[]{:S(2)}) collective-permute-start(f32[32,128]{1,0:T(8,128)S(1)} %add_add_fusion.1), channel_id=1, source_target_pairs={{0,64},{32,96},{64,0},{96,32},{1,65},{33,97},{65,1},{97,33},{2,66}... | collective-permute-start | bytes 49160 | tf_op jit(solution)/shard_map/ppermute | solution.py:53
  77.1 0.0 collective-permute-done.8
  77.1 0.7 collective-permute-done.7
  77.8 2.1 %collective-permute-done.6 = f32[32,128]{1,0:T(8,128)S(1)} collective-permute-done((f32[32,128]{1,0:T(8,128)S(1)}, f32[32,128]{1,0:T(8,128)S(1)}, u32[]{:S(2)}, u32[]{:S(2)}) %collective-permute-start.6) | collective-permute-done | bytes 16416 | tf_op jit(solution)/shard_map/ppermute | solution.py:53
  79.9 0.9 %collective-permute-start.11 = (f32[32,128]{1,0:T(8,128)S(1)}, f32[32,128]{1,0:T(8,128)S(1)}, u32[]{:S(2)}, u32[]{:S(2)}) collective-permute-start(f32[32,128]{1,0:T(8,128)S(1)} %add_add_fusion.own_ref), channel_id=1, source_target_pairs={{0,136},{128,0},{8,128},{136,8},{1,137},{129,1},{9,129},{137,9},{2... | collective-permute-start | bytes 49160 | tf_op jit(solution)/shard_map/ppermute | solution.py:53
  80.8 1.2 %collective-permute-start.10 = (f32[32,128]{1,0:T(8,128)S(1)}, f32[32,128]{1,0:T(8,128)S(1)}, u32[]{:S(2)}, u32[]{:S(2)}) collective-permute-start(f32[32,128]{1,0:T(8,128)S(1)} %add_add_fusion.own_ref), channel_id=1, source_target_pairs={{0,128},{128,8},{8,136},{136,0},{1,129},{129,9},{9,137},{137,1},{2... | collective-permute-start | bytes 49160 | tf_op jit(solution)/shard_map/ppermute | solution.py:53
  82.0 0.9 %collective-permute-start.9 = (f32[32,128]{1,0:T(8,128)S(1)}, f32[32,128]{1,0:T(8,128)S(1)}, u32[]{:S(2)}, u32[]{:S(2)}) collective-permute-start(f32[32,128]{1,0:T(8,128)S(1)} %add_add_fusion.own_ref), channel_id=1, source_target_pairs={{0,8},{128,136},{8,0},{136,128},{1,9},{129,137},{9,1},{137,129},{2... | collective-permute-start | bytes 49160 | tf_op jit(solution)/shard_map/ppermute | solution.py:53
  83.0 0.8 collective-permute-done.11.right_ref
  83.7 2.1 %collective-permute-done.10.left_ref = f32[32,128]{1,0:T(8,128)S(1)} collective-permute-done((f32[32,128]{1,0:T(8,128)S(1)}, f32[32,128]{1,0:T(8,128)S(1)}, u32[]{:S(2)}, u32[]{:S(2)}) %collective-permute-start.10) | collective-permute-done | bytes 16416 | tf_op jit(solution)/shard_map/ppermute | solution.py:53
  85.8 1.5 %collective-permute-done.9.far_ref = f32[32,128]{1,0:T(8,128)S(1)} collective-permute-done((f32[32,128]{1,0:T(8,128)S(1)}, f32[32,128]{1,0:T(8,128)S(1)}, u32[]{:S(2)}, u32[]{:S(2)}) %collective-permute-start.9) | collective-permute-done | bytes 16416 | tf_op jit(solution)/shard_map/ppermute | solution.py:53
  87.3 2.3 %whitened.1 = f32[32,64]{1,0:T(8,128)} custom-call(f32[32,128]{1,0:T(8,128)S(1)} %add_add_fusion.own_ref, f32[32,128]{1,0:T(8,128)S(1)} %collective-permute-done.9.far_ref, f32[32,128]{1,0:T(8,128)S(1)} %collective-permute-done.10.left_ref, f32[32,128]{1,0:T(8,128)S(1)} %collective-permute-done.11.right_ref, f32[32,64]{1,0:T(8,128)S(1)} %get-tuple-element.14.update_ref), custom_call_target="tpu_custom_call" | custom-call | tf_op jit(solution)/shard_map/whitened/pallas_call | solution.py:293
  (8 shorter events, 0.1 us)
Async XLA Ops:
  3.6 47.4 %collective-permute-start = (f32[256,512]{1,0:T(8,128)S(1)}, f32[256,512]{1,0:T(8,128)S(1)}, u32[]{:S(2)}, u32[]{:S(2)}) collective-permute-start(f32[256,512]{1,0:T(8,128)S(1)} %get-tuple-element.11), channel_id=1, source_target_pairs={{0,8},{8,0},{1,9},{9,1},{2,10},{10,2},{3,11},{11,3},{4,12},{12,4},... | collective-permute-start | bytes 1572872 | tf_op jit(solution)/shard_map/ppermute | solution.py:41
  6.9 1.3 %collective-permute-start.1 = (f32[64,512]{1,0:T(8,128)S(1)}, f32[64,512]{1,0:T(8,128)S(1)}, u32[]{:S(2)}, u32[]{:S(2)}) collective-permute-start(f32[64,512]{1,0:T(8,128)S(1)} %get-tuple-element.12), channel_id=1, source_target_pairs={{0,16},{16,0},{1,17},{17,1},{2,18},{18,2},{3,19},{19,3},{4,20},{20... | collective-permute-start | bytes 393224 | tf_op jit(solution)/shard_map/ppermute | solution.py:41
  63.5 1.2 %collective-permute-start.2 = (f32[32,128]{1,0:T(8,128)S(1)}, f32[32,128]{1,0:T(8,128)S(1)}, u32[]{:S(2)}, u32[]{:S(2)}) collective-permute-start(f32[32,128]{1,0:T(8,128)S(1)} %get-tuple-element.13), channel_id=1, source_target_pairs={{0,16},{16,0},{1,17},{17,1},{2,18},{18,2},{3,19},{19,3},{4,20},{20... | collective-permute-start | bytes 49160 | tf_op jit(solution)/shard_map/ppermute | solution.py:41
  64.7 3.7 %collective-permute-start.5 = (f32[32,128]{1,0:T(8,128)S(1)}, f32[32,128]{1,0:T(8,128)S(1)}, u32[]{:S(2)}, u32[]{:S(2)}) collective-permute-start(f32[32,128]{1,0:T(8,128)S(1)} %add.25), channel_id=1, source_target_pairs={{0,7},{1,0},{2,1},{3,2},{4,3},{5,4},{6,5},{7,6},{8,15},{9,8},{10,9... | collective-permute-start | bytes 49160 | tf_op jit(solution)/shard_map/ppermute | solution.py:53
  64.7 5.0 %collective-permute-start.4 = (f32[32,128]{1,0:T(8,128)S(1)}, f32[32,128]{1,0:T(8,128)S(1)}, u32[]{:S(2)}, u32[]{:S(2)}) collective-permute-start(f32[32,128]{1,0:T(8,128)S(1)} %add.25), channel_id=1, source_target_pairs={{0,1},{1,2},{2,3},{3,4},{4,5},{5,6},{6,7},{7,0},{8,9},{9,10},{10,1... | collective-permute-start | bytes 49160 | tf_op jit(solution)/shard_map/ppermute | solution.py:53
  66.7 5.8 %collective-permute-start.3 = (f32[32,128]{1,0:T(8,128)S(1)}, f32[32,128]{1,0:T(8,128)S(1)}, u32[]{:S(2)}, u32[]{:S(2)}) collective-permute-start(f32[32,128]{1,0:T(8,128)S(1)} %add.25), channel_id=1, source_target_pairs={{0,2},{1,3},{2,4},{3,5},{4,6},{5,7},{6,0},{7,1},{8,10},{9,11},{10,... | collective-permute-start | bytes 49160 | tf_op jit(solution)/shard_map/ppermute | solution.py:53
  72.6 4.5 %collective-permute-start.8 = (f32[32,128]{1,0:T(8,128)S(1)}, f32[32,128]{1,0:T(8,128)S(1)}, u32[]{:S(2)}, u32[]{:S(2)}) collective-permute-start(f32[32,128]{1,0:T(8,128)S(1)} %add_add_fusion.1), channel_id=1, source_target_pairs={{0,96},{32,0},{64,32},{96,64},{1,97},{33,1},{65,33},{97,65},{2,98}... | collective-permute-start | bytes 49160 | tf_op jit(solution)/shard_map/ppermute | solution.py:53
  74.1 3.7 %collective-permute-start.7 = (f32[32,128]{1,0:T(8,128)S(1)}, f32[32,128]{1,0:T(8,128)S(1)}, u32[]{:S(2)}, u32[]{:S(2)}) collective-permute-start(f32[32,128]{1,0:T(8,128)S(1)} %add_add_fusion.1), channel_id=1, source_target_pairs={{0,32},{32,64},{64,96},{96,0},{1,33},{33,65},{65,97},{97,1},{2,34}... | collective-permute-start | bytes 49160 | tf_op jit(solution)/shard_map/ppermute | solution.py:53
  74.7 5.2 %collective-permute-start.6 = (f32[32,128]{1,0:T(8,128)S(1)}, f32[32,128]{1,0:T(8,128)S(1)}, u32[]{:S(2)}, u32[]{:S(2)}) collective-permute-start(f32[32,128]{1,0:T(8,128)S(1)} %add_add_fusion.1), channel_id=1, source_target_pairs={{0,64},{32,96},{64,0},{96,32},{1,65},{33,97},{65,1},{97,33},{2,66}... | collective-permute-start | bytes 49160 | tf_op jit(solution)/shard_map/ppermute | solution.py:53
  79.9 3.8 %collective-permute-start.11 = (f32[32,128]{1,0:T(8,128)S(1)}, f32[32,128]{1,0:T(8,128)S(1)}, u32[]{:S(2)}, u32[]{:S(2)}) collective-permute-start(f32[32,128]{1,0:T(8,128)S(1)} %add_add_fusion.own_ref), channel_id=1, source_target_pairs={{0,136},{128,0},{8,128},{136,8},{1,137},{129,1},{9,129},{137,9},{2... | collective-permute-start | bytes 49160 | tf_op jit(solution)/shard_map/ppermute | solution.py:53
  80.8 4.9 %collective-permute-start.10 = (f32[32,128]{1,0:T(8,128)S(1)}, f32[32,128]{1,0:T(8,128)S(1)}, u32[]{:S(2)}, u32[]{:S(2)}) collective-permute-start(f32[32,128]{1,0:T(8,128)S(1)} %add_add_fusion.own_ref), channel_id=1, source_target_pairs={{0,128},{128,8},{8,136},{136,0},{1,129},{129,9},{9,137},{137,1},{2... | collective-permute-start | bytes 49160 | tf_op jit(solution)/shard_map/ppermute | solution.py:53
  82.0 5.2 %collective-permute-start.9 = (f32[32,128]{1,0:T(8,128)S(1)}, f32[32,128]{1,0:T(8,128)S(1)}, u32[]{:S(2)}, u32[]{:S(2)}) collective-permute-start(f32[32,128]{1,0:T(8,128)S(1)} %add_add_fusion.own_ref), channel_id=1, source_target_pairs={{0,8},{128,136},{8,0},{136,128},{1,9},{129,137},{9,1},{137,129},{2... | collective-permute-start | bytes 49160 | tf_op jit(solution)/shard_map/ppermute | solution.py:53

commit v8 on v6

--- a/solution.py
+++ b/solution.py
@@ -8,11 +8,12 @@
 from jax.sharding import Mesh
 from jax.sharding import PartitionSpec as P
 
+
 AXES = ("y_lo", "x", "core", "y_hi", "z")
 GX = ("y_lo", "x", "core")
 GY = ("y_hi", "z")
-PLANE = ("y_hi", "y_lo", "x", "core")
 CHIPS = ("y_hi", "y_lo", "x")
+NEAR = ("y_lo", "x")
 HIGHEST = lax.Precision.HIGHEST
 EARLY = 6
 ON_CHIP = pl.BlockSpec(memory_space=pltpu.VMEM)
@@ -39,20 +40,20 @@
     return lax.ppermute(array, axis, [(i, i ^ 1) for i in range(lax.axis_size(axis))])
 
 
+def with_neighbour(value, axis):
+    return value + from_partner(value, axis)
+
+
 def summed_everywhere(matrix, sent):
     rows, cols = matrix.shape
-    chips, cores = lax.axis_size(CHIPS), lax.axis_size("core")
-    tiles = tiles_of(matrix).reshape(chips, 1, -1, 128)
-    tiles = jnp.broadcast_to(tiles, (chips, cores, *tiles.shape[2:]))
-    own = jnp.sum(exchanged(tiles.reshape(chips * cores, -1, 128), PLANE), axis=0)
-    own, sent = lax.optimization_barrier((own, sent))
+    tiles = tiles_of(with_neighbour(matrix, "core")).reshape(lax.axis_size(NEAR), -1, 128)
+    tiles = jnp.broadcast_to(tiles[None], (lax.axis_size("y_hi"), *tiles.shape))
+    tiles = tiles.reshape(lax.axis_size(CHIPS), -1, 128)
+    own = jnp.sum(exchanged(tiles, CHIPS), axis=0)
     come = from_partner(sent, "y_hi")
     own = jnp.sum(of_everyone(own, "z"), axis=0)
-    return from_tiles(of_everyone(own, CHIPS).reshape(-1, 8, 128), rows, cols), come
-
-
-def with_neighbour(value, axis):
-    return value + from_partner(value, axis)
+    own, come = lax.optimization_barrier((own, come))
+    return from_tiles(of_everyone(own, NEAR).reshape(-1, 8, 128), rows, cols), come
 
 
 def rounded_parts(matrix):
@@ -287,7 +288,7 @@
     )(terms, update_t)
 
 
-def per_device(tensor, y_factor, x_factor):
+def new_basis(tensor, y_factor, x_factor):
     width_x = x_factor.shape[1]
     kept, sent, folded_part = projected(tensor, y_factor, x_factor)
     folded, come = summed_everywhere(folded_part, sent)
@@ -303,5 +304,5 @@
     in_specs = (P(None, GX, GY), P(GY, None), P(None, GX))
     out_specs = P(None, AXES)
     return jax.shard_map(
-        per_device, mesh=finer, in_specs=in_specs, out_specs=out_specs, check_vma=False
+        new_basis, mesh=finer, in_specs=in_specs, out_specs=out_specs, check_vma=False
     )

time: 82.1 us -> 85.5 us (1.041)
  starting transfers between devices: 2.07 us -> 3.64 us
  blocking collectives: 68.3 us -> 69.8 us
    ppermute x3 -> x4, starting transfers between devices: 2.07 us -> 3.64 us  [from_partner(): lax.ppermute(array, axis, [(i, i ^ 1) for i in range(lax.axis_size(axis))])]
    all_to_all x5, blocking collectives: 68.3 us -> 69.8 us  [exchanged(): return lax.all_to_all(tiles, axis, 0, 0, tiled=True)]
    ppermute x3 -> x4, waiting for transfers between devices: 4.34 us -> 4.7 us  [from_partner(): lax.ppermute(array, axis, [(i, i ^ 1) for i in range(lax.axis_size(axis))])]
  transfers between devices with their start and end apart: 3 -> 4, of which waited for: 2 -> 2; matrix products, arithmetic and copies ran while one was open for 0% -> 0% of each run, Pallas kernels for 0% -> 0%
where the time goes in v8:
time: 85.5 us; the launch traced here: 85.2 us
  blocking collectives  69.8 us (82%)
  Pallas kernels  6.88 us (8%)
  waiting for transfers between devices  4.7 us (5%)
  starting transfers between devices  3.64 us (4%)
    all_to_all x5, blocking collectives, exchanged(): return lax.all_to_all(tiles, axis, 0, 0, tiled=True)  69.8 us
    ppermute x4, waiting for transfers between devices, from_partner(): lax.ppermute(array, axis, [(i, i ^ 1) for i in range(lax.axis_size(axis))])  4.7 us
    ppermute x4, starting transfers between devices, from_partner(): lax.ppermute(array, axis, [(i, i ^ 1) for i in range(lax.axis_size(axis))])  3.64 us
    pallas_call x1, Pallas kernels, projected(): pl.pallas_call(project_kernel, out_shape=[jax.ShapeDtypeStruct((n, rows),...  3.57 us
    pallas_call x1, Pallas kernels, whitened(): pl.pallas_call(functools.partial(whitened_kernel, scale), out_shape=jax.S...  2.3 us
  transfers between devices with their start and end apart: 4, of which 2 were waited for; matrix products, arithmetic and copies ran while one was open for 0% of the time, Pallas kernels for 0%

profile of v8, /device:TPU:2, one launch (start us, length us, event | category | flops | bytes accessed | tf_op | source)
XLA Modules:
  0.0 85.2 jit_solution(12726599323723108914)
XLA Ops:
  0.0 3.6 %projected.1 = (f32[256,512]{1,0:T(8,128)S(1)}, f32[256,512]{1,0:T(8,128)S(1)}, f32[64,512]{1,0:T(8,128)S(1)}) custom-call(bf16[8,512,512]{2,1,0:T(8,128)(2,1)} %tensor_ref.1, bf16[64,512]{1,0:T(8,128)(2,1)} %bitcast.16, bf16[64,512]{1,0:T(8,128)(2,1)} %x_ref.1), custom_call_target="tpu_custom_call" | custom-call | tf_op jit(solution)/shard_map/projected/pallas_call | solution.py:135
  3.6 0.1 collective-permute-start
  3.7 3.3 %collective-permute-start.1 = (f32[256,512]{1,0:T(8,128)S(1)}, f32[256,512]{1,0:T(8,128)S(1)}, u32[]{:S(2)}, u32[]{:S(2)}) collective-permute-start(f32[256,512]{1,0:T(8,128)S(1)} %get-tuple-element.14), channel_id=1, source_target_pairs={{0,8},{8,0},{1,9},{9,1},{2,10},{10,2},{3,11},{11,3},{4,12},{12,4},... | collective-permute-start | bytes 1572872 | tf_op jit(solution)/shard_map/ppermute | solution.py:40
  7.0 0.0 collective-permute-done
  7.0 15.7 %all_to_all.25 = f32[16,32,128]{2,1,0:T(8,128)S(1)} all-to-all(f32[16,32,128]{2,1,0:T(8,128)S(1)} %bitcast.15), channel_id=1, replica_groups=mesh['y_lo'=2,'x'=4,'core'=2,'y_hi'=2,'z'=8] {'y_hi','y_lo','x'}, dimensions={0} | all-to-all | bytes 524288 | tf_op jit(solution)/shard_map/all_to_all | solution.py:23
  22.8 17.3 %all_to_all.26 = f32[8,32,128]{2,1,0:T(8,128)S(1)} all-to-all(f32[8,32,128]{2,1,0:T(8,128)S(1)} %broadcast_in_dim.12), channel_id=1, replica_groups=mesh['y_lo'=2,'x'=4,'core'=2,'y_hi'=2,'z'=8] {'z'}, dimensions={0} | all-to-all | bytes 262144 | tf_op jit(solution)/shard_map/all_to_all | solution.py:23
  40.1 0.0 collective-permute-done.1.come_ref
  40.2 10.8 %all_to_all.27 = f32[8,32,128]{2,1,0:T(8,128)S(1)} all-to-all(f32[8,32,128]{2,1,0:T(8,128)S(1)} %broadcast_in_dim.13), channel_id=1, replica_groups=mesh['y_lo'=2,'x'=4,'core'=2,'y_hi'=2,'z'=8] {'y_lo','x'}, dimensions={0} | all-to-all | bytes 262144 | tf_op jit(solution)/shard_map/all_to_all | solution.py:23
  51.0 0.7 update_parts.1
  51.7 12.9 %all_to_all.28.parts_ref = f32[8,64,128]{2,1,0:T(8,128)S(1)} all-to-all(f32[8,64,128]{2,1,0:T(8,128)S(1)} %update_parts.1), channel_id=1, replica_groups=mesh['y_lo'=2,'x'=4,'core'=2,'y_hi'=2,'z'=8] {'z'}, dimensions={0} | all-to-all | bytes 524288 | tf_op jit(solution)/shard_map/all_to_all | solution.py:23
  64.5 0.4 own_update.1
  64.9 0.0 collective-permute-start.2
  64.9 1.2 %collective-permute-done.2 = f32[32,128]{1,0:T(8,128)S(1)} collective-permute-done((f32[32,128]{1,0:T(8,128)S(1)}, f32[32,128]{1,0:T(8,128)S(1)}, u32[]{:S(2)}, u32[]{:S(2)}) %collective-permute-start.2) | collective-permute-done | bytes 16416 | tf_op jit(solution)/shard_map/ppermute | solution.py:40
  66.1 0.2 collective-permute-start.3
  66.3 3.5 %collective-permute-done.3 = f32[32,128]{1,0:T(8,128)S(1)} collective-permute-done((f32[32,128]{1,0:T(8,128)S(1)}, f32[32,128]{1,0:T(8,128)S(1)}, u32[]{:S(2)}, u32[]{:S(2)}) %collective-permute-start.3) | collective-permute-done | bytes 16416 | tf_op jit(solution)/shard_map/ppermute | solution.py:40
  69.9 13.0 %all_to_all.29.cross_ref = f32[16,32,128]{2,1,0:T(8,128)S(1)} all-to-all(f32[16,32,128]{2,1,0:T(8,128)S(1)} %broadcast_in_dim.14), channel_id=1, replica_groups=mesh['y_lo'=2,'x'=4,'core'=2,'y_hi'=2,'z'=8] {'y_hi','y_lo','x'}, dimensions={0} | all-to-all | bytes 524288 | tf_op jit(solution)/shard_map/all_to_all | solution.py:23
  82.9 2.3 %whitened.1 = f32[32,64]{1,0:T(8,128)} custom-call(f32[16,32,128]{2,1,0:T(8,128)S(1)} %all_to_all.29.cross_ref, f32[32,64]{1,0:T(8,128)S(1)} %get-tuple-element.18.update_ref), custom_call_target="tpu_custom_call" | custom-call | tf_op jit(solution)/shard_map/whitened/pallas_call | solution.py:280
  (9 shorter events, 0.1 us)
Async XLA Ops:
  3.6 3.4 %collective-permute-start = (f32[64,512]{1,0:T(8,128)S(1)}, f32[64,512]{1,0:T(8,128)S(1)}, u32[]{:S(2)}, u32[]{:S(2)}) collective-permute-start(f32[64,512]{1,0:T(8,128)S(1)} %get-tuple-element.13), channel_id=1, source_target_pairs={{0,16},{16,0},{1,17},{17,1},{2,18},{18,2},{3,19},{19,3},{4,20},{20... | collective-permute-start | bytes 393224 | tf_op jit(solution)/shard_map/ppermute | solution.py:40
  3.7 36.5 %collective-permute-start.1 = (f32[256,512]{1,0:T(8,128)S(1)}, f32[256,512]{1,0:T(8,128)S(1)}, u32[]{:S(2)}, u32[]{:S(2)}) collective-permute-start(f32[256,512]{1,0:T(8,128)S(1)} %get-tuple-element.14), channel_id=1, source_target_pairs={{0,8},{8,0},{1,9},{9,1},{2,10},{10,2},{3,11},{11,3},{4,12},{12,4},... | collective-permute-start | bytes 1572872 | tf_op jit(solution)/shard_map/ppermute | solution.py:40
  64.9 1.2 %collective-permute-start.2 = (f32[32,128]{1,0:T(8,128)S(1)}, f32[32,128]{1,0:T(8,128)S(1)}, u32[]{:S(2)}, u32[]{:S(2)}) collective-permute-start(f32[32,128]{1,0:T(8,128)S(1)} %get-tuple-element.17), channel_id=1, source_target_pairs={{0,16},{16,0},{1,17},{17,1},{2,18},{18,2},{3,19},{19,3},{4,20},{20... | collective-permute-start | bytes 49160 | tf_op jit(solution)/shard_map/ppermute | solution.py:40
  66.1 3.7 %collective-permute-start.3 = (f32[32,128]{1,0:T(8,128)S(1)}, f32[32,128]{1,0:T(8,128)S(1)}, u32[]{:S(2)}, u32[]{:S(2)}) collective-permute-start(f32[32,128]{1,0:T(8,128)S(1)} %add.10), channel_id=1, source_target_pairs={{0,1},{1,0},{2,3},{3,2},{4,5},{5,4},{6,7},{7,6},{8,9},{9,8},{10,11... | collective-permute-start | bytes 49160 | tf_op jit(solution)/shard_map/ppermute | solution.py:40

commit v9 on v8

--- a/solution.py
+++ b/solution.py
@@ -13,7 +13,6 @@
 GX = ("y_lo", "x", "core")
 GY = ("y_hi", "z")
 CHIPS = ("y_hi", "y_lo", "x")
-NEAR = ("y_lo", "x")
 HIGHEST = lax.Precision.HIGHEST
 EARLY = 6
 ON_CHIP = pl.BlockSpec(memory_space=pltpu.VMEM)
@@ -46,14 +45,12 @@
 
 def summed_everywhere(matrix, sent):
     rows, cols = matrix.shape
-    tiles = tiles_of(with_neighbour(matrix, "core")).reshape(lax.axis_size(NEAR), -1, 128)
-    tiles = jnp.broadcast_to(tiles[None], (lax.axis_size("y_hi"), *tiles.shape))
-    tiles = tiles.reshape(lax.axis_size(CHIPS), -1, 128)
-    own = jnp.sum(exchanged(tiles, CHIPS), axis=0)
+    tiles = tiles_of(matrix).reshape(lax.axis_size("z"), -1, 128)
     come = from_partner(sent, "y_hi")
-    own = jnp.sum(of_everyone(own, "z"), axis=0)
+    own = jnp.sum(exchanged(tiles, "z"), axis=0)
+    own = jnp.sum(of_everyone(with_neighbour(own, "core"), CHIPS), axis=0)
     own, come = lax.optimization_barrier((own, come))
-    return from_tiles(of_everyone(own, NEAR).reshape(-1, 8, 128), rows, cols), come
+    return from_tiles(of_everyone(own, "z").reshape(-1, 8, 128), rows, cols), come
 
 
 def rounded_parts(matrix):

time: 85.5 us -> 82.9 us (0.970)
  blocking collectives: 69.8 us -> 66 us
    all_to_all x5, blocking collectives: 69.8 us -> 66 us  [exchanged(): return lax.all_to_all(tiles, axis, 0, 0, tiled=True)]
  transfers between devices with their start and end apart: 4 -> 4, of which waited for: 2 -> 3; matrix products, arithmetic and copies ran while one was open for 0% -> 0% of each run, Pallas kernels for 0% -> 0%
where the time goes in v9:
time: 82.9 us; the launch traced here: 82.6 us
  blocking collectives  66 us (80%)
  Pallas kernels  6.88 us (8%)
  waiting for transfers between devices  5.51 us (7%)
  starting transfers between devices  3.99 us (5%)
    all_to_all x5, blocking collectives, exchanged(): return lax.all_to_all(tiles, axis, 0, 0, tiled=True)  66 us
    ppermute x4, waiting for transfers between devices, from_partner(): lax.ppermute(array, axis, [(i, i ^ 1) for i in range(lax.axis_size(axis))])  5.51 us
    ppermute x4, starting transfers between devices, from_partner(): lax.ppermute(array, axis, [(i, i ^ 1) for i in range(lax.axis_size(axis))])  3.99 us
    pallas_call x1, Pallas kernels, projected(): pl.pallas_call(project_kernel, out_shape=[jax.ShapeDtypeStruct((n, rows),...  3.57 us
    pallas_call x1, Pallas kernels, whitened(): pl.pallas_call(functools.partial(whitened_kernel, scale), out_shape=jax.S...  2.3 us
  transfers between devices with their start and end apart: 4, of which 3 were waited for; matrix products, arithmetic and copies ran while one was open for 0% of the time, Pallas kernels for 0%

profile of v9, /device:TPU:2, one launch (start us, length us, event | category | flops | bytes accessed | tf_op | source)
XLA Modules:
  0.0 82.6 jit_solution(6785493623684750897)
XLA Ops:
  0.0 3.6 %projected.1 = (f32[256,512]{1,0:T(8,128)S(1)}, f32[256,512]{1,0:T(8,128)S(1)}, f32[64,512]{1,0:T(8,128)S(1)}) custom-call(bf16[8,512,512]{2,1,0:T(8,128)(2,1)} %tensor_ref.1, bf16[64,512]{1,0:T(8,128)(2,1)} %bitcast.14, bf16[64,512]{1,0:T(8,128)(2,1)} %x_ref.1), custom_call_target="tpu_custom_call" | custom-call | tf_op jit(solution)/shard_map/projected/pallas_call | solution.py:132
  3.6 3.3 %collective-permute-start.1 = (f32[256,512]{1,0:T(8,128)S(1)}, f32[256,512]{1,0:T(8,128)S(1)}, u32[]{:S(2)}, u32[]{:S(2)}) collective-permute-start(f32[256,512]{1,0:T(8,128)S(1)} %get-tuple-element.14), channel_id=1, source_target_pairs={{0,8},{8,0},{1,9},{9,1},{2,10},{10,2},{3,11},{11,3},{4,12},{12,4},... | collective-permute-start | bytes 1572872 | tf_op jit(solution)/shard_map/ppermute | solution.py:39
  6.9 17.3 %all_to_all.25 = f32[8,32,128]{2,1,0:T(8,128)S(1)} all-to-all(f32[8,32,128]{2,1,0:T(8,128)S(1)} %bitcast.13), channel_id=1, replica_groups=mesh['y_lo'=2,'x'=4,'core'=2,'y_hi'=2,'z'=8] {'z'}, dimensions={0} | all-to-all | bytes 262144 | tf_op jit(solution)/shard_map/all_to_all | solution.py:22
  24.2 0.1 collective-permute-start
  24.3 1.2 %collective-permute-done = f32[32,128]{1,0:T(8,128)S(1)} collective-permute-done((f32[32,128]{1,0:T(8,128)S(1)}, f32[32,128]{1,0:T(8,128)S(1)}, u32[]{:S(2)}, u32[]{:S(2)}) %collective-permute-start) | collective-permute-done | bytes 16416 | tf_op jit(solution)/shard_map/ppermute | solution.py:39
  25.5 12.8 %all_to_all.26 = f32[16,32,128]{2,1,0:T(8,128)S(1)} all-to-all(f32[16,32,128]{2,1,0:T(8,128)S(1)} %broadcast_in_dim.6), channel_id=1, replica_groups=mesh['y_lo'=2,'x'=4,'core'=2,'y_hi'=2,'z'=8] {'y_hi','y_lo','x'}, dimensions={0} | all-to-all | bytes 524288 | tf_op jit(solution)/shard_map/all_to_all | solution.py:22
  38.3 0.0 collective-permute-done.1.come_ref
  38.3 11.5 %all_to_all.27 = f32[8,32,128]{2,1,0:T(8,128)S(1)} all-to-all(f32[8,32,128]{2,1,0:T(8,128)S(1)} %broadcast_in_dim.7), channel_id=1, replica_groups=mesh['y_lo'=2,'x'=4,'core'=2,'y_hi'=2,'z'=8] {'z'}, dimensions={0} | all-to-all | bytes 262144 | tf_op jit(solution)/shard_map/all_to_all | solution.py:22
  49.8 0.7 update_parts.1
  50.5 12.9 %all_to_all.28.parts_ref = f32[8,64,128]{2,1,0:T(8,128)S(1)} all-to-all(f32[8,64,128]{2,1,0:T(8,128)S(1)} %update_parts.1), channel_id=1, replica_groups=mesh['y_lo'=2,'x'=4,'core'=2,'y_hi'=2,'z'=8] {'z'}, dimensions={0} | all-to-all | bytes 524288 | tf_op jit(solution)/shard_map/all_to_all | solution.py:22
  63.4 0.4 own_update.1
  63.7 0.0 collective-permute-start.2
  63.8 1.2 %collective-permute-done.2 = f32[32,128]{1,0:T(8,128)S(1)} collective-permute-done((f32[32,128]{1,0:T(8,128)S(1)}, f32[32,128]{1,0:T(8,128)S(1)}, u32[]{:S(2)}, u32[]{:S(2)}) %collective-permute-start.2) | collective-permute-done | bytes 16416 | tf_op jit(solution)/shard_map/ppermute | solution.py:39
  64.9 0.6 collective-permute-start.3
  65.5 3.2 %collective-permute-done.3 = f32[32,128]{1,0:T(8,128)S(1)} collective-permute-done((f32[32,128]{1,0:T(8,128)S(1)}, f32[32,128]{1,0:T(8,128)S(1)}, u32[]{:S(2)}, u32[]{:S(2)}) %collective-permute-start.3) | collective-permute-done | bytes 16416 | tf_op jit(solution)/shard_map/ppermute | solution.py:39
  68.7 11.6 %all_to_all.29.cross_ref = f32[16,32,128]{2,1,0:T(8,128)S(1)} all-to-all(f32[16,32,128]{2,1,0:T(8,128)S(1)} %broadcast_in_dim.8), channel_id=1, replica_groups=mesh['y_lo'=2,'x'=4,'core'=2,'y_hi'=2,'z'=8] {'y_hi','y_lo','x'}, dimensions={0} | all-to-all | bytes 524288 | tf_op jit(solution)/shard_map/all_to_all | solution.py:22
  80.3 2.3 %whitened.1 = f32[32,64]{1,0:T(8,128)} custom-call(f32[16,32,128]{2,1,0:T(8,128)S(1)} %all_to_all.29.cross_ref, f32[32,64]{1,0:T(8,128)S(1)} %get-tuple-element.18.update_ref), custom_call_target="tpu_custom_call" | custom-call | tf_op jit(solution)/shard_map/whitened/pallas_call | solution.py:277
  (8 shorter events, 0.1 us)
Async XLA Ops:
  3.6 34.7 %collective-permute-start.1 = (f32[256,512]{1,0:T(8,128)S(1)}, f32[256,512]{1,0:T(8,128)S(1)}, u32[]{:S(2)}, u32[]{:S(2)}) collective-permute-start(f32[256,512]{1,0:T(8,128)S(1)} %get-tuple-element.14), channel_id=1, source_target_pairs={{0,8},{8,0},{1,9},{9,1},{2,10},{10,2},{3,11},{11,3},{4,12},{12,4},... | collective-permute-start | bytes 1572872 | tf_op jit(solution)/shard_map/ppermute | solution.py:39
  24.2 1.3 %collective-permute-start = (f32[32,128]{1,0:T(8,128)S(1)}, f32[32,128]{1,0:T(8,128)S(1)}, u32[]{:S(2)}, u32[]{:S(2)}) collective-permute-start(f32[32,128]{1,0:T(8,128)S(1)} %reduce_sum.18), channel_id=1, source_target_pairs={{0,16},{16,0},{1,17},{17,1},{2,18},{18,2},{3,19},{19,3},{4,20},{20... | collective-permute-start | bytes 49160 | tf_op jit(solution)/shard_map/ppermute | solution.py:39
  63.7 1.2 %collective-permute-start.2 = (f32[32,128]{1,0:T(8,128)S(1)}, f32[32,128]{1,0:T(8,128)S(1)}, u32[]{:S(2)}, u32[]{:S(2)}) collective-permute-start(f32[32,128]{1,0:T(8,128)S(1)} %get-tuple-element.17), channel_id=1, source_target_pairs={{0,16},{16,0},{1,17},{17,1},{2,18},{18,2},{3,19},{19,3},{4,20},{20... | collective-permute-start | bytes 49160 | tf_op jit(solution)/shard_map/ppermute | solution.py:39
  64.9 3.7 %collective-permute-start.3 = (f32[32,128]{1,0:T(8,128)S(1)}, f32[32,128]{1,0:T(8,128)S(1)}, u32[]{:S(2)}, u32[]{:S(2)}) collective-permute-start(f32[32,128]{1,0:T(8,128)S(1)} %add.10), channel_id=1, source_target_pairs={{0,1},{1,0},{2,3},{3,2},{4,5},{5,4},{6,7},{7,6},{8,9},{9,8},{10,11... | collective-permute-start | bytes 49160 | tf_op jit(solution)/shard_map/ppermute | solution.py:39

commit v10 on v8

--- a/solution.py
+++ b/solution.py
@@ -7,7 +7,6 @@
 from jax.experimental.pallas import tpu as pltpu
 from jax.sharding import Mesh
 from jax.sharding import PartitionSpec as P
-
 
 AXES = ("y_lo", "x", "core", "y_hi", "z")
 GX = ("y_lo", "x", "core")
@@ -50,6 +49,7 @@
     tiles = jnp.broadcast_to(tiles[None], (lax.axis_size("y_hi"), *tiles.shape))
     tiles = tiles.reshape(lax.axis_size(CHIPS), -1, 128)
     own = jnp.sum(exchanged(tiles, CHIPS), axis=0)
+    own, sent = lax.optimization_barrier((own, sent))
     come = from_partner(sent, "y_hi")
     own = jnp.sum(of_everyone(own, "z"), axis=0)
     own, come = lax.optimization_barrier((own, come))
@@ -288,7 +288,7 @@
     )(terms, update_t)
 
 
-def new_basis(tensor, y_factor, x_factor):
+def per_device(tensor, y_factor, x_factor):
     width_x = x_factor.shape[1]
     kept, sent, folded_part = projected(tensor, y_factor, x_factor)
     folded, come = summed_everywhere(folded_part, sent)
@@ -304,5 +304,5 @@
     in_specs = (P(None, GX, GY), P(GY, None), P(None, GX))
     out_specs = P(None, AXES)
     return jax.shard_map(
-        new_basis, mesh=finer, in_specs=in_specs, out_specs=out_specs, check_vma=False
+        per_device, mesh=finer, in_specs=in_specs, out_specs=out_specs, check_vma=False
     )

time: 85.5 us -> 82.7 us (0.967)
  starting transfers between devices: 3.64 us -> 1.29 us
  blocking collectives: 69.8 us -> 68 us
  waiting for transfers between devices: 4.7 us -> 6.03 us
    ppermute x4, starting transfers between devices: 3.64 us -> 1.29 us  [from_partner(): lax.ppermute(array, axis, [(i, i ^ 1) for i in range(lax.axis_size(axis))])]
    all_to_all x5, blocking collectives: 69.8 us -> 68 us  [exchanged(): return lax.all_to_all(tiles, axis, 0, 0, tiled=True)]
    ppermute x4, waiting for transfers between devices: 4.7 us -> 6.03 us  [from_partner(): lax.ppermute(array, axis, [(i, i ^ 1) for i in range(lax.axis_size(axis))])]
  transfers between devices with their start and end apart: 4 -> 4, of which waited for: 2 -> 3; matrix products, arithmetic and copies ran while one was open for 0% -> 0% of each run, Pallas kernels for 0% -> 0%
where the time goes in v10:
time: 82.7 us; the launch traced here: 82.4 us
  blocking collectives  68 us (82%)
  Pallas kernels  6.88 us (8%)
  waiting for transfers between devices  6.03 us (7%)
  starting transfers between devices  1.29 us (2%)
    all_to_all x5, blocking collectives, exchanged(): return lax.all_to_all(tiles, axis, 0, 0, tiled=True)  68 us
    ppermute x4, waiting for transfers between devices, from_partner(): lax.ppermute(array, axis, [(i, i ^ 1) for i in range(lax.axis_size(axis))])  6.03 us
    pallas_call x1, Pallas kernels, projected(): pl.pallas_call(project_kernel, out_shape=[jax.ShapeDtypeStruct((n, rows),...  3.57 us
    pallas_call x1, Pallas kernels, whitened(): pl.pallas_call(functools.partial(whitened_kernel, scale), out_shape=jax.S...  2.3 us
  transfers between devices with their start and end apart: 4, of which 3 were waited for; matrix products, arithmetic and copies ran while one was open for 0% of the time, Pallas kernels for 0%

profile of v10, /device:TPU:2, one launch (start us, length us, event | category | flops | bytes accessed | tf_op | source)
XLA Modules:
  0.0 82.4 jit_solution(15566195869708608994)
XLA Ops:
  0.0 3.6 %projected.1 = (f32[256,512]{1,0:T(8,128)S(1)}, f32[256,512]{1,0:T(8,128)S(1)}, f32[64,512]{1,0:T(8,128)S(1)}) custom-call(bf16[8,512,512]{2,1,0:T(8,128)(2,1)} %tensor_ref.1, bf16[64,512]{1,0:T(8,128)(2,1)} %bitcast.16, bf16[64,512]{1,0:T(8,128)(2,1)} %x_ref.1), custom_call_target="tpu_custom_call" | custom-call | tf_op jit(solution)/shard_map/projected/pallas_call | solution.py:135
  3.6 0.1 collective-permute-start
  3.7 1.3 %collective-permute-done = f32[64,512]{1,0:T(8,128)S(1)} collective-permute-done((f32[64,512]{1,0:T(8,128)S(1)}, f32[64,512]{1,0:T(8,128)S(1)}, u32[]{:S(2)}, u32[]{:S(2)}) %collective-permute-start) | collective-permute-done | bytes 131104 | tf_op jit(solution)/shard_map/ppermute | solution.py:39
  5.1 14.9 %all_to_all.25 = f32[16,32,128]{2,1,0:T(8,128)S(1)} all-to-all(f32[16,32,128]{2,1,0:T(8,128)S(1)} %bitcast.15), channel_id=1, replica_groups=mesh['y_lo'=2,'x'=4,'core'=2,'y_hi'=2,'z'=8] {'y_hi','y_lo','x'}, dimensions={0} | all-to-all | bytes 524288 | tf_op jit(solution)/shard_map/all_to_all | solution.py:22
  20.0 0.9 %collective-permute-start.1 = (f32[256,512]{1,0:T(8,128)S(1)}, f32[256,512]{1,0:T(8,128)S(1)}, u32[]{:S(2)}, u32[]{:S(2)}) collective-permute-start(f32[256,512]{1,0:T(8,128)S(1)} %get-tuple-element.18), channel_id=1, source_target_pairs={{0,8},{8,0},{1,9},{9,1},{2,10},{10,2},{3,11},{11,3},{4,12},{12,4},... | collective-permute-start | bytes 1572872 | tf_op jit(solution)/shard_map/ppermute | solution.py:39
  20.9 17.3 %all_to_all.26 = f32[8,32,128]{2,1,0:T(8,128)S(1)} all-to-all(f32[8,32,128]{2,1,0:T(8,128)S(1)} %broadcast_in_dim.12), channel_id=1, replica_groups=mesh['y_lo'=2,'x'=4,'core'=2,'y_hi'=2,'z'=8] {'z'}, dimensions={0} | all-to-all | bytes 262144 | tf_op jit(solution)/shard_map/all_to_all | solution.py:22
  38.3 0.0 collective-permute-done.1.come_ref
  38.3 9.5 %all_to_all.27 = f32[8,32,128]{2,1,0:T(8,128)S(1)} all-to-all(f32[8,32,128]{2,1,0:T(8,128)S(1)} %broadcast_in_dim.13), channel_id=1, replica_groups=mesh['y_lo'=2,'x'=4,'core'=2,'y_hi'=2,'z'=8] {'y_lo','x'}, dimensions={0} | all-to-all | bytes 262144 | tf_op jit(solution)/shard_map/all_to_all | solution.py:22
  47.8 0.7 update_parts.1
  48.5 14.6 %all_to_all.28.parts_ref = f32[8,64,128]{2,1,0:T(8,128)S(1)} all-to-all(f32[8,64,128]{2,1,0:T(8,128)S(1)} %update_parts.1), channel_id=1, replica_groups=mesh['y_lo'=2,'x'=4,'core'=2,'y_hi'=2,'z'=8] {'z'}, dimensions={0} | all-to-all | bytes 524288 | tf_op jit(solution)/shard_map/all_to_all | solution.py:22
  63.1 0.4 own_update.1
  63.5 0.0 collective-permute-start.2
  63.5 1.2 %collective-permute-done.2 = f32[32,128]{1,0:T(8,128)S(1)} collective-permute-done((f32[32,128]{1,0:T(8,128)S(1)}, f32[32,128]{1,0:T(8,128)S(1)}, u32[]{:S(2)}, u32[]{:S(2)}) %collective-permute-start.2) | collective-permute-done | bytes 16416 | tf_op jit(solution)/shard_map/ppermute | solution.py:39
  64.7 0.2 collective-permute-start.3
  64.9 3.5 %collective-permute-done.3 = f32[32,128]{1,0:T(8,128)S(1)} collective-permute-done((f32[32,128]{1,0:T(8,128)S(1)}, f32[32,128]{1,0:T(8,128)S(1)}, u32[]{:S(2)}, u32[]{:S(2)}) %collective-permute-start.3) | collective-permute-done | bytes 16416 | tf_op jit(solution)/shard_map/ppermute | solution.py:39
  68.5 11.7 %all_to_all.29.cross_ref = f32[16,32,128]{2,1,0:T(8,128)S(1)} all-to-all(f32[16,32,128]{2,1,0:T(8,128)S(1)} %broadcast_in_dim.14), channel_id=1, replica_groups=mesh['y_lo'=2,'x'=4,'core'=2,'y_hi'=2,'z'=8] {'y_hi','y_lo','x'}, dimensions={0} | all-to-all | bytes 524288 | tf_op jit(solution)/shard_map/all_to_all | solution.py:22
  80.1 2.3 %whitened.1 = f32[32,64]{1,0:T(8,128)} custom-call(f32[16,32,128]{2,1,0:T(8,128)S(1)} %all_to_all.29.cross_ref, f32[32,64]{1,0:T(8,128)S(1)} %get-tuple-element.22.update_ref), custom_call_target="tpu_custom_call" | custom-call | tf_op jit(solution)/shard_map/whitened/pallas_call | solution.py:280
  (9 shorter events, 0.1 us)
Async XLA Ops:
  3.6 1.4 %collective-permute-start = (f32[64,512]{1,0:T(8,128)S(1)}, f32[64,512]{1,0:T(8,128)S(1)}, u32[]{:S(2)}, u32[]{:S(2)}) collective-permute-start(f32[64,512]{1,0:T(8,128)S(1)} %get-tuple-element.15), channel_id=1, source_target_pairs={{0,16},{16,0},{1,17},{17,1},{2,18},{18,2},{3,19},{19,3},{4,20},{20... | collective-permute-start | bytes 393224 | tf_op jit(solution)/shard_map/ppermute | solution.py:39
  20.0 18.3 %collective-permute-start.1 = (f32[256,512]{1,0:T(8,128)S(1)}, f32[256,512]{1,0:T(8,128)S(1)}, u32[]{:S(2)}, u32[]{:S(2)}) collective-permute-start(f32[256,512]{1,0:T(8,128)S(1)} %get-tuple-element.18), channel_id=1, source_target_pairs={{0,8},{8,0},{1,9},{9,1},{2,10},{10,2},{3,11},{11,3},{4,12},{12,4},... | collective-permute-start | bytes 1572872 | tf_op jit(solution)/shard_map/ppermute | solution.py:39
  63.5 1.2 %collective-permute-start.2 = (f32[32,128]{1,0:T(8,128)S(1)}, f32[32,128]{1,0:T(8,128)S(1)}, u32[]{:S(2)}, u32[]{:S(2)}) collective-permute-start(f32[32,128]{1,0:T(8,128)S(1)} %get-tuple-element.21), channel_id=1, source_target_pairs={{0,16},{16,0},{1,17},{17,1},{2,18},{18,2},{3,19},{19,3},{4,20},{20... | collective-permute-start | bytes 49160 | tf_op jit(solution)/shard_map/ppermute | solution.py:39
  64.7 3.7 %collective-permute-start.3 = (f32[32,128]{1,0:T(8,128)S(1)}, f32[32,128]{1,0:T(8,128)S(1)}, u32[]{:S(2)}, u32[]{:S(2)}) collective-permute-start(f32[32,128]{1,0:T(8,128)S(1)} %add.10), channel_id=1, source_target_pairs={{0,1},{1,0},{2,3},{3,2},{4,5},{5,4},{6,7},{7,6},{8,9},{9,8},{10,11... | collective-permute-start | bytes 49160 | tf_op jit(solution)/shard_map/ppermute | solution.py:39

commit v11 on v9

--- a/solution.py
+++ b/solution.py
@@ -45,12 +45,11 @@
 
 def summed_everywhere(matrix, sent):
     rows, cols = matrix.shape
-    tiles = tiles_of(matrix).reshape(lax.axis_size("z"), -1, 128)
+    tiles = tiles_of(matrix).reshape(lax.axis_size(CHIPS), -1, 128)
+    own = jnp.sum(exchanged(tiles, CHIPS), axis=0)
     come = from_partner(sent, "y_hi")
-    own = jnp.sum(exchanged(tiles, "z"), axis=0)
-    own = jnp.sum(of_everyone(with_neighbour(own, "core"), CHIPS), axis=0)
-    own, come = lax.optimization_barrier((own, come))
-    return from_tiles(of_everyone(own, "z").reshape(-1, 8, 128), rows, cols), come
+    own = jnp.sum(of_everyone(own, ("core", "z")), axis=0)
+    return from_tiles(of_everyone(own, CHIPS).reshape(-1, 8, 128), rows, cols), come
 
 
 def rounded_parts(matrix):

time: 82.9 us -> 85.3 us (1.029)
  blocking collectives: 66 us -> 69.8 us
  waiting for transfers between devices: 5.51 us -> 4.35 us
    all_to_all x5, blocking collectives: 66 us -> 69.8 us  [exchanged(): return lax.all_to_all(tiles, axis, 0, 0, tiled=True)]
    ppermute x4 -> x3, waiting for transfers between devices: 5.51 us -> 4.35 us  [from_partner(): lax.ppermute(array, axis, [(i, i ^ 1) for i in range(lax.axis_size(axis))])]
    ppermute x4 -> x3, starting transfers between devices: 3.99 us -> 3.89 us  [from_partner(): lax.ppermute(array, axis, [(i, i ^ 1) for i in range(lax.axis_size(axis))])]
  transfers between devices with their start and end apart: 4 -> 3, of which waited for: 3 -> 2; matrix products, arithmetic and copies ran while one was open for 0% -> 0% of each run, Pallas kernels for 0% -> 0%
where the time goes in v11:
time: 85.3 us; the launch traced here: 85 us
  blocking collectives  69.8 us (82%)
  Pallas kernels  6.88 us (8%)
  waiting for transfers between devices  4.35 us (5%)
  starting transfers between devices  3.89 us (5%)
    all_to_all x5, blocking collectives, exchanged(): return lax.all_to_all(tiles, axis, 0, 0, tiled=True)  69.8 us
    ppermute x3, waiting for transfers between devices, from_partner(): lax.ppermute(array, axis, [(i, i ^ 1) for i in range(lax.axis_size(axis))])  4.35 us
    ppermute x3, starting transfers between devices, from_partner(): lax.ppermute(array, axis, [(i, i ^ 1) for i in range(lax.axis_size(axis))])  3.89 us
    pallas_call x1, Pallas kernels, projected(): pl.pallas_call(project_kernel, out_shape=[jax.ShapeDtypeStruct((n, rows),...  3.57 us
    pallas_call x1, Pallas kernels, whitened(): pl.pallas_call(functools.partial(whitened_kernel, scale), out_shape=jax.S...  2.3 us
  transfers between devices with their start and end apart: 3, of which 2 were waited for; matrix products, arithmetic and copies ran while one was open for 0% of the time, Pallas kernels for 0%

profile of v11, /device:TPU:2, one launch (start us, length us, event | category | flops | bytes accessed | tf_op | source)
XLA Modules:
  0.0 85.0 jit_solution(5535008501132942678)
XLA Ops:
  0.0 3.6 %projected.1 = (f32[256,512]{1,0:T(8,128)S(1)}, f32[256,512]{1,0:T(8,128)S(1)}, f32[64,512]{1,0:T(8,128)S(1)}) custom-call(bf16[8,512,512]{2,1,0:T(8,128)(2,1)} %tensor_ref.1, bf16[64,512]{1,0:T(8,128)(2,1)} %bitcast.14, bf16[64,512]{1,0:T(8,128)(2,1)} %x_ref.1), custom_call_target="tpu_custom_call" | custom-call | tf_op jit(solution)/shard_map/projected/pallas_call | solution.py:131
  3.6 3.3 %collective-permute-start = (f32[256,512]{1,0:T(8,128)S(1)}, f32[256,512]{1,0:T(8,128)S(1)}, u32[]{:S(2)}, u32[]{:S(2)}) collective-permute-start(f32[256,512]{1,0:T(8,128)S(1)} %get-tuple-element.11), channel_id=1, source_target_pairs={{0,8},{8,0},{1,9},{9,1},{2,10},{10,2},{3,11},{11,3},{4,12},{12,4},... | collective-permute-start | bytes 1572872 | tf_op jit(solution)/shard_map/ppermute | solution.py:39
  6.9 13.8 %all_to_all.25 = f32[16,16,128]{2,1,0:T(8,128)S(1)} all-to-all(f32[16,16,128]{2,1,0:T(8,128)S(1)} %bitcast.13), channel_id=1, replica_groups=mesh['y_lo'=2,'x'=4,'core'=2,'y_hi'=2,'z'=8] {'y_hi','y_lo','x'}, dimensions={0} | all-to-all | bytes 262144 | tf_op jit(solution)/shard_map/all_to_all | solution.py:22
  20.8 16.9 %all_to_all.26 = f32[16,16,128]{2,1,0:T(8,128)S(1)} all-to-all(f32[16,16,128]{2,1,0:T(8,128)S(1)} %broadcast_in_dim.6), channel_id=1, replica_groups=mesh['y_lo'=2,'x'=4,'core'=2,'y_hi'=2,'z'=8] {'core','z'}, dimensions={0} | all-to-all | bytes 262144 | tf_op jit(solution)/shard_map/all_to_all | solution.py:22
  37.7 13.6 %all_to_all.27 = f32[16,16,128]{2,1,0:T(8,128)S(1)} all-to-all(f32[16,16,128]{2,1,0:T(8,128)S(1)} %broadcast_in_dim.7), channel_id=1, replica_groups=mesh['y_lo'=2,'x'=4,'core'=2,'y_hi'=2,'z'=8] {'y_hi','y_lo','x'}, dimensions={0} | all-to-all | bytes 262144 | tf_op jit(solution)/shard_map/all_to_all | solution.py:22
  51.3 0.0 collective-permute-done.come_ref
  51.3 0.7 update_parts.1
  51.9 13.7 %all_to_all.28.parts_ref = f32[8,64,128]{2,1,0:T(8,128)S(1)} all-to-all(f32[8,64,128]{2,1,0:T(8,128)S(1)} %update_parts.1), channel_id=1, replica_groups=mesh['y_lo'=2,'x'=4,'core'=2,'y_hi'=2,'z'=8] {'z'}, dimensions={0} | all-to-all | bytes 524288 | tf_op jit(solution)/shard_map/all_to_all | solution.py:22
  65.6 0.4 own_update.1
  65.9 0.0 collective-permute-start.1
  66.0 1.2 %collective-permute-done.1 = f32[32,128]{1,0:T(8,128)S(1)} collective-permute-done((f32[32,128]{1,0:T(8,128)S(1)}, f32[32,128]{1,0:T(8,128)S(1)}, u32[]{:S(2)}, u32[]{:S(2)}) %collective-permute-start.1) | collective-permute-done | bytes 16416 | tf_op jit(solution)/shard_map/ppermute | solution.py:39
  67.2 0.6 collective-permute-start.2
  67.7 3.2 %collective-permute-done.2 = f32[32,128]{1,0:T(8,128)S(1)} collective-permute-done((f32[32,128]{1,0:T(8,128)S(1)}, f32[32,128]{1,0:T(8,128)S(1)}, u32[]{:S(2)}, u32[]{:S(2)}) %collective-permute-start.2) | collective-permute-done | bytes 16416 | tf_op jit(solution)/shard_map/ppermute | solution.py:39
  70.9 11.8 %all_to_all.29.cross_ref = f32[16,32,128]{2,1,0:T(8,128)S(1)} all-to-all(f32[16,32,128]{2,1,0:T(8,128)S(1)} %broadcast_in_dim.8), channel_id=1, replica_groups=mesh['y_lo'=2,'x'=4,'core'=2,'y_hi'=2,'z'=8] {'y_hi','y_lo','x'}, dimensions={0} | all-to-all | bytes 524288 | tf_op jit(solution)/shard_map/all_to_all | solution.py:22
  82.7 2.3 %whitened.1 = f32[32,64]{1,0:T(8,128)} custom-call(f32[16,32,128]{2,1,0:T(8,128)S(1)} %all_to_all.29.cross_ref, f32[32,64]{1,0:T(8,128)S(1)} %get-tuple-element.14.update_ref), custom_call_target="tpu_custom_call" | custom-call | tf_op jit(solution)/shard_map/whitened/pallas_call | solution.py:276
  (7 shorter events, 0.1 us)
Async XLA Ops:
  3.6 47.7 %collective-permute-start = (f32[256,512]{1,0:T(8,128)S(1)}, f32[256,512]{1,0:T(8,128)S(1)}, u32[]{:S(2)}, u32[]{:S(2)}) collective-permute-start(f32[256,512]{1,0:T(8,128)S(1)} %get-tuple-element.11), channel_id=1, source_target_pairs={{0,8},{8,0},{1,9},{9,1},{2,10},{10,2},{3,11},{11,3},{4,12},{12,4},... | collective-permute-start | bytes 1572872 | tf_op jit(solution)/shard_map/ppermute | solution.py:39
  65.9 1.2 %collective-permute-start.1 = (f32[32,128]{1,0:T(8,128)S(1)}, f32[32,128]{1,0:T(8,128)S(1)}, u32[]{:S(2)}, u32[]{:S(2)}) collective-permute-start(f32[32,128]{1,0:T(8,128)S(1)} %get-tuple-element.13), channel_id=1, source_target_pairs={{0,16},{16,0},{1,17},{17,1},{2,18},{18,2},{3,19},{19,3},{4,20},{20... | collective-permute-start | bytes 49160 | tf_op jit(solution)/shard_map/ppermute | solution.py:39
  67.2 3.7 %collective-permute-start.2 = (f32[32,128]{1,0:T(8,128)S(1)}, f32[32,128]{1,0:T(8,128)S(1)}, u32[]{:S(2)}, u32[]{:S(2)}) collective-permute-start(f32[32,128]{1,0:T(8,128)S(1)} %add.6), channel_id=1, source_target_pairs={{0,1},{1,0},{2,3},{3,2},{4,5},{5,4},{6,7},{7,6},{8,9},{9,8},{10,11... | collective-permute-start | bytes 49160 | tf_op jit(solution)/shard_map/ppermute | solution.py:39

commit v12 on v11

--- a/solution.py
+++ b/solution.py
@@ -70,7 +70,9 @@
     planes,
     y_here,
     x_here,
+    folded_here,
     arrived,
+    left_here,
 ):
     depth, width_x, _ = planes.shape
     rank = y_ref.shape[0]
@@ -81,6 +83,12 @@
 
     def plane(z):
         return pltpu.make_async_copy(tensor_ref.at[z], planes.at[z], arrived.at[z])
+
+    def result(pair):
+        lanes = pl.ds(2 * rank * pair, 2 * rank)
+        return pltpu.make_async_copy(
+            folded_here.at[:, lanes], folded_ref.at[:, lanes], left_here.at[pair]
+        )
 
     for z in range(EARLY):
         plane(z).start()
@@ -121,7 +129,10 @@
                     term = jnp.dot(x_part, part, preferred_element_type=jnp.float32)
                     folded = term if folded is None else folded + term
         if step > 0:
-            folded_ref[:, pl.ds(2 * rank * (step - 1), 2 * rank)] = folded
+            folded_here[:, pl.ds(2 * rank * (step - 1), 2 * rank)] = folded
+            result(step - 1).start()
+    for pair in range(pairs):
+        result(pair).wait()
 
 
 def projected(tensor, y_factor, x_factor):
@@ -135,12 +146,14 @@
             for n in (width_x // 2, width_x // 2, rank)
         ],
         in_specs=[pl.BlockSpec(memory_space=pltpu.HBM)] * 3,
-        out_specs=[ON_CHIP] * 3,
+        out_specs=[ON_CHIP, ON_CHIP, pl.BlockSpec(memory_space=pltpu.HBM)],
         scratch_shapes=[
             pltpu.VMEM(tensor.shape, tensor.dtype),
             pltpu.VMEM((rank, width_y), y_factor.dtype),
             pltpu.VMEM(x_factor.shape, x_factor.dtype),
+            pltpu.VMEM((rank, rows), jnp.float32),
             pltpu.SemaphoreType.DMA((depth + 2,)),
+            pltpu.SemaphoreType.DMA((depth // 2,)),
         ],
         compiler_params=pltpu.CompilerParams(vmem_limit_bytes=24 * 2**20),
         name="projected",
@@ -290,7 +303,7 @@
     folded, come = summed_everywhere(folded_part, sent)
     parts = update_parts(kept, come, folded, lax.axis_size("z"))
     update_t, wide = own_update(exchanged(parts, "z"))
-    wide = with_neighbour(with_neighbour(wide, "core"), "z")
+    wide = with_neighbour(with_neighbour(wide, "z"), "core")
     total_x = width_x * lax.axis_size(GX)
     return whitened(of_everyone(wide, CHIPS), update_t, float(total_x) ** 0.5).T
 

time: 85.3 us -> 86.9 us (1.019); the launches traced: 85 us -> 85.7 us
  no operation moved by 1% of the time
where the time goes in v12:
time: 86.9 us; the launch traced here: 85.7 us
  blocking collectives  70.3 us (81%)
  Pallas kernels  6.99 us (8%)
  waiting for transfers between devices  4.61 us (5%)
  starting transfers between devices  3.64 us (4%)
    all_to_all x5, blocking collectives, exchanged(): return lax.all_to_all(tiles, axis, 0, 0, tiled=True)  70.3 us
    ppermute x3, waiting for transfers between devices, from_partner(): lax.ppermute(array, axis, [(i, i ^ 1) for i in range(lax.axis_size(axis))])  4.61 us
    pallas_call x1, Pallas kernels, projected(): pl.pallas_call(project_kernel, out_shape=[jax.ShapeDtypeStruct((n, rows),...  3.68 us
    ppermute x3, starting transfers between devices, from_partner(): lax.ppermute(array, axis, [(i, i ^ 1) for i in range(lax.axis_size(axis))])  3.64 us
    pallas_call x1, Pallas kernels, whitened(): pl.pallas_call(functools.partial(whitened_kernel, scale), out_shape=jax.S...  2.3 us
  transfers between devices with their start and end apart: 3, of which 2 were waited for; matrix products, arithmetic and copies ran while one was open for 0% of the time, Pallas kernels for 0%

profile of v12, /device:TPU:2, one launch (start us, length us, event | category | flops | bytes accessed | tf_op | source)
XLA Modules:
  0.0 85.7 jit_solution(8031548295650098001)
XLA Ops:
  0.0 3.7 %projected.1 = (f32[256,512]{1,0:T(8,128)S(1)}, f32[256,512]{1,0:T(8,128)S(1)}, f32[64,512]{1,0:T(8,128)S(1)}) custom-call(bf16[8,512,512]{2,1,0:T(8,128)(2,1)} %tensor_ref.1, bf16[64,512]{1,0:T(8,128)(2,1)} %bitcast.14, bf16[64,512]{1,0:T(8,128)(2,1)} %x_ref.1), custom_call_target="tpu_custom_call" | custom-call | tf_op jit(solution)/shard_map/projected/pallas_call | solution.py:142
  3.7 3.3 %collective-permute-start = (f32[256,512]{1,0:T(8,128)S(1)}, f32[256,512]{1,0:T(8,128)S(1)}, u32[]{:S(2)}, u32[]{:S(2)}) collective-permute-start(f32[256,512]{1,0:T(8,128)S(1)} %get-tuple-element.11), channel_id=1, source_target_pairs={{0,8},{8,0},{1,9},{9,1},{2,10},{10,2},{3,11},{11,3},{4,12},{12,4},... | collective-permute-start | bytes 1572872 | tf_op jit(solution)/shard_map/ppermute | solution.py:39
  7.0 13.8 %all_to_all.25 = f32[16,16,128]{2,1,0:T(8,128)S(1)} all-to-all(f32[16,16,128]{2,1,0:T(8,128)S(1)} %bitcast.13), channel_id=1, replica_groups=mesh['y_lo'=2,'x'=4,'core'=2,'y_hi'=2,'z'=8] {'y_hi','y_lo','x'}, dimensions={0} | all-to-all | bytes 262144 | tf_op jit(solution)/shard_map/all_to_all | solution.py:22
  20.9 16.9 %all_to_all.26 = f32[16,16,128]{2,1,0:T(8,128)S(1)} all-to-all(f32[16,16,128]{2,1,0:T(8,128)S(1)} %broadcast_in_dim.6), channel_id=1, replica_groups=mesh['y_lo'=2,'x'=4,'core'=2,'y_hi'=2,'z'=8] {'core','z'}, dimensions={0} | all-to-all | bytes 262144 | tf_op jit(solution)/shard_map/all_to_all | solution.py:22
  37.8 13.6 %all_to_all.27 = f32[16,16,128]{2,1,0:T(8,128)S(1)} all-to-all(f32[16,16,128]{2,1,0:T(8,128)S(1)} %broadcast_in_dim.7), channel_id=1, replica_groups=mesh['y_lo'=2,'x'=4,'core'=2,'y_hi'=2,'z'=8] {'y_hi','y_lo','x'}, dimensions={0} | all-to-all | bytes 262144 | tf_op jit(solution)/shard_map/all_to_all | solution.py:22
  51.4 0.0 collective-permute-done.come_ref
  51.4 0.7 update_parts.1
  52.0 13.9 %all_to_all.28.parts_ref = f32[8,64,128]{2,1,0:T(8,128)S(1)} all-to-all(f32[8,64,128]{2,1,0:T(8,128)S(1)} %update_parts.1), channel_id=1, replica_groups=mesh['y_lo'=2,'x'=4,'core'=2,'y_hi'=2,'z'=8] {'z'}, dimensions={0} | all-to-all | bytes 524288 | tf_op jit(solution)/shard_map/all_to_all | solution.py:22
  66.0 0.4 own_update.1
  66.3 0.3 collective-permute-start.1
  66.7 3.4 %collective-permute-done.1 = f32[32,128]{1,0:T(8,128)S(1)} collective-permute-done((f32[32,128]{1,0:T(8,128)S(1)}, f32[32,128]{1,0:T(8,128)S(1)}, u32[]{:S(2)}, u32[]{:S(2)}) %collective-permute-start.1) | collective-permute-done | bytes 16416 | tf_op jit(solution)/shard_map/ppermute | solution.py:39
  70.1 0.0 collective-permute-start.2
  70.1 1.2 %collective-permute-done.2 = f32[32,128]{1,0:T(8,128)S(1)} collective-permute-done((f32[32,128]{1,0:T(8,128)S(1)}, f32[32,128]{1,0:T(8,128)S(1)}, u32[]{:S(2)}, u32[]{:S(2)}) %collective-permute-start.2) | collective-permute-done | bytes 16416 | tf_op jit(solution)/shard_map/ppermute | solution.py:39
  71.3 12.1 %all_to_all.29.cross_ref = f32[16,32,128]{2,1,0:T(8,128)S(1)} all-to-all(f32[16,32,128]{2,1,0:T(8,128)S(1)} %broadcast_in_dim.8), channel_id=1, replica_groups=mesh['y_lo'=2,'x'=4,'core'=2,'y_hi'=2,'z'=8] {'y_hi','y_lo','x'}, dimensions={0} | all-to-all | bytes 524288 | tf_op jit(solution)/shard_map/all_to_all | solution.py:22
  83.4 2.3 %whitened.1 = f32[32,64]{1,0:T(8,128)} custom-call(f32[16,32,128]{2,1,0:T(8,128)S(1)} %all_to_all.29.cross_ref, f32[32,64]{1,0:T(8,128)S(1)} %get-tuple-element.14.update_ref), custom_call_target="tpu_custom_call" | custom-call | tf_op jit(solution)/shard_map/whitened/pallas_call | solution.py:289
  (7 shorter events, 0.1 us)
Async XLA Ops:
  3.7 47.7 %collective-permute-start = (f32[256,512]{1,0:T(8,128)S(1)}, f32[256,512]{1,0:T(8,128)S(1)}, u32[]{:S(2)}, u32[]{:S(2)}) collective-permute-start(f32[256,512]{1,0:T(8,128)S(1)} %get-tuple-element.11), channel_id=1, source_target_pairs={{0,8},{8,0},{1,9},{9,1},{2,10},{10,2},{3,11},{11,3},{4,12},{12,4},... | collective-permute-start | bytes 1572872 | tf_op jit(solution)/shard_map/ppermute | solution.py:39
  66.3 3.8 %collective-permute-start.1 = (f32[32,128]{1,0:T(8,128)S(1)}, f32[32,128]{1,0:T(8,128)S(1)}, u32[]{:S(2)}, u32[]{:S(2)}) collective-permute-start(f32[32,128]{1,0:T(8,128)S(1)} %get-tuple-element.13), channel_id=1, source_target_pairs={{0,1},{1,0},{2,3},{3,2},{4,5},{5,4},{6,7},{7,6},{8,9},{9,8},{10,11... | collective-permute-start | bytes 49160 | tf_op jit(solution)/shard_map/ppermute | solution.py:39
  70.1 1.2 %collective-permute-start.2 = (f32[32,128]{1,0:T(8,128)S(1)}, f32[32,128]{1,0:T(8,128)S(1)}, u32[]{:S(2)}, u32[]{:S(2)}) collective-permute-start(f32[32,128]{1,0:T(8,128)S(1)} %add.6), channel_id=1, source_target_pairs={{0,16},{16,0},{1,17},{17,1},{2,18},{18,2},{3,19},{19,3},{4,20},{20... | collective-permute-start | bytes 49160 | tf_op jit(solution)/shard_map/ppermute | solution.py:39
